TPU v7x, 32 devices: a whole 2x2x4 slice. The times are simulated.
32 devices in a mesh: dp: 8 (over z, core), tensor: 4 (over y, x).
Axes of the slice: x: 2, y: 2, z: 4, core: 2. Of those that a mesh axis runs over, the one named last changes fastest.
Arguments:
- inputs: bfloat16 [8192, 2048], P(('dp', 'tensor')), may hold values from -6 to 6
- teacher: bfloat16 [8192, 2048], P(('dp', 'tensor')), may hold values from -6 to 6
- segment: int32 [8192], P('dp'), may hold values from 0 to 13, as said below
- position: int32 [8192], P('dp'), may hold values from 0 to 1023, as said below
- wq: bfloat16 [2048, 2048], P('dp', 'tensor'), may hold values from -0.125 to 0.125
- wk: bfloat16 [2048, 2048], P('dp', 'tensor'), may hold values from -0.125 to 0.125
- wv: bfloat16 [2048, 2048], P('dp', 'tensor'), may hold values from -0.125 to 0.125
- wo: bfloat16 [2048, 2048], P('tensor', 'dp'), may hold values from -0.125 to 0.125
- wg: bfloat16 [2048, 8192], P('dp', 'tensor'), may hold values from -0.125 to 0.125
- wu: bfloat16 [2048, 8192], P('dp', 'tensor'), may hold values from -0.125 to 0.125
- wd: bfloat16 [8192, 2048], P('tensor', 'dp'), may hold values from -0.0625 to 0.0625
- q_gain: bfloat16 [2048], P('dp'), may hold values from 0.099609375 to 1.8984375
- k_gain: bfloat16 [2048], P('dp'), may hold values from 0.099609375 to 1.8984375
- attn_gain: bfloat16 [2048], P('dp'), may hold values from 0.099609375 to 1.8984375
- ffn_gain: bfloat16 [2048], P('dp'), may hold values from 0.099609375 to 1.8984375
Outputs:
- output: bfloat16 [8192, 2048], P(('dp', 'tensor'))
- loss: float32 [], replicated
- grad_x: float32 [8192, 2048], P(('dp', 'tensor'))
- grad_wq: float32 [2048, 2048], P('dp', 'tensor')
- grad_wk: float32 [2048, 2048], P('dp', 'tensor')
- grad_wv: float32 [2048, 2048], P('dp', 'tensor')
- grad_wo: float32 [2048, 2048], P('tensor', 'dp')
- grad_wg: float32 [2048, 8192], P('dp', 'tensor')
- grad_wu: float32 [2048, 8192], P('dp', 'tensor')
- grad_wd: float32 [8192, 2048], P('tensor', 'dp')
- grad_q_gain: float32 [2048], P('dp')
- grad_k_gain: float32 [2048], P('dp')
- grad_attn_gain: float32 [2048], P('dp')
- grad_ffn_gain: float32 [2048], P('dp')
Inputs may be any that keep to these rules, and one draw needn't show every extreme that they name: `segment`: each sequence is 1024 consecutive tokens; in it, documents are runs of one nonzero number that never falls, followed at the sequence's end by a run of zeros (padding), which may be empty. Numbers repeat in other sequences. Sequence 0 is one whole document; sequence 1 holds thirteen. `position`: each token's index within its document; padding tokens count from the start of their padding run.
All inputs are finite; a program needn't handle non-finite values.
Results may differ from a plain program's by a relative error of at most 0.025.
Values may be sent and summed in bfloat16 or wider, within the bound.
No kernel may reach another device: no remote copies, remote signals or barrier semaphores. Data moves between devices by JAX's collectives and lax.ppermute only.
A program may use at most 192 MiB of HBM per device.

v0:
```python
import jax
import jax.numpy as jnp
from jax import lax
from jax.sharding import PartitionSpec as P


HD = 128
LEN = 1024
EPS = 1e-06
THETA = 500000.0
NEGATIVE = -1e30
BF = jnp.bfloat16
F32 = jnp.float32


def tables(position):
    freq = 1.0 / THETA ** (jnp.arange(0, HD, 2).astype(F32) / HD)
    angle = position.astype(F32)[:, None] * freq[None, :]
    angle = jnp.concatenate([angle, angle], axis=1)[:, None, :]
    return (jnp.cos(angle), jnp.sin(angle))


def rotate(values, cosines, sines):
    half = values.shape[-1] // 2
    turned = jnp.concatenate([-values[..., half:], values[..., :half]], axis=-1)
    return values * cosines + turned * sines


def unrotate(grad, cosines, sines):
    half = grad.shape[-1] // 2
    turned = grad * sines
    return grad * cosines + jnp.concatenate([turned[..., half:], -turned[..., :half]], axis=-1)


def inner_rows(left, right):
    return lax.dot_general(left, right, (((0,), (0,)), ((), ())), preferred_element_type=F32)


def times(left, right):
    return jnp.dot(left, right, preferred_element_type=F32)


def times_transposed(left, right):
    return lax.dot_general(left, right, (((1,), (1,)), ((), ())), preferred_element_type=F32)


def hop(value, way, size=4):
    return lax.ppermute(value, "tensor", [(i, i ^ way) for i in range(size)])


class Square:
    def __init__(self, size):
        self.me = lax.axis_index("tensor")
        self.order = self.me ^ jnp.arange(size)

    def gather(self, own):
        half = own.shape[0] // 2
        across = hop(own, 1)
        along = hop(own, 2)
        first = hop(across[:half], 2)
        second = hop(along[half:], 1)
        return jnp.concatenate([own, across, along, first, second], axis=0)

    def scatter(self, parts):
        rows = parts.shape[0] // 4
        half = rows // 2
        own, across, along, far = (parts[i * rows : (i + 1) * rows] for i in range(4))
        far = far.astype(BF)
        first = hop(far[:half], 1).astype(F32)
        second = hop(far[half:], 2).astype(F32)
        along = jnp.concatenate([along[:half] + first, along[half:]], axis=0).astype(BF)
        across = jnp.concatenate([across[:half], across[half:] + second], axis=0).astype(BF)
        across = hop(across, 1)
        along = hop(along, 2)
        return own + across.astype(F32) + along.astype(F32)

    def total(self, value):
        return (value + hop(value, 1)) + (hop(value, 2) + hop(value, 3))

    def total_by_token(self, value):
        blocks = value.reshape(value.shape[0], 4, -1)
        result = blocks
        for way in (1, 2, 3):
            got = hop(blocks, way)
            result = result + jnp.stack([got[:, r ^ way] for r in range(4)], axis=1)
        return result.reshape(value.shape)


class Plain:
    def __init__(self, size):
        self.me = lax.axis_index("tensor")
        self.order = jnp.arange(size)

    def gather(self, own):
        return lax.all_gather(own, "tensor", axis=0, tiled=True)

    def scatter(self, parts):
        return lax.psum_scatter(
            parts.astype(BF), "tensor", scatter_dimension=0, tiled=True
        ).astype(F32)

    def total(self, value):
        return lax.psum(value, "tensor")

    def total_by_token(self, value):
        return lax.psum(value, "tensor")


def attend_forward(query, key, value, allowed):
    scores = jnp.einsum("qhd,khd->hqk", query, key, preferred_element_type=F32) * HD ** (-0.5)
    scores = jnp.where(allowed[None], scores, NEGATIVE)
    highest = jnp.max(scores, axis=-1, keepdims=True)
    raised = jnp.exp(scores - highest)
    total = jnp.sum(raised, axis=-1, keepdims=True)
    prob = (raised / total).astype(BF)
    mixed = jnp.einsum("hqk,khd->qhd", prob, value, preferred_element_type=F32)
    return (mixed.astype(BF), (highest + jnp.log(total))[..., 0])


def attend_backward(query, key, value, allowed, logsum, grad_mixed):
    scores = jnp.einsum("qhd,khd->hqk", query, key, preferred_element_type=F32) * HD ** (-0.5)
    scores = jnp.where(allowed[None], scores, NEGATIVE)
    prob = jnp.exp(scores - logsum[..., None])
    grad_prob = jnp.einsum("qhd,khd->hqk", grad_mixed, value, preferred_element_type=F32)
    delta = jnp.sum(grad_prob * prob, axis=-1, keepdims=True)
    grad_scores = (prob * (grad_prob - delta)).astype(BF)
    factor = HD ** (-0.5)
    grad_value = jnp.einsum("hqk,qhd->khd", prob.astype(BF), grad_mixed, preferred_element_type=F32)
    grad_query = jnp.einsum("hqk,khd->qhd", grad_scores, key, preferred_element_type=F32) * factor
    grad_key = jnp.einsum("hqk,qhd->khd", grad_scores, query, preferred_element_type=F32) * factor
    return (grad_query, grad_key, grad_value.astype(BF))


def pick_halves(array, axis):
    dp = lax.axis_size("dp")
    first = lax.axis_index("dp") % 2 == 0
    share = array.shape[axis] // dp
    chunks = [lax.slice_in_dim(array, i * share, (i + 1) * share, axis=axis) for i in range(dp)]
    even = jnp.concatenate(chunks[0::2], axis=axis)
    odd = jnp.concatenate(chunks[1::2], axis=axis)
    return jnp.where(first, odd, even), jnp.where(first, even, odd)


def pair_sum(product, sides):
    size = lax.axis_size("dp")
    theirs = product(sides[0]).astype(BF)
    got = lax.ppermute(theirs, "dp", [(i, i ^ 1) for i in range(size)])
    return (product(sides[1]) + got.astype(F32)).astype(BF)


def scatter_pairs(value, axis):
    size = lax.axis_size("dp")
    groups = [list(range(core, size, 2)) for core in (0, 1)]
    return lax.psum_scatter(
        value, "dp", scatter_dimension=axis, axis_index_groups=groups, tiled=True
    )


def spread_over_dp(chunks):
    size = chunks.shape[0]
    me = lax.axis_index("dp")
    total = lax.dynamic_index_in_dim(chunks, me, 0, keepdims=False)
    for shift in range(1, size):
        sent = lax.dynamic_index_in_dim(chunks, me ^ shift, 0, keepdims=False)
        total = total + lax.ppermute(sent, "dp", [(i, i ^ shift) for i in range(size)])
    return total


def layer(
    inputs, teacher, segment, position, wq, wk, wv, wo, wg, wu, wd, q_gain, k_gain, attn_gain, ffn_gain
):
    dp = lax.axis_size("dp")
    tensor = lax.axis_size("tensor")
    ring = Square(tensor) if tensor == 4 else Plain(tensor)
    rows, width = inputs.shape
    share, local_width = wq.shape
    units = wg.shape[1]
    heads_here = local_width // HD
    group = segment.shape[0]
    assert group == LEN and rows * tensor == group

    pieces = local_width // share
    wo_side = jnp.concatenate([wo[i * share : (i + 1) * share] for i in range(pieces)], axis=1)
    attn_shard = jnp.concatenate([wq, wk, wv, wo_side], axis=1)
    attn_all = lax.all_gather(attn_shard, "dp", axis=0, tiled=True)
    pair_all = lax.all_gather(jnp.concatenate([wg, wu], axis=1), "dp", axis=0, tiled=True)
    full_down = lax.all_gather(wd, "dp", axis=1, tiled=True)

    counted = jnp.sum((segment != 0).astype(F32))
    small = jnp.concatenate(
        [
            jnp.stack([q_gain, k_gain, attn_gain, ffn_gain]).astype(F32),
            jnp.broadcast_to(counted, (4, share)),
        ]
    )
    small_all = lax.all_gather(small, "dp", axis=1)
    gains = small_all[:4].reshape(4, width)
    valid_total = jnp.sum(small_all[4, :, 0])
    offset = ring.me * local_width
    gain_qk = lax.dynamic_slice(gains, (0, offset), (2, local_width))
    gain_attn = gains[2]
    gain_ffn = gains[3]

    segment_rel = jnp.take(segment.reshape(tensor, rows), ring.order, axis=0).reshape(group)
    position_rel = jnp.take(position.reshape(tensor, rows), ring.order, axis=0).reshape(group)
    place = (ring.order[:, None] * rows + jnp.arange(rows)[None, :]).reshape(group)
    allowed = (segment_rel[:, None] == segment_rel[None, :]) & (place[:, None] >= place[None, :])
    cosines, sines = tables(position_rel)

    whole_inputs = ring.gather(inputs)
    qkv = attn_all[:, : 3 * local_width]
    full_out = (
        attn_all[:, 3 * local_width :]
        .reshape(dp, share, pieces, share)
        .transpose(2, 1, 0, 3)
        .reshape(local_width, width)
    )
    raw = times(whole_inputs, qkv)
    raw_q = raw[:, :local_width]
    raw_k = raw[:, local_width : 2 * local_width]
    value = raw[:, 2 * local_width :].astype(BF).reshape(group, heads_here, HD)
    squares = ring.total_by_token(jnp.stack([jnp.sum(raw_q * raw_q, axis=1), jnp.sum(raw_k * raw_k, axis=1)]))
    scales = lax.rsqrt(squares / width + EPS)
    scale_q = scales[0][:, None]
    scale_k = scales[1][:, None]
    normed_q = raw_q * scale_q
    normed_k = raw_k * scale_k
    query = rotate(
        (normed_q * gain_qk[0]).reshape(group, heads_here, HD), cosines, sines
    ).astype(BF)
    key = rotate((normed_k * gain_qk[1]).reshape(group, heads_here, HD), cosines, sines).astype(BF)
    mixed, logsum = attend_forward(query, key, value, allowed)
    attn_rows = mixed.reshape(group, local_width)
    branch_attn = ring.scatter(times(attn_rows, full_out))
    scale_attn = lax.rsqrt(jnp.mean(branch_attn * branch_attn, axis=1, keepdims=True) + EPS)
    normed_attn = branch_attn * scale_attn
    resid = inputs.astype(F32) + normed_attn * gain_attn
    whole_h = ring.gather(resid.astype(BF))

    pair = times(whole_h, pair_all)
    gate = pair[:, :units]
    up = pair[:, units:]
    sigma = jax.nn.sigmoid(gate)
    activated = gate * sigma
    hidden = (activated * up).astype(BF)
    branch_ffn = ring.scatter(times(hidden, full_down))
    scale_ffn = lax.rsqrt(jnp.mean(branch_ffn * branch_ffn, axis=1, keepdims=True) + EPS)
    normed_ffn = branch_ffn * scale_ffn
    output = resid + normed_ffn * gain_ffn
    my_segment = lax.dynamic_slice_in_dim(segment, ring.me * rows, rows)
    valid = (my_segment != 0).astype(F32)[:, None]
    error = output - teacher.astype(F32)
    loss_part = jnp.sum(valid * error * error)
    tokens_all = rows * dp * tensor
    grad_output = 2.0 * tokens_all * valid * error / valid_total
    grad_gain_ffn = jnp.sum(grad_output * normed_ffn, axis=0)
    grad_normed = grad_output * gain_ffn
    grad_branch_ffn = (
        scale_ffn
        * (grad_normed - normed_ffn * jnp.mean(grad_normed * normed_ffn, axis=1, keepdims=True))
    ).astype(BF)
    piece = ring.gather(grad_branch_ffn)
    grad_down = pair_sum(lambda side: inner_rows(hidden, side), pick_halves(piece, 1))
    sum_down = scatter_pairs(grad_down, 1)
    piece, grad_down = lax.optimization_barrier((piece, grad_down))
    grad_hidden = times_transposed(piece, full_down)
    grad_gate = (grad_hidden * up * sigma * (1.0 + gate * (1.0 - sigma))).astype(BF)
    grad_up = (grad_hidden * activated).astype(BF)
    grad_pair = jnp.concatenate([grad_gate, grad_up], axis=1)
    back_h = times_transposed(grad_pair, pair_all)
    back_h, grad_pair = lax.optimization_barrier((back_h, grad_pair))
    back_h = ring.scatter(back_h)
    pair_grads = pair_sum(lambda side: inner_rows(side, grad_pair), pick_halves(whole_h, 1))
    sum_pair = scatter_pairs(pair_grads, 0)
    back_h, pair_grads = lax.optimization_barrier((back_h, pair_grads))
    grad_resid = grad_output + back_h
    grad_gain_attn = jnp.sum(grad_resid * normed_attn, axis=0)
    grad_normed = grad_resid * gain_attn
    grad_branch_attn = (
        scale_attn
        * (grad_normed - normed_attn * jnp.mean(grad_normed * normed_attn, axis=1, keepdims=True))
    ).astype(BF)
    piece = ring.gather(grad_branch_attn)
    grad_mixed = times_transposed(piece, full_out).astype(BF).reshape(group, heads_here, HD)
    out_grads = pair_sum(lambda side: inner_rows(attn_rows, side), pick_halves(piece, 1))
    out_grads = (
        out_grads.reshape(pieces, share, dp // 2, share)
        .transpose(2, 1, 0, 3)
        .reshape(dp // 2 * share, pieces * share)
    )
    grad_query, grad_key, grad_value = attend_backward(
        query, key, value, allowed, logsum, grad_mixed
    )
    grad_normed_q = unrotate(grad_query, cosines, sines).reshape(group, local_width)
    grad_normed_k = unrotate(grad_key, cosines, sines).reshape(group, local_width)
    grad_value = grad_value.reshape(group, local_width)
    grad_hat_q = grad_normed_q * gain_qk[0]
    grad_hat_k = grad_normed_k * gain_qk[1]
    inner = ring.total_by_token(
        jnp.stack([jnp.sum(grad_hat_q * normed_q, axis=1), jnp.sum(grad_hat_k * normed_k, axis=1)])
    )
    grad_raw_q = (scale_q * (grad_hat_q - normed_q * (inner[0] / width)[:, None])).astype(BF)
    grad_raw_k = (scale_k * (grad_hat_k - normed_k * (inner[1] / width)[:, None])).astype(BF)
    grad_raw = jnp.concatenate([grad_raw_q, grad_raw_k, grad_value], axis=1)
    qkv_grads = pair_sum(lambda side: inner_rows(side, grad_raw), pick_halves(whole_inputs, 1))
    attn_grads = jnp.concatenate([qkv_grads, out_grads], axis=1)
    sum_attn = scatter_pairs(attn_grads, 0)
    grad_raw, attn_grads = lax.optimization_barrier((grad_raw, attn_grads))
    back_x = times_transposed(grad_raw, qkv)
    grad_input = grad_resid + ring.scatter(back_x)

    placed_q = lax.dynamic_update_slice_in_dim(
        jnp.zeros((width,), F32), jnp.sum(grad_normed_q * normed_q, axis=0), offset, 0
    )
    placed_k = lax.dynamic_update_slice_in_dim(
        jnp.zeros((width,), F32), jnp.sum(grad_normed_k * normed_k, axis=0), offset, 0
    )
    late = jnp.stack(
        [placed_q, placed_k, grad_gain_attn, grad_gain_ffn, jnp.broadcast_to(loss_part, (width,))]
    )
    late = jnp.concatenate([late, jnp.zeros((3, width), F32)])
    late = ring.total(late)
    late = spread_over_dp(late.reshape(8, dp, share).transpose(1, 0, 2))
    loss = late[4, 0] / (valid_total * width)

    sum_attn = sum_attn.astype(F32)
    sum_out = sum_attn[:, 3 * local_width :].reshape(share, pieces, share)
    sum_out = sum_out.transpose(1, 0, 2).reshape(local_width, share)
    sum_pair = sum_pair.astype(F32)
    return (
        output.astype(BF),
        loss,
        grad_input,
        sum_attn[:, :local_width],
        sum_attn[:, local_width : 2 * local_width],
        sum_attn[:, 2 * local_width : 3 * local_width],
        sum_out,
        sum_pair[:, :units],
        sum_pair[:, units:],
        sum_down.astype(F32),
        late[0],
        late[1],
        late[2],
        late[3],
    )


def solution(mesh):
    cols = P("dp", "tensor")
    side = P("tensor", "dp")
    both = P(("dp", "tensor"), None)
    one = P("dp")
    return jax.shard_map(
        layer,
        mesh=mesh,
        in_specs=(both, both, one, one, cols, cols, cols, side, cols, cols, side, one, one, one, one),
        out_specs=(both, P(), both, cols, cols, cols, side, cols, cols, side, one, one, one, one),
        check_vma=False,
    )
```

profile of v0, /device:TPU:0, one launch (start us, length us, event | category | flops | bytes accessed | tf_op | source)
XLA Modules:
  0.0 966.6 jit_solution(18269025715631661077)
XLA Ops:
  29.0 13.6 %collective-permute-done = bf16[256,2048]{1,0:T(8,128)(2,1)S(1)} collective-permute-done((bf16[256,2048]{1,0:T(8,128)(2,1)S(1)}, bf16[256,2048]{1,0:T(8,128)(2,1)S(1)}, u32[]{:S(2)}, u32[]{:S(2)}) %collective-permute-start) | collective-permute-done | bytes 1048608 | tf_op jit(solution)/shard_map/ppermute | solution.py:48
  45.1 15.6 %all-gather = f32[8,2048]{1,0:T(8,128)S(1)} all-gather(f32[8,256]{1,0:T(8,128)S(1)} %concatenate.117), channel_id=2, replica_groups=mesh['dp'=8,'tensor'=4] {'dp'}, dimensions={1}, use_global_device_ids=true | all-gather | bytes 73728 | tf_op jit(solution)/shard_map/all_gather | solution.py:196
  68.6 7.5 collective-permute-done.3
  76.9 21.6 %all-gather.5.cloned.1.call-done = bf16[2048,2048]{1,0:T(8,128)(2,1)} async-done(((bf16[256,2048]{1,0:T(8,128)(2,1)}), bf16[2048,2048]{1,0:T(8,128)(2,1)}) %all-gather.5.cloned.1.call-update) | async-done | bytes 8388624 | tf_op jit(solution)/shard_map/all_gather | solution.py:185
  98.5 10.0 %fusion.9 = f32[1024,1536]{1,0:T(8,128)S(1)} fusion(bf16[1024,2048]{1,0:T(8,128)(2,1)} %constant_dynamic-update-slice_fusion, bf16[2048,2048]{1,0:T(8,128)(2,1)} %all-gather.5.cloned.1.call-done), kind=kOutput, calls=%fused_computation.25 | convolution fusion | flops 6442450944 | bytes 16777216 | tf_op jit(solution)/shard_map/dot_general | solution.py:40
  119.2 4.1 reshape.356
  139.6 7.8 fusion.125
  147.4 8.3 fusion
  155.7 9.8 %fusion.47 = bf16[4,128,1024]{2,1,0:T(8,128)(2,1)S(1)} fusion(f32[4,1024,1024]{1,2,0:T(8,128)} %get-tuple-element.179, f32[4,1024]{1,0:T(4,128)S(1)} %fusion, f32[4,1024]{1,0:T(4,128)S(1)} %get-tuple-element.178, f32[1024,1536]{1,0:T(8,128)} %copy-done.1), kind=kOutput, calls=%fused_computation.108 | convolution fusion | flops 1086849024 | bytes 18907136 | tf_op jit(solution)/shard_map/hqk,khd->qhd/dot_general | solution.py:116
  171.1 10.3 %collective-permute-done.7 = bf16[128,2048]{1,0:T(8,128)(2,1)S(1)} collective-permute-done((bf16[128,2048]{1,0:T(8,128)(2,1)S(1)}, bf16[128,2048]{1,0:T(8,128)(2,1)S(1)}, u32[]{:S(2)}, u32[]{:S(2)}) %collective-permute-start.7) | collective-permute-done | bytes 524320 | tf_op jit(solution)/shard_map/ppermute | solution.py:48
  185.2 21.0 %collective-permute-done.8 = bf16[256,2048]{1,0:T(8,128)(2,1)S(1)} collective-permute-done((bf16[256,2048]{1,0:T(8,128)(2,1)S(1)}, bf16[256,2048]{1,0:T(8,128)(2,1)S(1)}, u32[]{:S(2)}, u32[]{:S(2)}) %collective-permute-start.8) | collective-permute-done | bytes 1048608 | tf_op jit(solution)/shard_map/ppermute | solution.py:48
  210.9 21.2 %collective-permute-done.11 = bf16[256,2048]{1,0:T(8,128)(2,1)S(1)} collective-permute-done((bf16[256,2048]{1,0:T(8,128)(2,1)S(1)}, bf16[256,2048]{1,0:T(8,128)(2,1)S(1)}, u32[]{:S(2)}, u32[]{:S(2)}) %collective-permute-start.11) | collective-permute-done | bytes 1048608 | tf_op jit(solution)/shard_map/ppermute | solution.py:48
  237.9 5.6 collective-permute-done.13
  245.1 5.2 all-gather.7.cloned.1.call-done
  250.3 21.9 %fusion.129 = f32[1024,4096]{1,0:T(8,128)S(1)} fusion(bf16[1024,2048]{1,0:T(8,128)(2,1)} %constant_dynamic-update-slice_fusion.10, bf16[2048,4096]{1,0:T(8,128)(2,1)} %all-gather.7.cloned.1.call-done), kind=kOutput, calls=%fused_computation.273 | convolution fusion | flops 17179869184 | bytes 37748736 | tf_op jit(solution)/shard_map/dot_general | solution.py:40
  272.2 5.9 copy-done.6
  278.1 3.9 multiply_convert_fusion.3
  282.0 50.7 %all-gather.9.cloned.1.call-done = bf16[2048,2048]{1,0:T(8,128)(2,1)} async-done(((bf16[2048,256]{1,0:T(8,128)(2,1)}), bf16[2048,2048]{1,0:T(8,128)(2,1)}) %all-gather.9.cloned.1.call-update) | async-done | bytes 8388624 | tf_op jit(solution)/shard_map/all_gather | solution.py:187
  332.6 12.7 %fusion.127 = (bf16[1024,2048]{1,0:T(8,128)(2,1)S(1)}, f32[1024,2048]{1,0:T(8,128)S(1)}) fusion(bf16[1024,2048]{1,0:T(8,128)(2,1)} %multiply_convert_fusion.3, bf16[2048,2048]{1,0:T(8,128)(2,1)} %all-gather.9.cloned.1.call-done), kind=kOutput, calls=%fused_computation.271 | convolution fusion | flops 8592031744 | bytes 25165824 | tf_op jit(solution)/shard_map/dot_general | solution.py:40
  348.6 11.1 %collective-permute-done.15 = bf16[128,2048]{1,0:T(8,128)(2,1)S(1)} collective-permute-done((bf16[128,2048]{1,0:T(8,128)(2,1)S(1)}, bf16[128,2048]{1,0:T(8,128)(2,1)S(1)}, u32[]{:S(2)}, u32[]{:S(2)}) %collective-permute-start.15) | collective-permute-done | bytes 524320 | tf_op jit(solution)/shard_map/ppermute | solution.py:48
  366.1 20.6 %collective-permute-done.16 = bf16[256,2048]{1,0:T(8,128)(2,1)} collective-permute-done((bf16[256,2048]{1,0:T(8,128)(2,1)}, bf16[256,2048]{1,0:T(8,128)(2,1)}, u32[]{:S(2)}, u32[]{:S(2)}) %collective-permute-start.16) | collective-permute-done | bytes 1048608 | tf_op jit(solution)/shard_map/ppermute | solution.py:48
  398.5 22.1 %collective-permute-done.19 = bf16[256,2048]{1,0:T(8,128)(2,1)S(1)} collective-permute-done((bf16[256,2048]{1,0:T(8,128)(2,1)}, bf16[256,2048]{1,0:T(8,128)(2,1)S(1)}, u32[]{:S(2)}, u32[]{:S(2)}) %collective-permute-start.19) | collective-permute-done | bytes 1048608 | tf_op jit(solution)/shard_map/ppermute | solution.py:48
  427.3 5.5 collective-permute-done.21
  439.1 5.9 convolution_convert_fusion.2
  445.0 3.9 fusion.106
  452.2 7.4 add_convert_fusion.1
  459.6 20.7 %multiply_convert_fusion.2 = (bf16[1024,2048]{1,0:T(8,128)(2,1)}, bf16[1024,2048]{1,0:T(8,128)(2,1)}) fusion(f32[1024,4096]{1,0:T(8,128)} %copy-done.6, bf16[1024,2048]{1,0:T(8,128)(2,1)} %constant_dynamic-update-slice_fusion.15, bf16[2048,2048]{1,0:T(8,128)(2,1)} %all-gather.9.cloned.1.call-done), kind=kOutput, calls=%fused_computation.14 | convolution fusion | flops 8617197568 | bytes 37748736 | tf_op jit(solution)/shard_map/dot_general | solution.py:44
  480.3 7.8 pad_maximum_fusion
  488.1 21.4 %fusion.97 = f32[1024,2048]{1,0:T(8,128)S(1)} fusion(bf16[2048,4096]{1,0:T(8,128)(2,1)} %all-gather.7.cloned.1.call-done, bf16[1024,2048]{1,0:T(8,128)(2,1)} %get-tuple-element.51, bf16[1024,2048]{1,0:T(8,128)(2,1)} %get-tuple-element.50), kind=kOutput, calls=%fused_computation.245 | convolution fusion | flops 17196646400 | bytes 33554432 | tf_op jit(solution)/shard_map/dot_general | solution.py:44
  509.6 14.1 %convolution_convert_fusion = bf16[1024,4096]{1,0:T(8,128)(2,1)} fusion(bf16[1024,4096]{1,0:T(8,128)(2,1)} %pad_maximum_fusion, pred[]{:T(512)S(6)} %eq.34, bf16[1024,256]{1,0:T(8,128)(2,1)S(1)} %get-tuple-element.85, bf16[1024,256]{1,0:T(8,128)(2,1)S(1)} %copy-done.50, bf16[1024,256]{1,0:T(8,128)(2,1)S(1)} %copy-done.51, ...), kind=kOutput, calls=%fused_computation.21 | convolution fusion | flops 8611954688 | bytes 20971520 | tf_op jit(solution)/shard_map/dot_general | solution.py:36
  526.2 12.8 %collective-permute-done.24 = bf16[128,2048]{1,0:T(8,128)(2,1)S(1)} collective-permute-done((bf16[128,2048]{1,0:T(8,128)(2,1)S(1)}, bf16[128,2048]{1,0:T(8,128)(2,1)S(1)}, u32[]{:S(2)}, u32[]{:S(2)}) %collective-permute-start.24) | collective-permute-done | bytes 524320 | tf_op jit(solution)/shard_map/ppermute | solution.py:48
  542.2 21.9 %collective-permute-done.25 = bf16[256,2048]{1,0:T(8,128)(2,1)S(1)} collective-permute-done((bf16[256,2048]{1,0:T(8,128)(2,1)S(1)}, bf16[256,2048]{1,0:T(8,128)(2,1)S(1)}, u32[]{:S(2)}, u32[]{:S(2)}) %collective-permute-start.25) | collective-permute-done | bytes 1048608 | tf_op jit(solution)/shard_map/ppermute | solution.py:48
  566.6 15.8 %add_convert_fusion = bf16[1024,4096]{1,0:T(8,128)(2,1)} fusion(bf16[1024,4096]{1,0:T(8,128)(2,1)} %collective-permute-done.28, bf16[1024,4096]{1,0:T(8,128)(2,1)} %pad_maximum_fusion, pred[]{:T(512)S(6)} %eq.34, bf16[1024,256]{1,0:T(8,128)(2,1)} %copy-done.49, bf16[1024,256]{1,0:T(8,128)(2,1)} %get-tuple-element.86, ...), kind=kOutput, calls=%fused_computation.4 | convolution fusion | flops 8620343296 | bytes 29360128 | tf_op jit(solution)/shard_map/dot_general | solution.py:36
  582.4 5.5 multiply_reduce_fusion.4
  594.5 18.7 %collective-permute-done.29 = bf16[256,2048]{1,0:T(8,128)(2,1)S(1)} collective-permute-done((bf16[256,2048]{1,0:T(8,128)(2,1)}, bf16[256,2048]{1,0:T(8,128)(2,1)S(1)}, u32[]{:S(2)}, u32[]{:S(2)}) %collective-permute-start.29) | collective-permute-done | bytes 1048608 | tf_op jit(solution)/shard_map/ppermute | solution.py:48
  628.6 4.6 convolution_convert_fusion.3
  633.3 14.2 %multiply_reduce_fusion = (f32[4,1024]{1,0:T(4,128)S(1)}, f32[4,1024,1024]{1,2,0:T(8,128)}) fusion(f32[4,1024,1024]{1,2,0:T(8,128)} %get-tuple-element.179, f32[4,1024]{1,0:T(4,128)S(1)} %log_add_fusion, bf16[1024,4,128]{0,2,1:T(8,128)(2,1)S(1)} %bitcast.158, f32[1024,1536]{1,0:T(8,128)} %copy-done.1), kind=kOutput, calls=%fused_computation.3 | convolution fusion | flops 1086320640 | bytes 35684352 | tf_op jit(solution)/shard_map/qhd,khd->hqk/dot_general | solution.py:124
  650.5 10.6 %multiply_convert_fusion = bf16[4,1024,1024]{1,2,0:T(8,128)(2,1)} fusion(f32[4,1024,1024]{1,2,0:T(8,128)} %get-tuple-element.185, f32[4,1024,1024]{1,2,0:T(8,128)S(1)} %bitcast.146, f32[4,1024]{1,0:T(4,128)S(1)} %get-tuple-element.184, f32[4,1024]{1,0:T(4,128)S(1)} %log_add_fusion), kind=kLoop, calls=%fused_computation.2 | loop fusion | flops 16777216 | bytes 41975808 | tf_op jit(solution)/shard_map/convert_element_type | solution.py:126
  661.2 6.4 fusion.130
  685.4 9.7 %fusion.51 = bf16[4,128,1024]{2,1,0:T(8,128)(2,1)} fusion(bf16[1024,4,128]{0,2,1:T(8,128)(2,1)S(1)} %bitcast.159, f32[4,1024,1024]{1,2,0:T(8,128)} %get-tuple-element.179, f32[4,1024]{1,0:T(4,128)S(1)} %log_add_fusion), kind=kOutput, calls=%fused_computation.110 | convolution fusion | flops 1082654720 | bytes 18890752 | tf_op jit(solution)/shard_map/hqk,qhd->khd/dot_general | solution.py:128
  701.9 5.1 convolution_convert_fusion.1
  722.5 5.8 add_convert_fusion.2
  732.4 10.7 %fusion.128 = (bf16[1024,2048]{1,0:T(8,128)(2,1)S(1)}, f32[1024,2048]{1,0:T(8,128)}) fusion(bf16[1024,1536]{1,0:T(8,128)(2,1)S(1)} %pad_maximum_fusion.2, bf16[2048,2048]{1,0:T(8,128)(2,1)} %all-gather.5.cloned.1.call-done), kind=kOutput, calls=%fused_computation.272 | convolution fusion | flops 6444548096 | bytes 22020096 | tf_op jit(solution)/shard_map/dot_general | solution.py:44
  749.9 8.1 collective-permute-done.48
  781.0 4.4 collective-permute-done.49
  790.9 16.1 %reduce-scatter.4.cloned.1.call-done = bf16[256,2048]{1,0:T(8,128)(2,1)} async-done(((bf16[1024,2048]{1,0:T(8,128)(2,1)}), bf16[256,2048]{1,0:T(8,128)(2,1)}) %reduce-scatter.4.cloned.1.call-update) | async-done | bytes 1048592 | tf_op jit(solution)/shard_map/reduce_scatter | solution.py:154
  810.6 143.7 %reduce-scatter.6.cloned.1.call-done = bf16[256,4096]{1,0:T(8,128)(2,1)} async-done(((bf16[1024,4096]{1,0:T(8,128)(2,1)}), bf16[256,4096]{1,0:T(8,128)(2,1)}) %reduce-scatter.6.cloned.1.call-update) | async-done | bytes 2097168 | tf_op jit(solution)/shard_map/reduce_scatter | solution.py:154
  954.3 4.1 fusion.111
  (425 shorter events, 232.6 us)
Async XLA Ops:
  7.2 91.3 %all-gather.5.cloned.1.call-start = ((), (), s32[]{:S(2)}) async-start(), calls=%async_computation.3 | async-start | bytes 9437184 | tf_op jit(solution)/shard_map/all_gather | solution.py:185
  13.1 237.2 %all-gather.7.cloned.1.call-start = ((), (), s32[]{:S(2)}) async-start(), calls=%async_computation.4 | async-start | bytes 18874368 | tf_op jit(solution)/shard_map/all_gather | solution.py:186
  16.3 316.4 %all-gather.9.cloned.1.call-start = ((), (), s32[]{:S(2)}) async-start(), calls=%async_computation.5 | async-start | bytes 9437184 | tf_op jit(solution)/shard_map/all_gather | solution.py:187
  16.3 26.2 %collective-permute-start = (bf16[256,2048]{1,0:T(8,128)(2,1)S(1)}, bf16[256,2048]{1,0:T(8,128)(2,1)S(1)}, u32[]{:S(2)}, u32[]{:S(2)}) collective-permute-start(bf16[256,2048]{1,0:T(8,128)(2,1)S(1)} %copy-done.11), channel_id=1, source_target_pairs={{0,1},{1,0},{2,3},{3,2},{4,5},{5,4},{6,7},{7,6},{8,9},{9,8},{10,11... | collective-permute-start | bytes 3145736 | tf_op jit(solution)/shard_map/ppermute | solution.py:48
  19.4 41.4 %collective-permute-start.1 = (bf16[256,2048]{1,0:T(8,128)(2,1)S(1)}, bf16[256,2048]{1,0:T(8,128)(2,1)}, u32[]{:S(2)}, u32[]{:S(2)}) collective-permute-start(bf16[256,2048]{1,0:T(8,128)(2,1)S(1)} %copy-done.11), channel_id=1, source_target_pairs={{0,2},{1,3},{2,0},{3,1},{4,6},{5,7},{6,4},{7,5},{8,10},{9,11},{10,... | collective-permute-start | bytes 3145736 | tf_op jit(solution)/shard_map/ppermute | solution.py:48
  20.9 754.1 %reduce-scatter.8.cloned.1.call-start = ((), (), s32[]{:S(2)}) async-start(), calls=%async_computation.8 | async-start | bytes 5242880 | tf_op jit(solution)/shard_map/reduce_scatter | solution.py:154
  43.3 23.3 %collective-permute-start.2 = (bf16[128,2048]{1,0:T(8,128)(2,1)}, bf16[128,2048]{1,0:T(8,128)(2,1)}, u32[]{:S(2)}, u32[]{:S(2)}) collective-permute-start(bf16[128,2048]{1,0:T(8,128)(2,1)} %slice.577), channel_id=1, source_target_pairs={{0,2},{1,3},{2,0},{3,1},{4,6},{5,7},{6,4},{7,5},{8,10},{9,11},{10,... | collective-permute-start | bytes 1572872 | tf_op jit(solution)/shard_map/ppermute | solution.py:48
  61.8 14.2 %collective-permute-start.3 = (bf16[128,2048]{1,0:T(8,128)(2,1)S(1)}, bf16[128,2048]{1,0:T(8,128)(2,1)S(1)}, u32[]{:S(2)}, u32[]{:S(2)}) collective-permute-start(bf16[128,2048]{1,0:T(8,128)(2,1)S(1)} %slice.578), channel_id=1, source_target_pairs={{0,1},{1,0},{2,3},{3,2},{4,5},{5,4},{6,7},{7,6},{8,9},{9,8},{10,11... | collective-permute-start | bytes 1572872 | tf_op jit(solution)/shard_map/ppermute | solution.py:48
  112.4 15.8 %collective-permute-start.4 = (f32[2,4,256]{2,1,0:T(4,128)S(1)}, f32[2,4,256]{2,1,0:T(4,128)S(1)}, u32[]{:S(2)}, u32[]{:S(2)}) collective-permute-start(f32[2,4,256]{2,1,0:T(4,128)S(1)} %constant_dynamic-update-slice_fusion.8), channel_id=1, source_target_pairs={{0,1},{1,0},{2,3},{3,2},{4,5},{5,4},{6,7},{7,6},{8,9},{9,8},{10,11... | collective-permute-start | bytes 24584 | tf_op jit(solution)/shard_map/ppermute | solution.py:48
  113.9 14.3 %collective-permute-start.6 = (f32[2,4,256]{2,1,0:T(4,128)S(1)}, f32[2,4,256]{2,1,0:T(4,128)S(1)}, u32[]{:S(2)}, u32[]{:S(2)}) collective-permute-start(f32[2,4,256]{2,1,0:T(4,128)S(1)} %constant_dynamic-update-slice_fusion.8), channel_id=1, source_target_pairs={{0,3},{1,2},{2,1},{3,0},{4,7},{5,6},{6,5},{7,4},{8,11},{9,10},{10,... | collective-permute-start | bytes 24584 | tf_op jit(solution)/shard_map/ppermute | solution.py:48
  115.4 12.9 %collective-permute-start.5 = (f32[2,4,256]{2,1,0:T(4,128)S(1)}, f32[2,4,256]{2,1,0:T(4,128)S(1)}, u32[]{:S(2)}, u32[]{:S(2)}) collective-permute-start(f32[2,4,256]{2,1,0:T(4,128)S(1)} %constant_dynamic-update-slice_fusion.8), channel_id=1, source_target_pairs={{0,2},{1,3},{2,0},{3,1},{4,6},{5,7},{6,4},{7,5},{8,10},{9,11},{10,... | collective-permute-start | bytes 24584 | tf_op jit(solution)/shard_map/ppermute | solution.py:48
  168.2 13.2 %collective-permute-start.7 = (bf16[128,2048]{1,0:T(8,128)(2,1)S(1)}, bf16[128,2048]{1,0:T(8,128)(2,1)S(1)}, u32[]{:S(2)}, u32[]{:S(2)}) collective-permute-start(bf16[128,2048]{1,0:T(8,128)(2,1)S(1)} %get-tuple-element.111), channel_id=1, source_target_pairs={{0,2},{1,3},{2,0},{3,1},{4,6},{5,7},{6,4},{7,5},{8,10},{9,11},{10,... | collective-permute-start | bytes 1572872 | tf_op jit(solution)/shard_map/ppermute | solution.py:48
  169.6 12.8 %collective-permute-start.9 = (bf16[128,2048]{1,0:T(8,128)(2,1)S(1)}, bf16[128,2048]{1,0:T(8,128)(2,1)S(1)}, u32[]{:S(2)}, u32[]{:S(2)}) collective-permute-start(bf16[128,2048]{1,0:T(8,128)(2,1)S(1)} %get-tuple-element.110), channel_id=1, source_target_pairs={{0,1},{1,0},{2,3},{3,2},{4,5},{5,4},{6,7},{7,6},{8,9},{9,8},{10,11... | collective-permute-start | bytes 1572872 | tf_op jit(solution)/shard_map/ppermute | solution.py:48
  182.8 23.4 %collective-permute-start.8 = (bf16[256,2048]{1,0:T(8,128)(2,1)S(1)}, bf16[256,2048]{1,0:T(8,128)(2,1)S(1)}, u32[]{:S(2)}, u32[]{:S(2)}) collective-permute-start(bf16[256,2048]{1,0:T(8,128)(2,1)S(1)} %pad_maximum_fusion.12), channel_id=1, source_target_pairs={{0,1},{1,0},{2,3},{3,2},{4,5},{5,4},{6,7},{7,6},{8,9},{9,8},{10,11... | collective-permute-start | bytes 3145736 | tf_op jit(solution)/shard_map/ppermute | solution.py:48
  184.5 23.1 %collective-permute-start.10 = (bf16[256,2048]{1,0:T(8,128)(2,1)S(1)}, bf16[256,2048]{1,0:T(8,128)(2,1)S(1)}, u32[]{:S(2)}, u32[]{:S(2)}) collective-permute-start(bf16[256,2048]{1,0:T(8,128)(2,1)S(1)} %pad_maximum_fusion.13), channel_id=1, source_target_pairs={{0,2},{1,3},{2,0},{3,1},{4,6},{5,7},{6,4},{7,5},{8,10},{9,11},{10,... | collective-permute-start | bytes 3145736 | tf_op jit(solution)/shard_map/ppermute | solution.py:48
  209.6 22.5 %collective-permute-start.11 = (bf16[256,2048]{1,0:T(8,128)(2,1)S(1)}, bf16[256,2048]{1,0:T(8,128)(2,1)S(1)}, u32[]{:S(2)}, u32[]{:S(2)}) collective-permute-start(bf16[256,2048]{1,0:T(8,128)(2,1)S(1)} %get-tuple-element.47), channel_id=1, source_target_pairs={{0,1},{1,0},{2,3},{3,2},{4,5},{5,4},{6,7},{7,6},{8,9},{9,8},{10,11... | collective-permute-start | bytes 3145736 | tf_op jit(solution)/shard_map/ppermute | solution.py:48
  210.2 23.1 %collective-permute-start.12 = (bf16[256,2048]{1,0:T(8,128)(2,1)S(1)}, bf16[256,2048]{1,0:T(8,128)(2,1)S(1)}, u32[]{:S(2)}, u32[]{:S(2)}) collective-permute-start(bf16[256,2048]{1,0:T(8,128)(2,1)S(1)} %get-tuple-element.47), channel_id=1, source_target_pairs={{0,2},{1,3},{2,0},{3,1},{4,6},{5,7},{6,4},{7,5},{8,10},{9,11},{10,... | collective-permute-start | bytes 3145736 | tf_op jit(solution)/shard_map/ppermute | solution.py:48
  232.2 11.2 %collective-permute-start.13 = (bf16[128,2048]{1,0:T(8,128)(2,1)S(1)}, bf16[128,2048]{1,0:T(8,128)(2,1)S(1)}, u32[]{:S(2)}, u32[]{:S(2)}) collective-permute-start(bf16[128,2048]{1,0:T(8,128)(2,1)S(1)} %slice.609), channel_id=1, source_target_pairs={{0,2},{1,3},{2,0},{3,1},{4,6},{5,7},{6,4},{7,5},{8,10},{9,11},{10,... | collective-permute-start | bytes 1572872 | tf_op jit(solution)/shard_map/ppermute | solution.py:48
  345.6 14.1 %collective-permute-start.15 = (bf16[128,2048]{1,0:T(8,128)(2,1)S(1)}, bf16[128,2048]{1,0:T(8,128)(2,1)S(1)}, u32[]{:S(2)}, u32[]{:S(2)}) collective-permute-start(bf16[128,2048]{1,0:T(8,128)(2,1)S(1)} %get-tuple-element.107), channel_id=1, source_target_pairs={{0,2},{1,3},{2,0},{3,1},{4,6},{5,7},{6,4},{7,5},{8,10},{9,11},{10,... | collective-permute-start | bytes 1572872 | tf_op jit(solution)/shard_map/ppermute | solution.py:48
  347.1 13.8 %collective-permute-start.17 = (bf16[128,2048]{1,0:T(8,128)(2,1)S(1)}, bf16[128,2048]{1,0:T(8,128)(2,1)S(1)}, u32[]{:S(2)}, u32[]{:S(2)}) collective-permute-start(bf16[128,2048]{1,0:T(8,128)(2,1)S(1)} %get-tuple-element.106), channel_id=1, source_target_pairs={{0,1},{1,0},{2,3},{3,2},{4,5},{5,4},{6,7},{7,6},{8,9},{9,8},{10,11... | collective-permute-start | bytes 1572872 | tf_op jit(solution)/shard_map/ppermute | solution.py:48
  362.2 24.5 %collective-permute-start.16 = (bf16[256,2048]{1,0:T(8,128)(2,1)}, bf16[256,2048]{1,0:T(8,128)(2,1)}, u32[]{:S(2)}, u32[]{:S(2)}) collective-permute-start(bf16[256,2048]{1,0:T(8,128)(2,1)} %pad_maximum_fusion.14), channel_id=1, source_target_pairs={{0,1},{1,0},{2,3},{3,2},{4,5},{5,4},{6,7},{7,6},{8,9},{9,8},{10,11... | collective-permute-start | bytes 3145736 | tf_op jit(solution)/shard_map/ppermute | solution.py:48
  364.8 24.2 %collective-permute-start.18 = (bf16[256,2048]{1,0:T(8,128)(2,1)}, bf16[256,2048]{1,0:T(8,128)(2,1)}, u32[]{:S(2)}, u32[]{:S(2)}) collective-permute-start(bf16[256,2048]{1,0:T(8,128)(2,1)} %pad_maximum_fusion.15), channel_id=1, source_target_pairs={{0,2},{1,3},{2,0},{3,1},{4,6},{5,7},{6,4},{7,5},{8,10},{9,11},{10,... | collective-permute-start | bytes 3145736 | tf_op jit(solution)/shard_map/ppermute | solution.py:48
  397.4 23.3 %collective-permute-start.19 = (bf16[256,2048]{1,0:T(8,128)(2,1)}, bf16[256,2048]{1,0:T(8,128)(2,1)S(1)}, u32[]{:S(2)}, u32[]{:S(2)}) collective-permute-start(bf16[256,2048]{1,0:T(8,128)(2,1)} %get-tuple-element.42), channel_id=1, source_target_pairs={{0,1},{1,0},{2,3},{3,2},{4,5},{5,4},{6,7},{7,6},{8,9},{9,8},{10,11... | collective-permute-start | bytes 3145736 | tf_op jit(solution)/shard_map/ppermute | solution.py:48
  397.9 24.1 %collective-permute-start.20 = (bf16[256,2048]{1,0:T(8,128)(2,1)}, bf16[256,2048]{1,0:T(8,128)(2,1)}, u32[]{:S(2)}, u32[]{:S(2)}) collective-permute-start(bf16[256,2048]{1,0:T(8,128)(2,1)} %get-tuple-element.42), channel_id=1, source_target_pairs={{0,2},{1,3},{2,0},{3,1},{4,6},{5,7},{6,4},{7,5},{8,10},{9,11},{10,... | collective-permute-start | bytes 3145736 | tf_op jit(solution)/shard_map/ppermute | solution.py:48
  421.4 11.4 %collective-permute-start.21 = (bf16[128,2048]{1,0:T(8,128)(2,1)}, bf16[128,2048]{1,0:T(8,128)(2,1)}, u32[]{:S(2)}, u32[]{:S(2)}) collective-permute-start(bf16[128,2048]{1,0:T(8,128)(2,1)} %slice.622), channel_id=1, source_target_pairs={{0,2},{1,3},{2,0},{3,1},{4,6},{5,7},{6,4},{7,5},{8,10},{9,11},{10,... | collective-permute-start | bytes 1572872 | tf_op jit(solution)/shard_map/ppermute | solution.py:48
  423.1 11.6 %collective-permute-start.22 = (bf16[128,2048]{1,0:T(8,128)(2,1)S(1)}, bf16[128,2048]{1,0:T(8,128)(2,1)S(1)}, u32[]{:S(2)}, u32[]{:S(2)}) collective-permute-start(bf16[128,2048]{1,0:T(8,128)(2,1)S(1)} %slice.623), channel_id=1, source_target_pairs={{0,1},{1,0},{2,3},{3,2},{4,5},{5,4},{6,7},{7,6},{8,9},{9,8},{10,11... | collective-permute-start | bytes 1572872 | tf_op jit(solution)/shard_map/ppermute | solution.py:48
  523.7 42.9 %collective-permute-start.28 = (bf16[1024,4096]{1,0:T(8,128)(2,1)}, bf16[1024,4096]{1,0:T(8,128)(2,1)}, u32[]{:S(2)}, u32[]{:S(2)}) collective-permute-start(bf16[1024,4096]{1,0:T(8,128)(2,1)} %convolution_convert_fusion), channel_id=1, source_target_pairs={{0,4},{4,0},{8,12},{12,8},{16,20},{20,16},{24,28},{28,24},{1,5},{5... | collective-permute-start | bytes 25165832 | tf_op jit(solution)/shard_map/ppermute | solution.py:147
  524.7 14.3 %collective-permute-start.24 = (bf16[128,2048]{1,0:T(8,128)(2,1)S(1)}, bf16[128,2048]{1,0:T(8,128)(2,1)S(1)}, u32[]{:S(2)}, u32[]{:S(2)}) collective-permute-start(bf16[128,2048]{1,0:T(8,128)(2,1)S(1)} %get-tuple-element.95), channel_id=1, source_target_pairs={{0,2},{1,3},{2,0},{3,1},{4,6},{5,7},{6,4},{7,5},{8,10},{9,11},{10,... | collective-permute-start | bytes 1572872 | tf_op jit(solution)/shard_map/ppermute | solution.py:48
  525.5 13.9 %collective-permute-start.26 = (bf16[128,2048]{1,0:T(8,128)(2,1)S(1)}, bf16[128,2048]{1,0:T(8,128)(2,1)S(1)}, u32[]{:S(2)}, u32[]{:S(2)}) collective-permute-start(bf16[128,2048]{1,0:T(8,128)(2,1)S(1)} %get-tuple-element.94), channel_id=1, source_target_pairs={{0,1},{1,0},{2,3},{3,2},{4,5},{5,4},{6,7},{7,6},{8,9},{9,8},{10,11... | collective-permute-start | bytes 1572872 | tf_op jit(solution)/shard_map/ppermute | solution.py:48
  539.8 24.4 %collective-permute-start.25 = (bf16[256,2048]{1,0:T(8,128)(2,1)S(1)}, bf16[256,2048]{1,0:T(8,128)(2,1)S(1)}, u32[]{:S(2)}, u32[]{:S(2)}) collective-permute-start(bf16[256,2048]{1,0:T(8,128)(2,1)S(1)} %pad_maximum_fusion.16), channel_id=1, source_target_pairs={{0,1},{1,0},{2,3},{3,2},{4,5},{5,4},{6,7},{7,6},{8,9},{9,8},{10,11... | collective-permute-start | bytes 3145736 | tf_op jit(solution)/shard_map/ppermute | solution.py:48
  540.7 24.1 %collective-permute-start.27 = (bf16[256,2048]{1,0:T(8,128)(2,1)S(1)}, bf16[256,2048]{1,0:T(8,128)(2,1)S(1)}, u32[]{:S(2)}, u32[]{:S(2)}) collective-permute-start(bf16[256,2048]{1,0:T(8,128)(2,1)S(1)} %pad_maximum_fusion.17), channel_id=1, source_target_pairs={{0,2},{1,3},{2,0},{3,1},{4,6},{5,7},{6,4},{7,5},{8,10},{9,11},{10,... | collective-permute-start | bytes 3145736 | tf_op jit(solution)/shard_map/ppermute | solution.py:48
  589.8 23.4 %collective-permute-start.29 = (bf16[256,2048]{1,0:T(8,128)(2,1)}, bf16[256,2048]{1,0:T(8,128)(2,1)S(1)}, u32[]{:S(2)}, u32[]{:S(2)}) collective-permute-start(bf16[256,2048]{1,0:T(8,128)(2,1)} %get-tuple-element.39), channel_id=1, source_target_pairs={{0,1},{1,0},{2,3},{3,2},{4,5},{5,4},{6,7},{7,6},{8,9},{9,8},{10,11... | collective-permute-start | bytes 3145736 | tf_op jit(solution)/shard_map/ppermute | solution.py:48
  591.1 24.5 %collective-permute-start.30 = (bf16[256,2048]{1,0:T(8,128)(2,1)}, bf16[256,2048]{1,0:T(8,128)(2,1)}, u32[]{:S(2)}, u32[]{:S(2)}) collective-permute-start(bf16[256,2048]{1,0:T(8,128)(2,1)} %get-tuple-element.39), channel_id=1, source_target_pairs={{0,2},{1,3},{2,0},{3,1},{4,6},{5,7},{6,4},{7,5},{8,10},{9,11},{10,... | collective-permute-start | bytes 3145736 | tf_op jit(solution)/shard_map/ppermute | solution.py:48
  614.0 11.5 %collective-permute-start.31 = (bf16[128,2048]{1,0:T(8,128)(2,1)}, bf16[128,2048]{1,0:T(8,128)(2,1)}, u32[]{:S(2)}, u32[]{:S(2)}) collective-permute-start(bf16[128,2048]{1,0:T(8,128)(2,1)} %slice.644), channel_id=1, source_target_pairs={{0,2},{1,3},{2,0},{3,1},{4,6},{5,7},{6,4},{7,5},{8,10},{9,11},{10,... | collective-permute-start | bytes 1572872 | tf_op jit(solution)/shard_map/ppermute | solution.py:48
  615.5 191.5 %reduce-scatter.4.cloned.1.call-start = ((), (), s32[]{:S(2)}) async-start(), calls=%async_computation.6 | async-start | bytes 5242880 | tf_op jit(solution)/shard_map/reduce_scatter | solution.py:154
  616.8 11.0 %collective-permute-start.32 = (bf16[128,2048]{1,0:T(8,128)(2,1)S(1)}, bf16[128,2048]{1,0:T(8,128)(2,1)S(1)}, u32[]{:S(2)}, u32[]{:S(2)}) collective-permute-start(bf16[128,2048]{1,0:T(8,128)(2,1)S(1)} %slice.645), channel_id=1, source_target_pairs={{0,1},{1,0},{2,3},{3,2},{4,5},{5,4},{6,7},{7,6},{8,9},{9,8},{10,11... | collective-permute-start | bytes 1572872 | tf_op jit(solution)/shard_map/ppermute | solution.py:48
  681.8 15.6 %collective-permute-start.45 = (f32[2,4,256]{2,1,0:T(4,128)S(1)}, f32[2,4,256]{2,1,0:T(4,128)S(1)}, u32[]{:S(2)}, u32[]{:S(2)}) collective-permute-start(f32[2,4,256]{2,1,0:T(4,128)S(1)} %constant_dynamic-update-slice_fusion.25), channel_id=1, source_target_pairs={{0,3},{1,2},{2,1},{3,0},{4,7},{5,6},{6,5},{7,4},{8,11},{9,10},{10,... | collective-permute-start | bytes 24584 | tf_op jit(solution)/shard_map/ppermute | solution.py:48
  683.5 13.9 %collective-permute-start.44 = (f32[2,4,256]{2,1,0:T(4,128)S(1)}, f32[2,4,256]{2,1,0:T(4,128)S(1)}, u32[]{:S(2)}, u32[]{:S(2)}) collective-permute-start(f32[2,4,256]{2,1,0:T(4,128)S(1)} %constant_dynamic-update-slice_fusion.25), channel_id=1, source_target_pairs={{0,2},{1,3},{2,0},{3,1},{4,6},{5,7},{6,4},{7,5},{8,10},{9,11},{10,... | collective-permute-start | bytes 24584 | tf_op jit(solution)/shard_map/ppermute | solution.py:48
  684.5 12.9 %collective-permute-start.43 = (f32[2,4,256]{2,1,0:T(4,128)S(1)}, f32[2,4,256]{2,1,0:T(4,128)S(1)}, u32[]{:S(2)}, u32[]{:S(2)}) collective-permute-start(f32[2,4,256]{2,1,0:T(4,128)S(1)} %constant_dynamic-update-slice_fusion.25), channel_id=1, source_target_pairs={{0,1},{1,0},{2,3},{3,2},{4,5},{5,4},{6,7},{7,6},{8,9},{9,8},{10,11... | collective-permute-start | bytes 24584 | tf_op jit(solution)/shard_map/ppermute | solution.py:48
  707.0 14.8 %collective-permute-start.46 = (bf16[1024,1536]{1,0:T(8,128)(2,1)}, bf16[1024,1536]{1,0:T(8,128)(2,1)}, u32[]{:S(2)}, u32[]{:S(2)}) collective-permute-start(bf16[1024,1536]{1,0:T(8,128)(2,1)} %convolution_convert_fusion.1), channel_id=1, source_target_pairs={{0,4},{4,0},{8,12},{12,8},{16,20},{20,16},{24,28},{28,24},{1,5},{5... | collective-permute-start | bytes 9437192 | tf_op jit(solution)/shard_map/ppermute | solution.py:147
  730.9 223.4 %reduce-scatter.6.cloned.1.call-start = ((), (), s32[]{:S(2)}) async-start(), calls=%async_computation.7 | async-start | bytes 10485760 | tf_op jit(solution)/shard_map/reduce_scatter | solution.py:154
  743.2 14.7 %collective-permute-start.48 = (bf16[128,2048]{1,0:T(8,128)(2,1)S(1)}, bf16[128,2048]{1,0:T(8,128)(2,1)S(1)}, u32[]{:S(2)}, u32[]{:S(2)}) collective-permute-start(bf16[128,2048]{1,0:T(8,128)(2,1)S(1)} %get-tuple-element.67), channel_id=1, source_target_pairs={{0,2},{1,3},{2,0},{3,1},{4,6},{5,7},{6,4},{7,5},{8,10},{9,11},{10,... | collective-permute-start | bytes 1572872 | tf_op jit(solution)/shard_map/ppermute | solution.py:48
  744.4 14.8 %collective-permute-start.50 = (bf16[128,2048]{1,0:T(8,128)(2,1)S(1)}, bf16[128,2048]{1,0:T(8,128)(2,1)S(1)}, u32[]{:S(2)}, u32[]{:S(2)}) collective-permute-start(bf16[128,2048]{1,0:T(8,128)(2,1)S(1)} %get-tuple-element.66), channel_id=1, source_target_pairs={{0,1},{1,0},{2,3},{3,2},{4,5},{5,4},{6,7},{7,6},{8,9},{9,8},{10,11... | collective-permute-start | bytes 1572872 | tf_op jit(solution)/shard_map/ppermute | solution.py:48
  746.3 18.9 %collective-permute-start.33 = (f32[8,2048]{1,0:T(8,128)S(1)}, f32[8,2048]{1,0:T(8,128)S(1)}, u32[]{:S(2)}, u32[]{:S(2)}) collective-permute-start(f32[8,2048]{1,0:T(8,128)S(1)} %concatenate.138), channel_id=1, source_target_pairs={{0,1},{1,0},{2,3},{3,2},{4,5},{5,4},{6,7},{7,6},{8,9},{9,8},{10,11... | collective-permute-start | bytes 196616 | tf_op jit(solution)/shard_map/ppermute | solution.py:48
  747.3 17.9 %collective-permute-start.34 = (f32[8,2048]{1,0:T(8,128)S(1)}, f32[8,2048]{1,0:T(8,128)S(1)}, u32[]{:S(2)}, u32[]{:S(2)}) collective-permute-start(f32[8,2048]{1,0:T(8,128)S(1)} %concatenate.138), channel_id=1, source_target_pairs={{0,2},{1,3},{2,0},{3,1},{4,6},{5,7},{6,4},{7,5},{8,10},{9,11},{10,... | collective-permute-start | bytes 196616 | tf_op jit(solution)/shard_map/ppermute | solution.py:48
  748.2 17.0 %collective-permute-start.35 = (f32[8,2048]{1,0:T(8,128)S(1)}, f32[8,2048]{1,0:T(8,128)S(1)}, u32[]{:S(2)}, u32[]{:S(2)}) collective-permute-start(f32[8,2048]{1,0:T(8,128)S(1)} %concatenate.138), channel_id=1, source_target_pairs={{0,3},{1,2},{2,1},{3,0},{4,7},{5,6},{6,5},{7,4},{8,11},{9,10},{10,... | collective-permute-start | bytes 196616 | tf_op jit(solution)/shard_map/ppermute | solution.py:48
  762.1 23.4 %collective-permute-start.49 = (bf16[256,2048]{1,0:T(8,128)(2,1)}, bf16[256,2048]{1,0:T(8,128)(2,1)}, u32[]{:S(2)}, u32[]{:S(2)}) collective-permute-start(bf16[256,2048]{1,0:T(8,128)(2,1)} %pad_maximum_fusion.18), channel_id=1, source_target_pairs={{0,1},{1,0},{2,3},{3,2},{4,5},{5,4},{6,7},{7,6},{8,9},{9,8},{10,11... | collective-permute-start | bytes 3145736 | tf_op jit(solution)/shard_map/ppermute | solution.py:48
  764.2 23.0 %collective-permute-start.51 = (bf16[256,2048]{1,0:T(8,128)(2,1)}, bf16[256,2048]{1,0:T(8,128)(2,1)S(1)}, u32[]{:S(2)}, u32[]{:S(2)}) collective-permute-start(bf16[256,2048]{1,0:T(8,128)(2,1)} %pad_maximum_fusion.19), channel_id=1, source_target_pairs={{0,2},{1,3},{2,0},{3,1},{4,6},{5,7},{6,4},{7,5},{8,10},{9,11},{10,... | collective-permute-start | bytes 3145736 | tf_op jit(solution)/shard_map/ppermute | solution.py:48
  (90 other events, 883.1 us)
Sparse Core Ops, SparseCore 0:
  13.2 85.1 all-gather.4
  100.6 149.6 all-gather.6
  251.9 80.6 all-gather.8
  615.6 74.8 reduce-scatter.7
  731.0 75.9 reduce-scatter.3
  809.2 145.0 reduce-scatter.5
where the time goes:
time: 971 us; the launch traced here: 967 us
  waiting for transfers between devices  467 us (48%)
  matrix products  215 us (22%)
  local copies, waits for them, and re-layouts  102 us (11%)
  other arithmetic  93.2 us (10%)
  starting transfers between devices  55.8 us (6%)
  between operations  18.5 us (2%)
  blocking collectives  15.6 us (2%)
    ppermute x41, waiting for transfers between devices, hop(): return lax.ppermute(value, 'tensor', [(i, i ^ way) for i in range(size)])  219 us
    reduce_scatter x3, waiting for transfers between devices, scatter_pairs(): lax.psum_scatter(value, 'dp', scatter_dimension=axis, axis_index_groups=g...  160 us
    dot_general x8, matrix products, inner_rows(): lax.dot_general(left, right, (((0,), (0,)), ((), ())), preferred_element_...  60.8 us
    dot_general x4, matrix products, times_transposed(): lax.dot_general(left, right, (((1,), (1,)), ((), ())), preferred_element_...  57.5 us
    all_gather x1, waiting for transfers between devices, layer(): full_down = lax.all_gather(wd, 'dp', axis=1, tiled=True)  50.7 us
    ppermute x41, starting transfers between devices, hop(): return lax.ppermute(value, 'tensor', [(i, i ^ way) for i in range(size)])  48.7 us
    dot_general x4, matrix products, times(): return jnp.dot(left, right, preferred_element_type=F32)  47 us
    unnamed x190, local copies, waits for them, and re-layouts  44.7 us
  transfers between devices with their start and end apart: 58, of which 36 were waited for; matrix products, arithmetic and copies ran while one was open for 26% of the time, Pallas kernels for 0%

commit v1 on v0

--- a/solution.py
+++ b/solution.py
@@ -1,6 +1,8 @@
 import jax
 import jax.numpy as jnp
 from jax import lax
+from jax.experimental import pallas as pl
+from jax.experimental.pallas import tpu as pltpu
 from jax.sharding import PartitionSpec as P
 
 
@@ -9,6 +11,7 @@
 EPS = 1e-06
 THETA = 500000.0
 NEGATIVE = -1e30
+BLOCK = 256
 BF = jnp.bfloat16
 F32 = jnp.float32
 
@@ -26,12 +29,6 @@
     return values * cosines + turned * sines
 
 
-def unrotate(grad, cosines, sines):
-    half = grad.shape[-1] // 2
-    turned = grad * sines
-    return grad * cosines + jnp.concatenate([turned[..., half:], -turned[..., :half]], axis=-1)
-
-
 def inner_rows(left, right):
     return lax.dot_general(left, right, (((0,), (0,)), ((), ())), preferred_element_type=F32)
 
@@ -50,6 +47,7 @@
 
 class Square:
     def __init__(self, size):
+        self.size = size
         self.me = lax.axis_index("tensor")
         self.order = self.me ^ jnp.arange(size)
 
@@ -88,6 +86,7 @@
 
 class Plain:
     def __init__(self, size):
+        self.size = size
         self.me = lax.axis_index("tensor")
         self.order = jnp.arange(size)
 
@@ -117,18 +116,135 @@
     return (mixed.astype(BF), (highest + jnp.log(total))[..., 0])
 
 
-def attend_backward(query, key, value, allowed, logsum, grad_mixed):
-    scores = jnp.einsum("qhd,khd->hqk", query, key, preferred_element_type=F32) * HD ** (-0.5)
-    scores = jnp.where(allowed[None], scores, NEGATIVE)
-    prob = jnp.exp(scores - logsum[..., None])
-    grad_prob = jnp.einsum("qhd,khd->hqk", grad_mixed, value, preferred_element_type=F32)
-    delta = jnp.sum(grad_prob * prob, axis=-1, keepdims=True)
-    grad_scores = (prob * (grad_prob - delta)).astype(BF)
+def contract(left, right, left_axis, right_axis):
+    return lax.dot_general(
+        left, right, (((left_axis,), (right_axis,)), ((), ())), preferred_element_type=F32
+    )
+
+
+def cost(flops, *arrays):
+    moved = sum(a.size * jnp.dtype(a.dtype).itemsize for a in arrays)
+    return pl.CostEstimate(flops=flops, bytes_accessed=moved, transcendentals=0)
+
+
+def turn_back(grad, cosine, sine):
+    return grad * cosine + pltpu.roll(grad * sine, HD // 2, 1)
+
+
+def attend_backward(query, key, value, grad_mixed, logsum, bias, cosine, sine, block=512):
+    group, width = query.shape
+    heads = width // HD
     factor = HD ** (-0.5)
-    grad_value = jnp.einsum("hqk,qhd->khd", prob.astype(BF), grad_mixed, preferred_element_type=F32)
-    grad_query = jnp.einsum("hqk,khd->qhd", grad_scores, key, preferred_element_type=F32) * factor
-    grad_key = jnp.einsum("hqk,qhd->khd", grad_scores, query, preferred_element_type=F32) * factor
-    return (grad_query, grad_key, grad_value.astype(BF))
+    steps = group // block
+
+    def body(q_ref, k_ref, v_ref, g_ref, l_ref, b_ref, c_ref, s_ref, cq_ref, sq_ref, dq_ref, dk_ref, dv_ref, ak, av):
+        head = pl.program_id(0)
+        step = pl.program_id(1)
+
+        @pl.when(step == 0)
+        def _():
+            ak[...] = jnp.zeros_like(ak)
+            av[...] = jnp.zeros_like(av)
+
+        q = q_ref[...]
+        k = k_ref[...]
+        g = g_ref[...]
+        scores = contract(k, q, 1, 1) * factor + b_ref[...]
+        prob = jnp.exp(scores - l_ref[pl.ds(head, 1), :])
+        grad_prob = contract(v_ref[...], g, 1, 1)
+        delta = jnp.sum(prob * grad_prob, axis=0, keepdims=True)
+        grad_scores = (prob * (grad_prob - delta)).astype(BF)
+        av[...] += contract(prob.astype(BF), g, 1, 0)
+        ak[...] += contract(grad_scores, q, 1, 0)
+        dq_ref[...] = turn_back(contract(grad_scores, k, 0, 0) * factor, cq_ref[...], sq_ref[...])
+
+        @pl.when(step == steps - 1)
+        def _():
+            dk_ref[...] = turn_back(ak[...] * factor, c_ref[...], s_ref[...])
+            dv_ref[...] = av[...].astype(BF)
+
+    part = pl.BlockSpec((block, HD), lambda h, i: (i, h))
+    whole = pl.BlockSpec((group, HD), lambda h, i: (0, h))
+    table = pl.BlockSpec((group, HD), lambda h, i: (0, 0))
+    table_part = pl.BlockSpec((block, HD), lambda h, i: (i, 0))
+    return pl.pallas_call(
+        body,
+        grid=(heads, steps),
+        in_specs=[
+            part, whole, whole, part,
+            pl.BlockSpec((heads, block), lambda h, i: (0, i)),
+            pl.BlockSpec((group, block), lambda h, i: (0, i)),
+            table, table, table_part, table_part,
+        ],
+        out_specs=[part, whole, whole],
+        out_shape=[
+            jax.ShapeDtypeStruct((group, width), F32),
+            jax.ShapeDtypeStruct((group, width), F32),
+            jax.ShapeDtypeStruct((group, width), BF),
+        ],
+        scratch_shapes=[pltpu.VMEM((group, HD), F32), pltpu.VMEM((group, HD), F32)],
+        cost_estimate=cost(10 * group * group * width, bias, query, key, value, grad_mixed),
+        name="attend_backward",
+    )(query, key, value, grad_mixed, logsum, bias, cosine, sine, cosine, sine)
+
+
+def pair_backward(piece, down, pair, block=BLOCK):
+    group, width = piece.shape
+    units = down.shape[0]
+
+    def body(g_ref, w_ref, p_ref, o_ref):
+        grad = contract(g_ref[...], w_ref[...], 1, 1)
+        gate = p_ref[:, :block]
+        up = p_ref[:, block:]
+        sigma = 1.0 / (1.0 + jnp.exp(-gate))
+        o_ref[:, :block] = (grad * up * sigma * (1.0 + gate * (1.0 - sigma))).astype(BF)
+        o_ref[:, block:] = (grad * (gate * sigma)).astype(BF)
+
+    return pl.pallas_call(
+        body,
+        grid=(units // block,),
+        in_specs=[
+            pl.BlockSpec((group, width), lambda j: (0, 0)),
+            pl.BlockSpec((block, width), lambda j: (j, 0)),
+            pl.BlockSpec((group, 2 * block), lambda j: (0, j)),
+        ],
+        out_specs=pl.BlockSpec((group, 2 * block), lambda j: (0, j)),
+        out_shape=jax.ShapeDtypeStruct((group, 2 * units), BF),
+        cost_estimate=cost(2 * group * width * units, piece, down, pair),
+        compiler_params=pltpu.CompilerParams(vmem_limit_bytes=48 << 20),
+        name="pair_backward",
+    )(piece, down, pair)
+
+
+def pair_forward(rows, weights, block=BLOCK):
+    group, width = rows.shape
+    units = weights.shape[1] // 2
+
+    def body(x_ref, w_ref, p_ref, h_ref):
+        both = contract(x_ref[...], w_ref[...], 1, 0)
+        p_ref[...] = both
+        gate = both[:, :block]
+        h_ref[...] = (gate / (1.0 + jnp.exp(-gate)) * both[:, block:]).astype(BF)
+
+    return pl.pallas_call(
+        body,
+        grid=(units // block,),
+        in_specs=[
+            pl.BlockSpec((group, width), lambda j: (0, 0)),
+            pl.BlockSpec((width, 2 * block), lambda j: (0, j)),
+        ],
+        out_specs=[
+            pl.BlockSpec((group, 2 * block), lambda j: (0, j)),
+            pl.BlockSpec((group, block), lambda j: (0, j)),
+        ],
+        out_shape=[
+            jax.ShapeDtypeStruct((group, 2 * units), F32),
+            jax.ShapeDtypeStruct((group, units), BF),
+        ],
+        cost_estimate=cost(4 * group * width * units, rows, weights),
+        compiler_params=pltpu.CompilerParams(vmem_limit_bytes=48 << 20),
+        name="pair_forward",
+    )(rows, weights)
 
 
 def pick_halves(array, axis):
@@ -141,11 +257,21 @@
     return jnp.where(first, odd, even), jnp.where(first, even, odd)
 
 
+def swap_cores(value):
+    return lax.ppermute(value, "dp", [(i, i ^ 1) for i in range(lax.axis_size("dp"))])
+
+
 def pair_sum(product, sides):
-    size = lax.axis_size("dp")
-    theirs = product(sides[0]).astype(BF)
-    got = lax.ppermute(theirs, "dp", [(i, i ^ 1) for i in range(size)])
+    got = swap_cores(product(sides[0]).astype(BF))
     return (product(sides[1]) + got.astype(F32)).astype(BF)
+
+
+def interleave(left, right, block):
+    count = left.shape[1] // block
+    parts = []
+    for i in range(count):
+        parts += [left[:, i * block : (i + 1) * block], right[:, i * block : (i + 1) * block]]
+    return jnp.concatenate(parts, axis=1)
 
 
 def scatter_pairs(value, axis):
@@ -183,7 +309,7 @@
     wo_side = jnp.concatenate([wo[i * share : (i + 1) * share] for i in range(pieces)], axis=1)
     attn_shard = jnp.concatenate([wq, wk, wv, wo_side], axis=1)
     attn_all = lax.all_gather(attn_shard, "dp", axis=0, tiled=True)
-    pair_all = lax.all_gather(jnp.concatenate([wg, wu], axis=1), "dp", axis=0, tiled=True)
+    pair_all = lax.all_gather(interleave(wg, wu, BLOCK), "dp", axis=0, tiled=True)
     full_down = lax.all_gather(wd, "dp", axis=1, tiled=True)
 
     counted = jnp.sum((segment != 0).astype(F32))
@@ -205,7 +331,12 @@
     position_rel = jnp.take(position.reshape(tensor, rows), ring.order, axis=0).reshape(group)
     place = (ring.order[:, None] * rows + jnp.arange(rows)[None, :]).reshape(group)
     allowed = (segment_rel[:, None] == segment_rel[None, :]) & (place[:, None] >= place[None, :])
+    bias = jnp.where(
+        (segment_rel[:, None] == segment_rel[None, :]) & (place[:, None] <= place[None, :]), 0.0, NEGATIVE
+    )
     cosines, sines = tables(position_rel)
+    flat_cosines = cosines[:, 0]
+    flat_sines = jnp.concatenate([-sines[:, 0, : HD // 2], sines[:, 0, HD // 2 :]], axis=1)
 
     whole_inputs = ring.gather(inputs)
     qkv = attn_all[:, : 3 * local_width]
@@ -218,7 +349,7 @@
     raw = times(whole_inputs, qkv)
     raw_q = raw[:, :local_width]
     raw_k = raw[:, local_width : 2 * local_width]
-    value = raw[:, 2 * local_width :].astype(BF).reshape(group, heads_here, HD)
+    value = raw[:, 2 * local_width :].astype(BF)
     squares = ring.total_by_token(jnp.stack([jnp.sum(raw_q * raw_q, axis=1), jnp.sum(raw_k * raw_k, axis=1)]))
     scales = lax.rsqrt(squares / width + EPS)
     scale_q = scales[0][:, None]
@@ -229,7 +360,9 @@
         (normed_q * gain_qk[0]).reshape(group, heads_here, HD), cosines, sines
     ).astype(BF)
     key = rotate((normed_k * gain_qk[1]).reshape(group, heads_here, HD), cosines, sines).astype(BF)
-    mixed, logsum = attend_forward(query, key, value, allowed)
+    mixed, logsum = attend_forward(query, key, value.reshape(group, heads_here, HD), allowed)
+    query = query.reshape(group, local_width)
+    key = key.reshape(group, local_width)
     attn_rows = mixed.reshape(group, local_width)
     branch_attn = ring.scatter(times(attn_rows, full_out))
     scale_attn = lax.rsqrt(jnp.mean(branch_attn * branch_attn, axis=1, keepdims=True) + EPS)
@@ -237,12 +370,7 @@
     resid = inputs.astype(F32) + normed_attn * gain_attn
     whole_h = ring.gather(resid.astype(BF))
 
-    pair = times(whole_h, pair_all)
-    gate = pair[:, :units]
-    up = pair[:, units:]
-    sigma = jax.nn.sigmoid(gate)
-    activated = gate * sigma
-    hidden = (activated * up).astype(BF)
+    pair, hidden = pair_forward(whole_h, pair_all)
     branch_ffn = ring.scatter(times(hidden, full_down))
     scale_ffn = lax.rsqrt(jnp.mean(branch_ffn * branch_ffn, axis=1, keepdims=True) + EPS)
     normed_ffn = branch_ffn * scale_ffn
@@ -263,14 +391,15 @@
     grad_down = pair_sum(lambda side: inner_rows(hidden, side), pick_halves(piece, 1))
     sum_down = scatter_pairs(grad_down, 1)
     piece, grad_down = lax.optimization_barrier((piece, grad_down))
-    grad_hidden = times_transposed(piece, full_down)
-    grad_gate = (grad_hidden * up * sigma * (1.0 + gate * (1.0 - sigma))).astype(BF)
-    grad_up = (grad_hidden * activated).astype(BF)
-    grad_pair = jnp.concatenate([grad_gate, grad_up], axis=1)
+    grad_pair = pair_backward(piece, full_down, pair)
+    mine = pick_halves(whole_h, 1)
+    theirs = inner_rows(mine[0], grad_pair).astype(BF)
+    grad_pair, theirs = lax.optimization_barrier((grad_pair, theirs))
+    got = swap_cores(theirs)
     back_h = times_transposed(grad_pair, pair_all)
     back_h, grad_pair = lax.optimization_barrier((back_h, grad_pair))
     back_h = ring.scatter(back_h)
-    pair_grads = pair_sum(lambda side: inner_rows(side, grad_pair), pick_halves(whole_h, 1))
+    pair_grads = (inner_rows(mine[1], grad_pair) + got.astype(F32)).astype(BF)
     sum_pair = scatter_pairs(pair_grads, 0)
     back_h, pair_grads = lax.optimization_barrier((back_h, pair_grads))
     grad_resid = grad_output + back_h
@@ -281,19 +410,16 @@
         * (grad_normed - normed_attn * jnp.mean(grad_normed * normed_attn, axis=1, keepdims=True))
     ).astype(BF)
     piece = ring.gather(grad_branch_attn)
-    grad_mixed = times_transposed(piece, full_out).astype(BF).reshape(group, heads_here, HD)
+    grad_mixed = times_transposed(piece, full_out).astype(BF)
     out_grads = pair_sum(lambda side: inner_rows(attn_rows, side), pick_halves(piece, 1))
     out_grads = (
         out_grads.reshape(pieces, share, dp // 2, share)
         .transpose(2, 1, 0, 3)
         .reshape(dp // 2 * share, pieces * share)
     )
-    grad_query, grad_key, grad_value = attend_backward(
-        query, key, value, allowed, logsum, grad_mixed
-    )
-    grad_normed_q = unrotate(grad_query, cosines, sines).reshape(group, local_width)
-    grad_normed_k = unrotate(grad_key, cosines, sines).reshape(group, local_width)
-    grad_value = grad_value.reshape(group, local_width)
+    grad_normed_q, grad_normed_k, grad_value = attend_backward(
+        query, key, value, grad_mixed, logsum, bias, flat_cosines, flat_sines
+    )
     grad_hat_q = grad_normed_q * gain_qk[0]
     grad_hat_k = grad_normed_k * gain_qk[1]
     inner = ring.total_by_token(
@@ -326,7 +452,7 @@
     sum_attn = sum_attn.astype(F32)
     sum_out = sum_attn[:, 3 * local_width :].reshape(share, pieces, share)
     sum_out = sum_out.transpose(1, 0, 2).reshape(local_width, share)
-    sum_pair = sum_pair.astype(F32)
+    sum_pair = sum_pair.astype(F32).reshape(share, units // BLOCK, 2, BLOCK)
     return (
         output.astype(BF),
         loss,
@@ -335,8 +461,8 @@
         sum_attn[:, local_width : 2 * local_width],
         sum_attn[:, 2 * local_width : 3 * local_width],
         sum_out,
-        sum_pair[:, :units],
-        sum_pair[:, units:],
+        sum_pair[:, :, 0].reshape(share, units),
+        sum_pair[:, :, 1].reshape(share, units),
         sum_down.astype(F32),
         late[0],
         late[1],

time: 971 us -> 957 us (0.986)
  matrix products: 215 us -> 146 us
  Pallas kernels: 0 us -> 62.8 us
  local copies, waits for them, and re-layouts: 102 us -> 125 us
  other arithmetic: 93.2 us -> 73.6 us
  waiting for transfers between devices: 467 us -> 451 us
    pallas_call x0 -> x3, Pallas kernels: none -> 62.8 us  [the longest x1 23.5 us: pair_forward(): pl.pallas_call(body, grid=(units // block,), in_specs=[pl.BlockSpec((grou...]
    dot_general x4 -> x0, matrix products: 31.9 us -> none  [the longest x1 14.2 us: attend_backward(): jnp.einsum('qhd,khd->hqk', grad_mixed, value, preferred_element_type=F32)]
    dot_general x4 -> x3, matrix products: 47 us -> 25 us  [times(): return jnp.dot(left, right, preferred_element_type=F32)]
    dot_general x4 -> x3, matrix products: 57.5 us -> 36.6 us  [times_transposed(): lax.dot_general(left, right, (((1,), (1,)), ((), ())), preferred_element_...]
    unnamed x190 -> x235, local copies, waits for them, and re-layouts: 44.7 us -> 60.9 us
    convert_element_type x2 -> x0, other arithmetic: 14.5 us -> none  [the longest x1 10.6 us: attend_backward(): grad_scores = (prob * (grad_prob - delta)).astype(BF)]
    all_gather x1, waiting for transfers between devices: 21.6 us -> 9.13 us  [layer(): attn_all = lax.all_gather(attn_shard, 'dp', axis=0, tiled=True)]
    slice x3 -> x4, local copies, waits for them, and re-layouts: 4.16 us -> 16.2 us  [the longest x1 14.3 us: layer(): sum_pair[:, :, 1].reshape(share, units)]
  transfers between devices with their start and end apart: 58 -> 58, of which waited for: 36 -> 36; matrix products, arithmetic and copies ran while one was open for 26% -> 23% of each run, Pallas kernels for 0% -> 5%
where the time goes in v1:
time: 957 us; the launch traced here: 948 us
  waiting for transfers between devices  451 us (47%)
  matrix products  146 us (15%)
  local copies, waits for them, and re-layouts  125 us (13%)
  other arithmetic  73.6 us (8%)
  Pallas kernels  62.8 us (7%)
  starting transfers between devices  55.3 us (6%)
  between operations  18.7 us (2%)
  blocking collectives  14.7 us (2%)
    ppermute x41, waiting for transfers between devices, hop(): return lax.ppermute(value, 'tensor', [(i, i ^ way) for i in range(size)])  214 us
    reduce_scatter x3, waiting for transfers between devices, scatter_pairs(): lax.psum_scatter(value, 'dp', scatter_dimension=axis, axis_index_groups=g...  160 us
    dot_general x8, matrix products, inner_rows(): lax.dot_general(left, right, (((0,), (0,)), ((), ())), preferred_element_...  62.8 us
    unnamed x235, local copies, waits for them, and re-layouts  60.9 us
    all_gather x1, waiting for transfers between devices, layer(): full_down = lax.all_gather(wd, 'dp', axis=1, tiled=True)  53.7 us
    ppermute x41, starting transfers between devices, hop(): return lax.ppermute(value, 'tensor', [(i, i ^ way) for i in range(size)])  48.3 us
    dot_general x3, matrix products, times_transposed(): lax.dot_general(left, right, (((1,), (1,)), ((), ())), preferred_element_...  36.6 us
    dot_general x3, matrix products, times(): return jnp.dot(left, right, preferred_element_type=F32)  25 us
  transfers between devices with their start and end apart: 58, of which 36 were waited for; matrix products, arithmetic and copies ran while one was open for 23% of the time, Pallas kernels for 5%

profile of v1, /device:TPU:0, one launch (start us, length us, event | category | flops | bytes accessed | tf_op | source)
XLA Modules:
  0.0 947.6 jit_solution(11977709933286098998)
XLA Ops:
  43.0 12.7 %collective-permute-done = bf16[256,2048]{1,0:T(8,128)(2,1)S(1)} collective-permute-done((bf16[256,2048]{1,0:T(8,128)(2,1)S(1)}, bf16[256,2048]{1,0:T(8,128)(2,1)S(1)}, u32[]{:S(2)}, u32[]{:S(2)}) %collective-permute-start) | collective-permute-done | bytes 1048608 | tf_op jit(solution)/shard_map/ppermute | solution.py:45
  58.4 14.7 %all-gather = f32[8,2048]{1,0:T(8,128)S(1)} all-gather(f32[8,256]{1,0:T(8,128)S(1)} %concatenate.120), channel_id=2, replica_groups=mesh['dp'=8,'tensor'=4] {'dp'}, dimensions={1}, use_global_device_ids=true | all-gather | bytes 73728 | tf_op jit(solution)/shard_map/all_gather | solution.py:322
  80.9 7.5 collective-permute-done.3
  89.2 9.1 all-gather.5.cloned.1.call-done
  98.4 10.0 %fusion.5 = f32[1024,1536]{1,0:T(8,128)S(1)} fusion(bf16[1024,2048]{1,0:T(8,128)(2,1)} %constant_dynamic-update-slice_fusion, bf16[2048,2048]{1,0:T(8,128)(2,1)} %all-gather.5.cloned.1.call-done), kind=kOutput, calls=%fused_computation.14 | convolution fusion | flops 6442450944 | bytes 16777216 | tf_op jit(solution)/shard_map/dot_general | solution.py:37
  108.4 3.4 copy-done.3
  120.2 3.4 slice.648
  139.2 14.7 %fusion = (f32[4,1024]{1,0:T(4,128)S(1)}, f32[4,1024,1024]{1,2,0:T(8,128)}) fusion(pred[1024,1024]{0,1:T(8,128)(4,1)} %copy.73, f32[1024,128]{1,0:T(8,128)} %get-tuple-element.142.c_ref.cq_ref, f32[1024,128]{1,0:T(8,128)} %get-tuple-element.141, f32[1024,4,64]{2,0,1:T(8,128)S(1)} %get-tuple-element.132, f32[1024,4,64]{2,0,1:T(8,128)S(1)} %get-tuple-element.131, ...), kind=kOutput, calls=%fused_computation.6 | convolution fusion | flops 1091563520 | bytes 27279360 | tf_op jit(solution)/shard_map/qhd,khd->hqk/dot_general | solution.py:109
  153.9 8.7 fusion.1
  165.5 7.1 fusion.41
  178.3 10.3 %collective-permute-done.9 = bf16[128,2048]{1,0:T(8,128)(2,1)S(1)} collective-permute-done((bf16[128,2048]{1,0:T(8,128)(2,1)S(1)}, bf16[128,2048]{1,0:T(8,128)(2,1)S(1)}, u32[]{:S(2)}, u32[]{:S(2)}) %collective-permute-start.9) | collective-permute-done | bytes 524320 | tf_op jit(solution)/shard_map/ppermute | solution.py:45
  192.5 21.3 %collective-permute-done.10 = bf16[256,2048]{1,0:T(8,128)(2,1)S(1)} collective-permute-done((bf16[256,2048]{1,0:T(8,128)(2,1)S(1)}, bf16[256,2048]{1,0:T(8,128)(2,1)S(1)}, u32[]{:S(2)}, u32[]{:S(2)}) %collective-permute-start.10) | collective-permute-done | bytes 1048608 | tf_op jit(solution)/shard_map/ppermute | solution.py:45
  218.3 21.4 %collective-permute-done.11 = bf16[256,2048]{1,0:T(8,128)(2,1)S(1)} collective-permute-done((bf16[256,2048]{1,0:T(8,128)(2,1)S(1)}, bf16[256,2048]{1,0:T(8,128)(2,1)S(1)}, u32[]{:S(2)}, u32[]{:S(2)}) %collective-permute-start.11) | collective-permute-done | bytes 1048608 | tf_op jit(solution)/shard_map/ppermute | solution.py:45
  245.3 5.7 collective-permute-done.13
  252.7 23.5 %pair_forward.1 = (f32[1024,4096]{1,0:T(8,128)}, bf16[1024,2048]{1,0:T(8,128)(2,1)S(1)}) custom-call(bf16[1024,2048]{1,0:T(8,128)(2,1)} %constant_dynamic-update-slice_fusion.10.x_ref, bf16[2048,4096]{1,0:T(8,128)(2,1)} %all-gather.7.cloned.1.call-done.w_ref), custom_call_target="tpu_custom_call" | custom-call | flops 17179869184 | bytes 20971520 | tf_op jit(solution)/shard_map/pair_forward/pallas_call | solution.py:229
  278.2 53.7 %all-gather.9.cloned.1.call-done.w_ref = bf16[2048,2048]{1,0:T(8,128)(2,1)} async-done(((bf16[2048,256]{1,0:T(8,128)(2,1)}), bf16[2048,2048]{1,0:T(8,128)(2,1)}) %all-gather.9.cloned.1.call-update) | async-done | bytes 8388624 | tf_op jit(solution)/shard_map/all_gather | solution.py:313
  331.9 12.6 %fusion.113 = (bf16[1024,2048]{1,0:T(8,128)(2,1)S(1)}, f32[1024,2048]{1,0:T(8,128)S(1)}) fusion(bf16[1024,2048]{1,0:T(8,128)(2,1)} %copy-done.1, bf16[2048,2048]{1,0:T(8,128)(2,1)} %all-gather.9.cloned.1.call-done.w_ref), kind=kOutput, calls=%fused_computation.274 | convolution fusion | flops 8592031744 | bytes 25165824 | tf_op jit(solution)/shard_map/dot_general | solution.py:37
  347.8 11.1 %collective-permute-done.17 = bf16[128,2048]{1,0:T(8,128)(2,1)S(1)} collective-permute-done((bf16[128,2048]{1,0:T(8,128)(2,1)S(1)}, bf16[128,2048]{1,0:T(8,128)(2,1)S(1)}, u32[]{:S(2)}, u32[]{:S(2)}) %collective-permute-start.17) | collective-permute-done | bytes 524320 | tf_op jit(solution)/shard_map/ppermute | solution.py:45
  365.3 20.6 %collective-permute-done.18 = bf16[256,2048]{1,0:T(8,128)(2,1)} collective-permute-done((bf16[256,2048]{1,0:T(8,128)(2,1)}, bf16[256,2048]{1,0:T(8,128)(2,1)}, u32[]{:S(2)}, u32[]{:S(2)}) %collective-permute-start.18) | collective-permute-done | bytes 1048608 | tf_op jit(solution)/shard_map/ppermute | solution.py:45
  397.7 22.1 %collective-permute-done.19 = bf16[256,2048]{1,0:T(8,128)(2,1)S(1)} collective-permute-done((bf16[256,2048]{1,0:T(8,128)(2,1)}, bf16[256,2048]{1,0:T(8,128)(2,1)S(1)}, u32[]{:S(2)}, u32[]{:S(2)}) %collective-permute-start.19) | collective-permute-done | bytes 1048608 | tf_op jit(solution)/shard_map/ppermute | solution.py:45
  426.5 5.5 collective-permute-done.21
  438.3 5.9 convolution_convert_fusion.2
  444.2 3.9 fusion.98
  451.4 7.4 add_convert_fusion.1
  461.0 18.2 %pair_backward.1 = bf16[1024,4096]{1,0:T(8,128)(2,1)} custom-call(bf16[1024,2048]{1,0:T(8,128)(2,1)S(1)} %copy-done, bf16[2048,2048]{1,0:T(8,128)(2,1)} %all-gather.9.cloned.1.call-done.w_ref, f32[1024,4096]{1,0:T(8,128)} %get-tuple-element.29.p_ref), custom_call_target="tpu_custom_call" | custom-call | flops 8589934592 | bytes 29360128 | tf_op jit(solution)/shard_map/pair_backward/pallas_call | solution.py:203
  479.3 13.9 %convolution_convert_fusion = bf16[1024,4096]{1,0:T(8,128)(2,1)} fusion(bf16[1024,4096]{1,0:T(8,128)(2,1)} %pair_backward.1, pred[]{:T(512)S(6)} %eq.41, bf16[1024,256]{1,0:T(8,128)(2,1)S(1)} %get-tuple-element.105, bf16[1024,256]{1,0:T(8,128)(2,1)S(1)} %copy-done.59, bf16[1024,256]{1,0:T(8,128)(2,1)S(1)} %copy-done.60, ...), kind=kOutput, calls=%fused_computation.10 | convolution fusion | flops 8611954688 | bytes 20971520 | tf_op jit(solution)/shard_map/dot_general | solution.py:33
  493.3 20.3 %fusion.115 = f32[1024,2048]{1,0:T(8,128)S(1)} fusion(bf16[1024,4096]{1,0:T(8,128)(2,1)S(1)} %copy-done.28, bf16[2048,4096]{1,0:T(8,128)(2,1)} %all-gather.7.cloned.1.call-done.w_ref), kind=kOutput, calls=%fused_computation.276 | convolution fusion | flops 17179869184 | bytes 33554432 | tf_op jit(solution)/shard_map/dot_general | solution.py:41
  516.0 12.8 %collective-permute-done.26 = bf16[128,2048]{1,0:T(8,128)(2,1)S(1)} collective-permute-done((bf16[128,2048]{1,0:T(8,128)(2,1)S(1)}, bf16[128,2048]{1,0:T(8,128)(2,1)S(1)}, u32[]{:S(2)}, u32[]{:S(2)}) %collective-permute-start.26) | collective-permute-done | bytes 524320 | tf_op jit(solution)/shard_map/ppermute | solution.py:45
  537.6 16.6 %collective-permute-done.27 = bf16[256,2048]{1,0:T(8,128)(2,1)S(1)} collective-permute-done((bf16[256,2048]{1,0:T(8,128)(2,1)S(1)}, bf16[256,2048]{1,0:T(8,128)(2,1)S(1)}, u32[]{:S(2)}, u32[]{:S(2)}) %collective-permute-start.27) | collective-permute-done | bytes 1048608 | tf_op jit(solution)/shard_map/ppermute | solution.py:45
  556.5 18.2 %add_convert_fusion = bf16[1024,4096]{1,0:T(8,128)(2,1)} fusion(bf16[1024,4096]{1,0:T(8,128)(2,1)} %collective-permute-done.28, bf16[1024,4096]{1,0:T(8,128)(2,1)} %pair_backward.1, pred[]{:T(512)S(6)} %eq.41, bf16[1024,256]{1,0:T(8,128)(2,1)S(1)} %copy-done.58, bf16[1024,256]{1,0:T(8,128)(2,1)S(1)} %copy-done.59, bf16[1024,256]{1,0:T(8,128)(2,1)S(1)} %copy-done.60, ...), kind=kOutput, calls=%fused_computation.2 | convolution fusion | flops 8620343296 | bytes 29360128 | tf_op jit(solution)/shard_map/dot_general | solution.py:33
  574.7 5.6 multiply_reduce_fusion.3
  590.4 15.4 %collective-permute-done.29 = bf16[256,2048]{1,0:T(8,128)(2,1)S(1)} collective-permute-done((bf16[256,2048]{1,0:T(8,128)(2,1)}, bf16[256,2048]{1,0:T(8,128)(2,1)S(1)}, u32[]{:S(2)}, u32[]{:S(2)}) %collective-permute-start.29) | collective-permute-done | bytes 1048608 | tf_op jit(solution)/shard_map/ppermute | solution.py:45
  612.8 6.5 collective-permute-done.31
  620.9 5.6 convolution_convert_fusion.3.g_ref
  626.5 21.1 %attend_backward.1 = (f32[1024,512]{1,0:T(8,128)}, f32[1024,512]{1,0:T(8,128)}, bf16[1024,512]{1,0:T(8,128)(2,1)}) custom-call(bf16[1024,512]{1,0:T(8,128)(2,1)} %get-tuple-element.71.q_ref, bf16[1024,512]{1,0:T(8,128)(2,1)} %get-tuple-element.70.k_ref, bf16[1024,512]{1,0:T(8,128)(2,1)} %copy-done.31, bf16[1024,512]{1,0:T(8,128)(2,1)} %convolution_convert_fusion.3.g_ref, ...), custom_call_target="tpu_custom_call" | custom-call | flops 5368709120 | bytes 8388608 | tf_op jit(solution)/shard_map/attend_backward/pallas_call | solution.py:170
  647.6 4.2 multiply_reduce_fusion
  653.7 3.2 fusion.95
  662.5 5.2 convolution_convert_fusion.1
  681.2 6.2 add_convert_fusion.2
  691.5 10.7 %fusion.114 = (bf16[1024,2048]{1,0:T(8,128)(2,1)S(1)}, f32[1024,2048]{1,0:T(8,128)}) fusion(bf16[1024,1536]{1,0:T(8,128)(2,1)S(1)} %pad_maximum_fusion.1, bf16[2048,2048]{1,0:T(8,128)(2,1)} %all-gather.5.cloned.1.call-done), kind=kOutput, calls=%fused_computation.275 | convolution fusion | flops 6444548096 | bytes 22020096 | tf_op jit(solution)/shard_map/dot_general | solution.py:41
  709.2 8.1 collective-permute-done.50
  725.5 3.5 collective-permute-start.41
  732.6 3.4 collective-permute-done.40
  746.3 4.0 fusion.14
  750.4 16.2 %reduce-scatter.4.cloned.1.call-done = bf16[256,2048]{1,0:T(8,128)(2,1)} async-done(((bf16[1024,2048]{1,0:T(8,128)(2,1)}), bf16[256,2048]{1,0:T(8,128)(2,1)}) %reduce-scatter.4.cloned.1.call-update) | async-done | bytes 1048592 | tf_op jit(solution)/shard_map/reduce_scatter | solution.py:280
  770.2 143.8 %reduce-scatter.6.cloned.1.call-done = bf16[256,4096]{1,0:T(8,128)(2,1)} async-done(((bf16[1024,4096]{1,0:T(8,128)(2,1)}), bf16[256,4096]{1,0:T(8,128)(2,1)}) %reduce-scatter.6.cloned.1.call-update) | async-done | bytes 2097168 | tf_op jit(solution)/shard_map/reduce_scatter | solution.py:280
  914.0 6.6 reshape.412
  920.5 14.3 %slice_reduce_fusion = (f32[256,8,256]{2,1,0:T(8,128)S(1)}, f32[256,8,256]{2,1,0:T(8,128)S(1)}) fusion(f32[256,8,2,256]{3,2,1,0:T(2,128)} %reshape.412), kind=kLoop, calls=%fused_computation.33 | loop fusion | bytes 8388608 | tf_op jit(solution)/shard_map/slice | solution.py:465
  (469 shorter events, 228.9 us)
Async XLA Ops:
  7.2 91.2 %all-gather.5.cloned.1.call-start = ((), (), s32[]{:S(2)}) async-start(), calls=%async_computation.3 | async-start | bytes 9437184 | tf_op jit(solution)/shard_map/all_gather | solution.py:311
  13.0 239.7 %all-gather.7.cloned.1.call-start = ((), (), s32[]{:S(2)}) async-start(), calls=%async_computation.4 | async-start | bytes 18874368 | tf_op jit(solution)/shard_map/all_gather | solution.py:312
  29.5 302.4 %all-gather.9.cloned.1.call-start = ((), (), s32[]{:S(2)}) async-start(), calls=%async_computation.5 | async-start | bytes 9437184 | tf_op jit(solution)/shard_map/all_gather | solution.py:313
  29.5 26.2 %collective-permute-start = (bf16[256,2048]{1,0:T(8,128)(2,1)S(1)}, bf16[256,2048]{1,0:T(8,128)(2,1)S(1)}, u32[]{:S(2)}, u32[]{:S(2)}) collective-permute-start(bf16[256,2048]{1,0:T(8,128)(2,1)S(1)} %copy-done.18), channel_id=1, source_target_pairs={{0,1},{1,0},{2,3},{3,2},{4,5},{5,4},{6,7},{7,6},{8,9},{9,8},{10,11... | collective-permute-start | bytes 3145736 | tf_op jit(solution)/shard_map/ppermute | solution.py:45
  32.6 40.4 %collective-permute-start.1 = (bf16[256,2048]{1,0:T(8,128)(2,1)S(1)}, bf16[256,2048]{1,0:T(8,128)(2,1)}, u32[]{:S(2)}, u32[]{:S(2)}) collective-permute-start(bf16[256,2048]{1,0:T(8,128)(2,1)S(1)} %copy-done.18), channel_id=1, source_target_pairs={{0,2},{1,3},{2,0},{3,1},{4,6},{5,7},{6,4},{7,5},{8,10},{9,11},{10,... | collective-permute-start | bytes 3145736 | tf_op jit(solution)/shard_map/ppermute | solution.py:45
  34.1 702.5 %reduce-scatter.8.cloned.1.call-start = ((), (), s32[]{:S(2)}) async-start(), calls=%async_computation.8 | async-start | bytes 5242880 | tf_op jit(solution)/shard_map/reduce_scatter | solution.py:280
  56.6 22.4 %collective-permute-start.2 = (bf16[128,2048]{1,0:T(8,128)(2,1)}, bf16[128,2048]{1,0:T(8,128)(2,1)}, u32[]{:S(2)}, u32[]{:S(2)}) collective-permute-start(bf16[128,2048]{1,0:T(8,128)(2,1)} %slice.625), channel_id=1, source_target_pairs={{0,2},{1,3},{2,0},{3,1},{4,6},{5,7},{6,4},{7,5},{8,10},{9,11},{10,... | collective-permute-start | bytes 1572872 | tf_op jit(solution)/shard_map/ppermute | solution.py:45
  74.1 14.2 %collective-permute-start.3 = (bf16[128,2048]{1,0:T(8,128)(2,1)S(1)}, bf16[128,2048]{1,0:T(8,128)(2,1)S(1)}, u32[]{:S(2)}, u32[]{:S(2)}) collective-permute-start(bf16[128,2048]{1,0:T(8,128)(2,1)S(1)} %slice.626), channel_id=1, source_target_pairs={{0,1},{1,0},{2,3},{3,2},{4,5},{5,4},{6,7},{7,6},{8,9},{9,8},{10,11... | collective-permute-start | bytes 1572872 | tf_op jit(solution)/shard_map/ppermute | solution.py:45
  112.2 18.7 %collective-permute-start.5 = (f32[2,4,256]{2,1,0:T(4,128)S(1)}, f32[2,4,256]{2,1,0:T(4,128)S(1)}, u32[]{:S(2)}, u32[]{:S(2)}) collective-permute-start(f32[2,4,256]{2,1,0:T(4,128)S(1)} %constant_dynamic-update-slice_fusion.8), channel_id=1, source_target_pairs={{0,2},{1,3},{2,0},{3,1},{4,6},{5,7},{6,4},{7,5},{8,10},{9,11},{10,... | collective-permute-start | bytes 24584 | tf_op jit(solution)/shard_map/ppermute | solution.py:45
  116.5 14.5 %collective-permute-start.6 = (f32[2,4,256]{2,1,0:T(4,128)S(1)}, f32[2,4,256]{2,1,0:T(4,128)S(1)}, u32[]{:S(2)}, u32[]{:S(2)}) collective-permute-start(f32[2,4,256]{2,1,0:T(4,128)S(1)} %constant_dynamic-update-slice_fusion.8), channel_id=1, source_target_pairs={{0,3},{1,2},{2,1},{3,0},{4,7},{5,6},{6,5},{7,4},{8,11},{9,10},{10,... | collective-permute-start | bytes 24584 | tf_op jit(solution)/shard_map/ppermute | solution.py:45
  117.9 13.1 %collective-permute-start.4 = (f32[2,4,256]{2,1,0:T(4,128)S(1)}, f32[2,4,256]{2,1,0:T(4,128)S(1)}, u32[]{:S(2)}, u32[]{:S(2)}) collective-permute-start(f32[2,4,256]{2,1,0:T(4,128)S(1)} %constant_dynamic-update-slice_fusion.8), channel_id=1, source_target_pairs={{0,1},{1,0},{2,3},{3,2},{4,5},{5,4},{6,7},{7,6},{8,9},{9,8},{10,11... | collective-permute-start | bytes 24584 | tf_op jit(solution)/shard_map/ppermute | solution.py:45
  175.3 13.3 %collective-permute-start.9 = (bf16[128,2048]{1,0:T(8,128)(2,1)S(1)}, bf16[128,2048]{1,0:T(8,128)(2,1)S(1)}, u32[]{:S(2)}, u32[]{:S(2)}) collective-permute-start(bf16[128,2048]{1,0:T(8,128)(2,1)S(1)} %get-tuple-element.126), channel_id=1, source_target_pairs={{0,1},{1,0},{2,3},{3,2},{4,5},{5,4},{6,7},{7,6},{8,9},{9,8},{10,11... | collective-permute-start | bytes 1572872 | tf_op jit(solution)/shard_map/ppermute | solution.py:45
  176.8 13.0 %collective-permute-start.7 = (bf16[128,2048]{1,0:T(8,128)(2,1)S(1)}, bf16[128,2048]{1,0:T(8,128)(2,1)S(1)}, u32[]{:S(2)}, u32[]{:S(2)}) collective-permute-start(bf16[128,2048]{1,0:T(8,128)(2,1)S(1)} %get-tuple-element.127), channel_id=1, source_target_pairs={{0,2},{1,3},{2,0},{3,1},{4,6},{5,7},{6,4},{7,5},{8,10},{9,11},{10,... | collective-permute-start | bytes 1572872 | tf_op jit(solution)/shard_map/ppermute | solution.py:45
  190.2 23.5 %collective-permute-start.10 = (bf16[256,2048]{1,0:T(8,128)(2,1)S(1)}, bf16[256,2048]{1,0:T(8,128)(2,1)S(1)}, u32[]{:S(2)}, u32[]{:S(2)}) collective-permute-start(bf16[256,2048]{1,0:T(8,128)(2,1)S(1)} %pad_maximum_fusion.11), channel_id=1, source_target_pairs={{0,2},{1,3},{2,0},{3,1},{4,6},{5,7},{6,4},{7,5},{8,10},{9,11},{10,... | collective-permute-start | bytes 3145736 | tf_op jit(solution)/shard_map/ppermute | solution.py:45
  191.8 23.2 %collective-permute-start.8 = (bf16[256,2048]{1,0:T(8,128)(2,1)S(1)}, bf16[256,2048]{1,0:T(8,128)(2,1)S(1)}, u32[]{:S(2)}, u32[]{:S(2)}) collective-permute-start(bf16[256,2048]{1,0:T(8,128)(2,1)S(1)} %pad_maximum_fusion.10), channel_id=1, source_target_pairs={{0,1},{1,0},{2,3},{3,2},{4,5},{5,4},{6,7},{7,6},{8,9},{9,8},{10,11... | collective-permute-start | bytes 3145736 | tf_op jit(solution)/shard_map/ppermute | solution.py:45
  217.1 22.6 %collective-permute-start.11 = (bf16[256,2048]{1,0:T(8,128)(2,1)S(1)}, bf16[256,2048]{1,0:T(8,128)(2,1)S(1)}, u32[]{:S(2)}, u32[]{:S(2)}) collective-permute-start(bf16[256,2048]{1,0:T(8,128)(2,1)S(1)} %get-tuple-element.63), channel_id=1, source_target_pairs={{0,1},{1,0},{2,3},{3,2},{4,5},{5,4},{6,7},{7,6},{8,9},{9,8},{10,11... | collective-permute-start | bytes 3145736 | tf_op jit(solution)/shard_map/ppermute | solution.py:45
  217.6 23.1 %collective-permute-start.12 = (bf16[256,2048]{1,0:T(8,128)(2,1)S(1)}, bf16[256,2048]{1,0:T(8,128)(2,1)S(1)}, u32[]{:S(2)}, u32[]{:S(2)}) collective-permute-start(bf16[256,2048]{1,0:T(8,128)(2,1)S(1)} %get-tuple-element.63), channel_id=1, source_target_pairs={{0,2},{1,3},{2,0},{3,1},{4,6},{5,7},{6,4},{7,5},{8,10},{9,11},{10,... | collective-permute-start | bytes 3145736 | tf_op jit(solution)/shard_map/ppermute | solution.py:45
  239.7 11.3 %collective-permute-start.13 = (bf16[128,2048]{1,0:T(8,128)(2,1)S(1)}, bf16[128,2048]{1,0:T(8,128)(2,1)S(1)}, u32[]{:S(2)}, u32[]{:S(2)}) collective-permute-start(bf16[128,2048]{1,0:T(8,128)(2,1)S(1)} %slice.657), channel_id=1, source_target_pairs={{0,2},{1,3},{2,0},{3,1},{4,6},{5,7},{6,4},{7,5},{8,10},{9,11},{10,... | collective-permute-start | bytes 1572872 | tf_op jit(solution)/shard_map/ppermute | solution.py:45
  240.8 11.0 %collective-permute-start.14 = (bf16[128,2048]{1,0:T(8,128)(2,1)S(1)}, bf16[128,2048]{1,0:T(8,128)(2,1)S(1)}, u32[]{:S(2)}, u32[]{:S(2)}) collective-permute-start(bf16[128,2048]{1,0:T(8,128)(2,1)S(1)} %slice.658), channel_id=1, source_target_pairs={{0,1},{1,0},{2,3},{3,2},{4,5},{5,4},{6,7},{7,6},{8,9},{9,8},{10,11... | collective-permute-start | bytes 1572872 | tf_op jit(solution)/shard_map/ppermute | solution.py:45
  344.8 14.1 %collective-permute-start.17 = (bf16[128,2048]{1,0:T(8,128)(2,1)S(1)}, bf16[128,2048]{1,0:T(8,128)(2,1)S(1)}, u32[]{:S(2)}, u32[]{:S(2)}) collective-permute-start(bf16[128,2048]{1,0:T(8,128)(2,1)S(1)} %get-tuple-element.122), channel_id=1, source_target_pairs={{0,1},{1,0},{2,3},{3,2},{4,5},{5,4},{6,7},{7,6},{8,9},{9,8},{10,11... | collective-permute-start | bytes 1572872 | tf_op jit(solution)/shard_map/ppermute | solution.py:45
  346.3 13.8 %collective-permute-start.15 = (bf16[128,2048]{1,0:T(8,128)(2,1)S(1)}, bf16[128,2048]{1,0:T(8,128)(2,1)S(1)}, u32[]{:S(2)}, u32[]{:S(2)}) collective-permute-start(bf16[128,2048]{1,0:T(8,128)(2,1)S(1)} %get-tuple-element.123), channel_id=1, source_target_pairs={{0,2},{1,3},{2,0},{3,1},{4,6},{5,7},{6,4},{7,5},{8,10},{9,11},{10,... | collective-permute-start | bytes 1572872 | tf_op jit(solution)/shard_map/ppermute | solution.py:45
  361.4 24.5 %collective-permute-start.18 = (bf16[256,2048]{1,0:T(8,128)(2,1)}, bf16[256,2048]{1,0:T(8,128)(2,1)}, u32[]{:S(2)}, u32[]{:S(2)}) collective-permute-start(bf16[256,2048]{1,0:T(8,128)(2,1)} %pad_maximum_fusion.13), channel_id=1, source_target_pairs={{0,2},{1,3},{2,0},{3,1},{4,6},{5,7},{6,4},{7,5},{8,10},{9,11},{10,... | collective-permute-start | bytes 3145736 | tf_op jit(solution)/shard_map/ppermute | solution.py:45
  364.0 24.2 %collective-permute-start.16 = (bf16[256,2048]{1,0:T(8,128)(2,1)}, bf16[256,2048]{1,0:T(8,128)(2,1)}, u32[]{:S(2)}, u32[]{:S(2)}) collective-permute-start(bf16[256,2048]{1,0:T(8,128)(2,1)} %pad_maximum_fusion.12), channel_id=1, source_target_pairs={{0,1},{1,0},{2,3},{3,2},{4,5},{5,4},{6,7},{7,6},{8,9},{9,8},{10,11... | collective-permute-start | bytes 3145736 | tf_op jit(solution)/shard_map/ppermute | solution.py:45
  396.6 23.3 %collective-permute-start.19 = (bf16[256,2048]{1,0:T(8,128)(2,1)}, bf16[256,2048]{1,0:T(8,128)(2,1)S(1)}, u32[]{:S(2)}, u32[]{:S(2)}) collective-permute-start(bf16[256,2048]{1,0:T(8,128)(2,1)} %get-tuple-element.58), channel_id=1, source_target_pairs={{0,1},{1,0},{2,3},{3,2},{4,5},{5,4},{6,7},{7,6},{8,9},{9,8},{10,11... | collective-permute-start | bytes 3145736 | tf_op jit(solution)/shard_map/ppermute | solution.py:45
  397.2 24.1 %collective-permute-start.20 = (bf16[256,2048]{1,0:T(8,128)(2,1)}, bf16[256,2048]{1,0:T(8,128)(2,1)}, u32[]{:S(2)}, u32[]{:S(2)}) collective-permute-start(bf16[256,2048]{1,0:T(8,128)(2,1)} %get-tuple-element.58), channel_id=1, source_target_pairs={{0,2},{1,3},{2,0},{3,1},{4,6},{5,7},{6,4},{7,5},{8,10},{9,11},{10,... | collective-permute-start | bytes 3145736 | tf_op jit(solution)/shard_map/ppermute | solution.py:45
  420.7 11.4 %collective-permute-start.21 = (bf16[128,2048]{1,0:T(8,128)(2,1)}, bf16[128,2048]{1,0:T(8,128)(2,1)}, u32[]{:S(2)}, u32[]{:S(2)}) collective-permute-start(bf16[128,2048]{1,0:T(8,128)(2,1)} %slice.668), channel_id=1, source_target_pairs={{0,2},{1,3},{2,0},{3,1},{4,6},{5,7},{6,4},{7,5},{8,10},{9,11},{10,... | collective-permute-start | bytes 1572872 | tf_op jit(solution)/shard_map/ppermute | solution.py:45
  422.3 11.6 %collective-permute-start.22 = (bf16[128,2048]{1,0:T(8,128)(2,1)S(1)}, bf16[128,2048]{1,0:T(8,128)(2,1)S(1)}, u32[]{:S(2)}, u32[]{:S(2)}) collective-permute-start(bf16[128,2048]{1,0:T(8,128)(2,1)S(1)} %slice.669), channel_id=1, source_target_pairs={{0,1},{1,0},{2,3},{3,2},{4,5},{5,4},{6,7},{7,6},{8,9},{9,8},{10,11... | collective-permute-start | bytes 1572872 | tf_op jit(solution)/shard_map/ppermute | solution.py:45
  444.2 7.2 collective-permute-start.23
  493.2 63.2 %collective-permute-start.28 = (bf16[1024,4096]{1,0:T(8,128)(2,1)}, bf16[1024,4096]{1,0:T(8,128)(2,1)}, u32[]{:S(2)}, u32[]{:S(2)}) collective-permute-start(bf16[1024,4096]{1,0:T(8,128)(2,1)} %convolution_convert_fusion), channel_id=1, source_target_pairs={{0,4},{4,0},{8,12},{12,8},{16,20},{20,16},{24,28},{28,24},{1,5},{5... | collective-permute-start | bytes 25165832 | tf_op jit(solution)/shard_map/ppermute | solution.py:261
  514.5 14.3 %collective-permute-start.26 = (bf16[128,2048]{1,0:T(8,128)(2,1)S(1)}, bf16[128,2048]{1,0:T(8,128)(2,1)S(1)}, u32[]{:S(2)}, u32[]{:S(2)}) collective-permute-start(bf16[128,2048]{1,0:T(8,128)(2,1)S(1)} %get-tuple-element.102), channel_id=1, source_target_pairs={{0,1},{1,0},{2,3},{3,2},{4,5},{5,4},{6,7},{7,6},{8,9},{9,8},{10,11... | collective-permute-start | bytes 1572872 | tf_op jit(solution)/shard_map/ppermute | solution.py:45
  515.5 13.9 %collective-permute-start.24 = (bf16[128,2048]{1,0:T(8,128)(2,1)S(1)}, bf16[128,2048]{1,0:T(8,128)(2,1)S(1)}, u32[]{:S(2)}, u32[]{:S(2)}) collective-permute-start(bf16[128,2048]{1,0:T(8,128)(2,1)S(1)} %get-tuple-element.103), channel_id=1, source_target_pairs={{0,2},{1,3},{2,0},{3,1},{4,6},{5,7},{6,4},{7,5},{8,10},{9,11},{10,... | collective-permute-start | bytes 1572872 | tf_op jit(solution)/shard_map/ppermute | solution.py:45
  529.8 24.4 %collective-permute-start.27 = (bf16[256,2048]{1,0:T(8,128)(2,1)S(1)}, bf16[256,2048]{1,0:T(8,128)(2,1)S(1)}, u32[]{:S(2)}, u32[]{:S(2)}) collective-permute-start(bf16[256,2048]{1,0:T(8,128)(2,1)S(1)} %pad_maximum_fusion.15), channel_id=1, source_target_pairs={{0,2},{1,3},{2,0},{3,1},{4,6},{5,7},{6,4},{7,5},{8,10},{9,11},{10,... | collective-permute-start | bytes 3145736 | tf_op jit(solution)/shard_map/ppermute | solution.py:45
  530.6 24.1 %collective-permute-start.25 = (bf16[256,2048]{1,0:T(8,128)(2,1)S(1)}, bf16[256,2048]{1,0:T(8,128)(2,1)S(1)}, u32[]{:S(2)}, u32[]{:S(2)}) collective-permute-start(bf16[256,2048]{1,0:T(8,128)(2,1)S(1)} %pad_maximum_fusion.14), channel_id=1, source_target_pairs={{0,1},{1,0},{2,3},{3,2},{4,5},{5,4},{6,7},{7,6},{8,9},{9,8},{10,11... | collective-permute-start | bytes 3145736 | tf_op jit(solution)/shard_map/ppermute | solution.py:45
  582.4 23.4 %collective-permute-start.29 = (bf16[256,2048]{1,0:T(8,128)(2,1)}, bf16[256,2048]{1,0:T(8,128)(2,1)S(1)}, u32[]{:S(2)}, u32[]{:S(2)}) collective-permute-start(bf16[256,2048]{1,0:T(8,128)(2,1)} %get-tuple-element.55), channel_id=1, source_target_pairs={{0,1},{1,0},{2,3},{3,2},{4,5},{5,4},{6,7},{7,6},{8,9},{9,8},{10,11... | collective-permute-start | bytes 3145736 | tf_op jit(solution)/shard_map/ppermute | solution.py:45
  584.9 25.3 %collective-permute-start.30 = (bf16[256,2048]{1,0:T(8,128)(2,1)}, bf16[256,2048]{1,0:T(8,128)(2,1)S(1)}, u32[]{:S(2)}, u32[]{:S(2)}) collective-permute-start(bf16[256,2048]{1,0:T(8,128)(2,1)} %get-tuple-element.55), channel_id=1, source_target_pairs={{0,2},{1,3},{2,0},{3,1},{4,6},{5,7},{6,4},{7,5},{8,10},{9,11},{10,... | collective-permute-start | bytes 3145736 | tf_op jit(solution)/shard_map/ppermute | solution.py:45
  605.9 13.4 %collective-permute-start.31 = (bf16[128,2048]{1,0:T(8,128)(2,1)S(1)}, bf16[128,2048]{1,0:T(8,128)(2,1)S(1)}, u32[]{:S(2)}, u32[]{:S(2)}) collective-permute-start(bf16[128,2048]{1,0:T(8,128)(2,1)S(1)} %slice.690), channel_id=1, source_target_pairs={{0,2},{1,3},{2,0},{3,1},{4,6},{5,7},{6,4},{7,5},{8,10},{9,11},{10,... | collective-permute-start | bytes 1572872 | tf_op jit(solution)/shard_map/ppermute | solution.py:45
  608.0 158.6 %reduce-scatter.4.cloned.1.call-start = ((), (), s32[]{:S(2)}) async-start(), calls=%async_computation.6 | async-start | bytes 5242880 | tf_op jit(solution)/shard_map/reduce_scatter | solution.py:280
  610.2 9.9 %collective-permute-start.32 = (bf16[128,2048]{1,0:T(8,128)(2,1)S(1)}, bf16[128,2048]{1,0:T(8,128)(2,1)S(1)}, u32[]{:S(2)}, u32[]{:S(2)}) collective-permute-start(bf16[128,2048]{1,0:T(8,128)(2,1)S(1)} %slice.691), channel_id=1, source_target_pairs={{0,1},{1,0},{2,3},{3,2},{4,5},{5,4},{6,7},{7,6},{8,9},{9,8},{10,11... | collective-permute-start | bytes 1572872 | tf_op jit(solution)/shard_map/ppermute | solution.py:45
  667.7 12.8 %collective-permute-start.46 = (bf16[1024,1536]{1,0:T(8,128)(2,1)}, bf16[1024,1536]{1,0:T(8,128)(2,1)}, u32[]{:S(2)}, u32[]{:S(2)}) collective-permute-start(bf16[1024,1536]{1,0:T(8,128)(2,1)} %convolution_convert_fusion.1), channel_id=1, source_target_pairs={{0,4},{4,0},{8,12},{12,8},{16,20},{20,16},{24,28},{28,24},{1,5},{5... | collective-permute-start | bytes 9437192 | tf_op jit(solution)/shard_map/ppermute | solution.py:261
  690.0 223.9 %reduce-scatter.6.cloned.1.call-start = ((), (), s32[]{:S(2)}) async-start(), calls=%async_computation.7 | async-start | bytes 10485760 | tf_op jit(solution)/shard_map/reduce_scatter | solution.py:280
  702.3 14.9 %collective-permute-start.50 = (bf16[128,2048]{1,0:T(8,128)(2,1)S(1)}, bf16[128,2048]{1,0:T(8,128)(2,1)S(1)}, u32[]{:S(2)}, u32[]{:S(2)}) collective-permute-start(bf16[128,2048]{1,0:T(8,128)(2,1)S(1)} %get-tuple-element.82), channel_id=1, source_target_pairs={{0,1},{1,0},{2,3},{3,2},{4,5},{5,4},{6,7},{7,6},{8,9},{9,8},{10,11... | collective-permute-start | bytes 1572872 | tf_op jit(solution)/shard_map/ppermute | solution.py:45
  703.7 15.7 %collective-permute-start.48 = (bf16[128,2048]{1,0:T(8,128)(2,1)S(1)}, bf16[128,2048]{1,0:T(8,128)(2,1)S(1)}, u32[]{:S(2)}, u32[]{:S(2)}) collective-permute-start(bf16[128,2048]{1,0:T(8,128)(2,1)S(1)} %get-tuple-element.83), channel_id=1, source_target_pairs={{0,2},{1,3},{2,0},{3,1},{4,6},{5,7},{6,4},{7,5},{8,10},{9,11},{10,... | collective-permute-start | bytes 1572872 | tf_op jit(solution)/shard_map/ppermute | solution.py:45
  705.6 19.3 %collective-permute-start.35 = (f32[8,2048]{1,0:T(8,128)S(1)}, f32[8,2048]{1,0:T(8,128)S(1)}, u32[]{:S(2)}, u32[]{:S(2)}) collective-permute-start(f32[8,2048]{1,0:T(8,128)S(1)} %concatenate.141), channel_id=1, source_target_pairs={{0,3},{1,2},{2,1},{3,0},{4,7},{5,6},{6,5},{7,4},{8,11},{9,10},{10,... | collective-permute-start | bytes 196616 | tf_op jit(solution)/shard_map/ppermute | solution.py:45
  706.8 18.1 %collective-permute-start.34 = (f32[8,2048]{1,0:T(8,128)S(1)}, f32[8,2048]{1,0:T(8,128)S(1)}, u32[]{:S(2)}, u32[]{:S(2)}) collective-permute-start(f32[8,2048]{1,0:T(8,128)S(1)} %concatenate.141), channel_id=1, source_target_pairs={{0,2},{1,3},{2,0},{3,1},{4,6},{5,7},{6,4},{7,5},{8,10},{9,11},{10,... | collective-permute-start | bytes 196616 | tf_op jit(solution)/shard_map/ppermute | solution.py:45
  708.4 16.5 %collective-permute-start.33 = (f32[8,2048]{1,0:T(8,128)S(1)}, f32[8,2048]{1,0:T(8,128)S(1)}, u32[]{:S(2)}, u32[]{:S(2)}) collective-permute-start(f32[8,2048]{1,0:T(8,128)S(1)} %concatenate.141), channel_id=1, source_target_pairs={{0,1},{1,0},{2,3},{3,2},{4,5},{5,4},{6,7},{7,6},{8,9},{9,8},{10,11... | collective-permute-start | bytes 196616 | tf_op jit(solution)/shard_map/ppermute | solution.py:45
  721.4 22.8 %collective-permute-start.51 = (bf16[256,2048]{1,0:T(8,128)(2,1)S(1)}, bf16[256,2048]{1,0:T(8,128)(2,1)}, u32[]{:S(2)}, u32[]{:S(2)}) collective-permute-start(bf16[256,2048]{1,0:T(8,128)(2,1)S(1)} %pad_maximum_fusion.17), channel_id=1, source_target_pairs={{0,2},{1,3},{2,0},{3,1},{4,6},{5,7},{6,4},{7,5},{8,10},{9,11},{10,... | collective-permute-start | bytes 3145736 | tf_op jit(solution)/shard_map/ppermute | solution.py:45
  723.7 22.6 %collective-permute-start.49 = (bf16[256,2048]{1,0:T(8,128)(2,1)}, bf16[256,2048]{1,0:T(8,128)(2,1)}, u32[]{:S(2)}, u32[]{:S(2)}) collective-permute-start(bf16[256,2048]{1,0:T(8,128)(2,1)} %pad_maximum_fusion.16), channel_id=1, source_target_pairs={{0,1},{1,0},{2,3},{3,2},{4,5},{5,4},{6,7},{7,6},{8,9},{9,8},{10,11... | collective-permute-start | bytes 3145736 | tf_op jit(solution)/shard_map/ppermute | solution.py:45
  730.3 9.1 collective-permute-start.39
  (105 other events, 843.1 us)
Sparse Core Ops, SparseCore 0:
  13.1 85.1 all-gather.4
  100.0 149.5 all-gather.6
  251.2 80.6 all-gather.8
  608.1 75.0 reduce-scatter.7
  690.2 76.3 reduce-scatter.3
  768.8 145.1 reduce-scatter.5

commit v2 on v1

--- a/solution.py
+++ b/solution.py
@@ -51,13 +51,31 @@
         self.me = lax.axis_index("tensor")
         self.order = self.me ^ jnp.arange(size)
 
-    def gather(self, own):
+    def gather_parts(self, own):
         half = own.shape[0] // 2
         across = hop(own, 1)
         along = hop(own, 2)
         first = hop(across[:half], 2)
         second = hop(along[half:], 1)
-        return jnp.concatenate([own, across, along, first, second], axis=0)
+        return own, across, along, first, second
+
+    def gather(self, own):
+        return jnp.concatenate(self.gather_parts(own), axis=0)
+
+    def scatter_product(self, left, right):
+        rows = left.shape[0] // 4
+        half = rows // 2
+        far = times(left[3 * rows :], right).astype(BF)
+        first = hop(far[:half], 1)
+        second = hop(far[half:], 2)
+        near = lax.optimization_barrier(times(left[rows : 3 * rows], right))
+        across, along = near[:rows], near[rows:]
+        along = jnp.concatenate([along[:half] + first.astype(F32), along[half:]], axis=0).astype(BF)
+        across = jnp.concatenate([across[:half], across[half:] + second.astype(F32)], axis=0).astype(BF)
+        across = hop(across, 1)
+        along = hop(along, 2)
+        own = times(left[:rows], right)
+        return own, across, along
 
     def scatter(self, parts):
         rows = parts.shape[0] // 4
@@ -93,6 +111,9 @@
     def gather(self, own):
         return lax.all_gather(own, "tensor", axis=0, tiled=True)
 
+    def scatter_product(self, left, right):
+        return (self.scatter(times(left, right)),)
+
     def scatter(self, parts):
         return lax.psum_scatter(
             parts.astype(BF), "tensor", scatter_dimension=0, tiled=True
@@ -214,6 +235,52 @@
         compiler_params=pltpu.CompilerParams(vmem_limit_bytes=48 << 20),
         name="pair_backward",
     )(piece, down, pair)
+
+
+def loss_and_back(parts, resid, teacher, valid, gain, block=64):
+    rows, width = resid.shape
+    count = len(parts)
+
+    def body(*refs):
+        x_ref, t_ref, v_ref, w_ref, o_ref, g_ref, b_ref, sum_ref = refs[count:]
+        branch = refs[0][...]
+        for ref in refs[1:count]:
+            branch = branch + ref[...].astype(F32)
+        scale = lax.rsqrt(jnp.mean(branch * branch, axis=1, keepdims=True) + EPS)
+        normed = branch * scale
+        out = x_ref[...] + normed * w_ref[...]
+        o_ref[...] = out.astype(BF)
+        error = out - t_ref[...].astype(F32)
+        grad = error * v_ref[:, 1:2]
+        g_ref[...] = grad
+        back = grad * w_ref[...]
+        inner = jnp.mean(back * normed, axis=1, keepdims=True)
+        b_ref[...] = (scale * (back - normed * inner)).astype(BF)
+
+        @pl.when(pl.program_id(0) == 0)
+        def _():
+            sum_ref[...] = jnp.zeros_like(sum_ref)
+
+        sum_ref[0:1, :] += jnp.sum(grad * normed, axis=0, keepdims=True)
+        sum_ref[1:2, :] += jnp.sum(error * error * v_ref[:, 0:1], axis=0, keepdims=True)
+
+    row = pl.BlockSpec((block, width), lambda i: (i, 0))
+    arrays = (*parts, resid, teacher)
+    return pl.pallas_call(
+        body,
+        grid=(rows // block,),
+        in_specs=[row] * len(arrays)
+        + [pl.BlockSpec((block, 2), lambda i: (i, 0)), pl.BlockSpec((1, width), lambda i: (0, 0))],
+        out_specs=[row, row, row, pl.BlockSpec((8, width), lambda i: (0, 0))],
+        out_shape=[
+            jax.ShapeDtypeStruct((rows, width), BF),
+            jax.ShapeDtypeStruct((rows, width), F32),
+            jax.ShapeDtypeStruct((rows, width), BF),
+            jax.ShapeDtypeStruct((8, width), F32),
+        ],
+        cost_estimate=cost(30 * rows * width, *arrays),
+        name="loss_and_back",
+    )(*arrays, valid, gain.reshape(1, width))
 
 
 def pair_forward(rows, weights, block=BLOCK):
@@ -371,24 +438,31 @@
     whole_h = ring.gather(resid.astype(BF))
 
     pair, hidden = pair_forward(whole_h, pair_all)
-    branch_ffn = ring.scatter(times(hidden, full_down))
-    scale_ffn = lax.rsqrt(jnp.mean(branch_ffn * branch_ffn, axis=1, keepdims=True) + EPS)
-    normed_ffn = branch_ffn * scale_ffn
-    output = resid + normed_ffn * gain_ffn
     my_segment = lax.dynamic_slice_in_dim(segment, ring.me * rows, rows)
-    valid = (my_segment != 0).astype(F32)[:, None]
-    error = output - teacher.astype(F32)
-    loss_part = jnp.sum(valid * error * error)
-    tokens_all = rows * dp * tensor
-    grad_output = 2.0 * tokens_all * valid * error / valid_total
-    grad_gain_ffn = jnp.sum(grad_output * normed_ffn, axis=0)
-    grad_normed = grad_output * gain_ffn
-    grad_branch_ffn = (
-        scale_ffn
-        * (grad_normed - normed_ffn * jnp.mean(grad_normed * normed_ffn, axis=1, keepdims=True))
-    ).astype(BF)
-    piece = ring.gather(grad_branch_ffn)
-    grad_down = pair_sum(lambda side: inner_rows(hidden, side), pick_halves(piece, 1))
+    valid = (my_segment != 0).astype(F32)
+    valid = jnp.stack([valid, valid * (2.0 * (rows * dp * tensor) / valid_total)], axis=1)
+    parts = ring.scatter_product(hidden, full_down)
+    output, grad_output, grad_branch_ffn, sums = loss_and_back(
+        parts, resid, teacher, valid, gain_ffn
+    )
+    grad_gain_ffn = sums[0]
+    loss_part = jnp.sum(sums[1])
+    if tensor == 4:
+        got_rows = ring.gather_parts(grad_branch_ffn)
+        cut = 3 * rows
+        near_halves = pick_halves(jnp.concatenate(got_rows[:3], axis=0), 1)
+        far_halves = pick_halves(jnp.concatenate(got_rows[3:], axis=0), 1)
+        near = lax.optimization_barrier(
+            tuple(inner_rows(hidden[:cut], half) for half in near_halves)
+        )
+        theirs = (near[0] + inner_rows(hidden[cut:], far_halves[0])).astype(BF)
+        got = swap_cores(theirs)
+        grad_down = near[1] + inner_rows(hidden[cut:], far_halves[1])
+        grad_down = (grad_down + got.astype(F32)).astype(BF)
+        piece = jnp.concatenate(got_rows, axis=0)
+    else:
+        piece = ring.gather(grad_branch_ffn)
+        grad_down = pair_sum(lambda side: inner_rows(hidden, side), pick_halves(piece, 1))
     sum_down = scatter_pairs(grad_down, 1)
     piece, grad_down = lax.optimization_barrier((piece, grad_down))
     grad_pair = pair_backward(piece, full_down, pair)
@@ -454,7 +528,7 @@
     sum_out = sum_out.transpose(1, 0, 2).reshape(local_width, share)
     sum_pair = sum_pair.astype(F32).reshape(share, units // BLOCK, 2, BLOCK)
     return (
-        output.astype(BF),
+        output,
         loss,
         grad_input,
         sum_attn[:, :local_width],

time: 957 us -> 936 us (0.978)
  waiting for transfers between devices: 451 us -> 424 us
  other arithmetic: 73.6 us -> 61.3 us
    ppermute x41, waiting for transfers between devices: 214 us -> 192 us  [hop(): return lax.ppermute(value, 'tensor', [(i, i ^ way) for i in range(size)])]
    dot_general x3 -> x5, matrix products: 25 us -> 30.5 us  [times(): return jnp.dot(left, right, preferred_element_type=F32)]
    unnamed x235 -> x270, local copies, waits for them, and re-layouts: 60.9 us -> 62.9 us
    dot_general x8 -> x10, matrix products: 62.8 us -> 64.6 us  [inner_rows(): lax.dot_general(left, right, (((0,), (0,)), ((), ())), preferred_element_...]
  transfers between devices with their start and end apart: 58 -> 58, of which waited for: 36 -> 34; matrix products, arithmetic and copies ran while one was open for 23% -> 25% of each run, Pallas kernels for 5% -> 5%
where the time goes in v2:
time: 936 us; the launch traced here: 928 us
  waiting for transfers between devices  424 us (45%)
  matrix products  153 us (16%)
  local copies, waits for them, and re-layouts  127 us (14%)
  Pallas kernels  70.6 us (8%)
  other arithmetic  61.3 us (7%)
  starting transfers between devices  58.2 us (6%)
  between operations  19.7 us (2%)
  blocking collectives  14.7 us (2%)
    ppermute x41, waiting for transfers between devices, hop(): return lax.ppermute(value, 'tensor', [(i, i ^ way) for i in range(size)])  192 us
    reduce_scatter x3, waiting for transfers between devices, scatter_pairs(): lax.psum_scatter(value, 'dp', scatter_dimension=axis, axis_index_groups=g...  159 us
    dot_general x10, matrix products, inner_rows(): lax.dot_general(left, right, (((0,), (0,)), ((), ())), preferred_element_...  64.6 us
    unnamed x270, local copies, waits for them, and re-layouts  62.9 us
    ppermute x41, starting transfers between devices, hop(): return lax.ppermute(value, 'tensor', [(i, i ^ way) for i in range(size)])  51.4 us
    all_gather x1, waiting for transfers between devices, layer(): full_down = lax.all_gather(wd, 'dp', axis=1, tiled=True)  49.5 us
    dot_general x3, matrix products, times_transposed(): lax.dot_general(left, right, (((1,), (1,)), ((), ())), preferred_element_...  36.7 us
    dot_general x5, matrix products, times(): return jnp.dot(left, right, preferred_element_type=F32)  30.5 us
  transfers between devices with their start and end apart: 58, of which 34 were waited for; matrix products, arithmetic and copies ran while one was open for 25% of the time, Pallas kernels for 5%

profile of v2, /device:TPU:0, one launch (start us, length us, event | category | flops | bytes accessed | tf_op | source)
XLA Modules:
  0.0 928.1 jit_solution(12639843673832113358)
XLA Ops:
  43.1 12.6 %collective-permute-done = bf16[256,2048]{1,0:T(8,128)(2,1)S(1)} collective-permute-done((bf16[256,2048]{1,0:T(8,128)(2,1)S(1)}, bf16[256,2048]{1,0:T(8,128)(2,1)S(1)}, u32[]{:S(2)}, u32[]{:S(2)}) %collective-permute-start) | collective-permute-done | bytes 1048608 | tf_op jit(solution)/shard_map/ppermute | solution.py:45
  58.3 14.7 %all-gather = f32[8,2048]{1,0:T(8,128)S(1)} all-gather(f32[8,256]{1,0:T(8,128)S(1)} %concatenate.132), channel_id=2, replica_groups=mesh['dp'=8,'tensor'=4] {'dp'}, dimensions={1}, use_global_device_ids=true | all-gather | bytes 73728 | tf_op jit(solution)/shard_map/all_gather | solution.py:389
  80.9 7.4 collective-permute-done.3
  89.2 9.2 all-gather.5.cloned.1.call-done
  98.4 10.0 %fusion.5 = f32[1024,1536]{1,0:T(8,128)S(1)} fusion(bf16[1024,2048]{1,0:T(8,128)(2,1)} %constant_dynamic-update-slice_fusion, bf16[2048,2048]{1,0:T(8,128)(2,1)} %all-gather.5.cloned.1.call-done), kind=kOutput, calls=%fused_computation.15 | convolution fusion | flops 6442450944 | bytes 16777216 | tf_op jit(solution)/shard_map/dot_general | solution.py:37
  124.6 4.3 reshape.386
  140.1 14.6 %fusion = (f32[4,1024]{1,0:T(4,128)S(1)}, f32[4,1024,1024]{1,2,0:T(8,128)}) fusion(pred[1024,1024]{0,1:T(8,128)(4,1)} %copy.60, f32[1024,128]{1,0:T(8,128)} %get-tuple-element.164.c_ref.cq_ref, f32[1024,128]{1,0:T(8,128)} %get-tuple-element.163, f32[1024,4,64]{2,0,1:T(8,128)S(1)} %get-tuple-element.134, f32[1024,4,64]{2,0,1:T(8,128)S(1)} %get-tuple-element.133, ...), kind=kOutput, calls=%fused_computation.6 | convolution fusion | flops 1091563520 | bytes 27279360 | tf_op jit(solution)/shard_map/qhd,khd->hqk/dot_general | solution.py:130
  154.8 8.7 fusion.1
  166.4 7.0 fusion.45
  179.0 10.2 %collective-permute-done.7 = bf16[128,2048]{1,0:T(8,128)(2,1)S(1)} collective-permute-done((bf16[128,2048]{1,0:T(8,128)(2,1)S(1)}, bf16[128,2048]{1,0:T(8,128)(2,1)S(1)}, u32[]{:S(2)}, u32[]{:S(2)}) %collective-permute-start.7) | collective-permute-done | bytes 524320 | tf_op jit(solution)/shard_map/ppermute | solution.py:45
  193.8 20.7 %collective-permute-done.10 = bf16[256,2048]{1,0:T(8,128)(2,1)S(1)} collective-permute-done((bf16[256,2048]{1,0:T(8,128)(2,1)S(1)}, bf16[256,2048]{1,0:T(8,128)(2,1)S(1)}, u32[]{:S(2)}, u32[]{:S(2)}) %collective-permute-start.10) | collective-permute-done | bytes 1048608 | tf_op jit(solution)/shard_map/ppermute | solution.py:45
  220.9 19.6 %collective-permute-done.11 = bf16[256,2048]{1,0:T(8,128)(2,1)S(1)} collective-permute-done((bf16[256,2048]{1,0:T(8,128)(2,1)S(1)}, bf16[256,2048]{1,0:T(8,128)(2,1)S(1)}, u32[]{:S(2)}, u32[]{:S(2)}) %collective-permute-start.11) | collective-permute-done | bytes 1048608 | tf_op jit(solution)/shard_map/ppermute | solution.py:45
  247.7 5.3 collective-permute-done.13
  255.7 24.7 %pair_forward.1 = (f32[1024,4096]{1,0:T(8,128)}, bf16[1024,2048]{1,0:T(8,128)(2,1)S(1)}) custom-call(bf16[1024,2048]{1,0:T(8,128)(2,1)} %constant_dynamic-update-slice_fusion.10.x_ref, bf16[2048,4096]{1,0:T(8,128)(2,1)} %all-gather.7.cloned.1.call-done.w_ref), custom_call_target="tpu_custom_call" | custom-call | flops 17179869184 | bytes 20971520 | tf_op jit(solution)/shard_map/pair_forward/pallas_call | solution.py:296
  282.4 49.5 %all-gather.9.cloned.1.call-done.w_ref = bf16[2048,2048]{1,0:T(8,128)(2,1)} async-done(((bf16[2048,256]{1,0:T(8,128)(2,1)}), bf16[2048,2048]{1,0:T(8,128)(2,1)}) %all-gather.9.cloned.1.call-update) | async-done | bytes 8388624 | tf_op jit(solution)/shard_map/all_gather | solution.py:380
  331.9 6.2 convolution_convert_fusion.2
  341.2 4.5 fusion.33
  346.1 6.2 collective-permute-done.17
  357.1 7.4 fusion.58.refs_0_
  364.5 13.6 %collective-permute-done.16.refs_1_ = bf16[256,2048]{1,0:T(8,128)(2,1)S(1)} collective-permute-done((bf16[256,2048]{1,0:T(8,128)(2,1)S(1)}, bf16[256,2048]{1,0:T(8,128)(2,1)S(1)}, u32[]{:S(2)}, u32[]{:S(2)}) %collective-permute-start.16) | collective-permute-done | bytes 1048608 | tf_op jit(solution)/shard_map/ppermute | solution.py:45
  379.2 6.6 loss_and_back.1
  389.7 19.8 %collective-permute-done.19 = bf16[256,2048]{1,0:T(8,128)(2,1)S(1)} collective-permute-done((bf16[256,2048]{1,0:T(8,128)(2,1)}, bf16[256,2048]{1,0:T(8,128)(2,1)S(1)}, u32[]{:S(2)}, u32[]{:S(2)}) %collective-permute-start.19) | collective-permute-done | bytes 1048608 | tf_op jit(solution)/shard_map/ppermute | solution.py:45
  415.2 3.5 fusion.10
  418.7 3.5 fusion.8
  429.0 4.2 collective-permute-done.23
  433.2 3.5 add_convert_fusion.1
  439.0 18.3 %pair_backward.1 = bf16[1024,4096]{1,0:T(8,128)(2,1)} custom-call(bf16[1024,2048]{1,0:T(8,128)(2,1)S(1)} %copy-done.1, bf16[2048,2048]{1,0:T(8,128)(2,1)} %all-gather.9.cloned.1.call-done.w_ref, f32[1024,4096]{1,0:T(8,128)} %get-tuple-element.40.p_ref), custom_call_target="tpu_custom_call" | custom-call | flops 8589934592 | bytes 29360128 | tf_op jit(solution)/shard_map/pair_backward/pallas_call | solution.py:224
  457.4 16.7 %convolution_convert_fusion = bf16[1024,4096]{1,0:T(8,128)(2,1)} fusion(bf16[1024,4096]{1,0:T(8,128)(2,1)} %pair_backward.1, pred[]{:T(512)S(6)} %eq.43, bf16[1024,256]{1,0:T(8,128)(2,1)S(1)} %copy-done.68, bf16[1024,256]{1,0:T(8,128)(2,1)S(1)} %copy-done.69, bf16[1024,256]{1,0:T(8,128)(2,1)S(1)} %copy-done.70, bf16[1024,256]{1,0:T(8,128)(2,1)S(1)} %copy-done.71, ...), kind=kOutput, calls=%fused_computation.11 | convolution fusion | flops 8611954688 | bytes 20971520 | tf_op jit(solution)/shard_map/dot_general | solution.py:33
  474.2 20.3 %fusion.126 = f32[1024,2048]{1,0:T(8,128)S(1)} fusion(bf16[1024,4096]{1,0:T(8,128)(2,1)S(1)} %copy-done.28, bf16[2048,4096]{1,0:T(8,128)(2,1)} %all-gather.7.cloned.1.call-done.w_ref), kind=kOutput, calls=%fused_computation.288 | convolution fusion | flops 17179869184 | bytes 33554432 | tf_op jit(solution)/shard_map/dot_general | solution.py:41
  497.1 12.6 %collective-permute-done.24 = bf16[128,2048]{1,0:T(8,128)(2,1)S(1)} collective-permute-done((bf16[128,2048]{1,0:T(8,128)(2,1)S(1)}, bf16[128,2048]{1,0:T(8,128)(2,1)S(1)}, u32[]{:S(2)}, u32[]{:S(2)}) %collective-permute-start.24) | collective-permute-done | bytes 524320 | tf_op jit(solution)/shard_map/ppermute | solution.py:45
  517.6 18.0 %collective-permute-done.27 = bf16[256,2048]{1,0:T(8,128)(2,1)S(1)} collective-permute-done((bf16[256,2048]{1,0:T(8,128)(2,1)S(1)}, bf16[256,2048]{1,0:T(8,128)(2,1)S(1)}, u32[]{:S(2)}, u32[]{:S(2)}) %collective-permute-start.27) | collective-permute-done | bytes 1048608 | tf_op jit(solution)/shard_map/ppermute | solution.py:45
  537.9 18.3 %add_convert_fusion = bf16[1024,4096]{1,0:T(8,128)(2,1)} fusion(bf16[1024,4096]{1,0:T(8,128)(2,1)} %collective-permute-done.28, bf16[1024,4096]{1,0:T(8,128)(2,1)} %pair_backward.1, pred[]{:T(512)S(6)} %eq.43, bf16[1024,256]{1,0:T(8,128)(2,1)S(1)} %copy-done.68, bf16[1024,256]{1,0:T(8,128)(2,1)S(1)} %copy-done.69, bf16[1024,256]{1,0:T(8,128)(2,1)S(1)} %copy-done.70, ...), kind=kOutput, calls=%fused_computation.2 | convolution fusion | flops 8620343296 | bytes 29360128 | tf_op jit(solution)/shard_map/dot_general | solution.py:33
  568.5 16.4 %collective-permute-done.29 = bf16[256,2048]{1,0:T(8,128)(2,1)S(1)} collective-permute-done((bf16[256,2048]{1,0:T(8,128)(2,1)}, bf16[256,2048]{1,0:T(8,128)(2,1)S(1)}, u32[]{:S(2)}, u32[]{:S(2)}) %collective-permute-start.29) | collective-permute-done | bytes 1048608 | tf_op jit(solution)/shard_map/ppermute | solution.py:45
  592.7 5.0 collective-permute-done.31
  599.4 5.6 convolution_convert_fusion.3.g_ref
  605.0 21.1 %attend_backward.1 = (f32[1024,512]{1,0:T(8,128)}, f32[1024,512]{1,0:T(8,128)}, bf16[1024,512]{1,0:T(8,128)(2,1)}) custom-call(bf16[1024,512]{1,0:T(8,128)(2,1)} %get-tuple-element.76.q_ref, bf16[1024,512]{1,0:T(8,128)(2,1)} %get-tuple-element.75.k_ref, bf16[1024,512]{1,0:T(8,128)(2,1)} %copy-done.33, bf16[1024,512]{1,0:T(8,128)(2,1)} %convolution_convert_fusion.3.g_ref, ...), custom_call_target="tpu_custom_call" | custom-call | flops 5368709120 | bytes 8388608 | tf_op jit(solution)/shard_map/attend_backward/pallas_call | solution.py:191
  626.1 4.2 multiply_reduce_fusion
  642.7 5.2 convolution_convert_fusion.1
  655.2 3.8 add_convert_fusion.4
  663.3 5.8 add_convert_fusion.3
  673.2 10.8 %fusion.125 = (bf16[1024,2048]{1,0:T(8,128)(2,1)S(1)}, f32[1024,2048]{1,0:T(8,128)}) fusion(bf16[1024,1536]{1,0:T(8,128)(2,1)S(1)} %pad_maximum_fusion.1, bf16[2048,2048]{1,0:T(8,128)(2,1)} %all-gather.5.cloned.1.call-done), kind=kOutput, calls=%fused_computation.287 | convolution fusion | flops 6444548096 | bytes 22020096 | tf_op jit(solution)/shard_map/dot_general | solution.py:41
  690.9 8.6 collective-permute-done.48
  722.1 3.7 collective-permute-done.51
  727.9 3.7 fusion.17
  731.6 15.6 %reduce-scatter.4.cloned.1.call-done = bf16[256,2048]{1,0:T(8,128)(2,1)} async-done(((bf16[1024,2048]{1,0:T(8,128)(2,1)}), bf16[256,2048]{1,0:T(8,128)(2,1)}) %reduce-scatter.4.cloned.1.call-update) | async-done | bytes 1048592 | tf_op jit(solution)/shard_map/reduce_scatter | solution.py:347
  750.8 143.7 %reduce-scatter.6.cloned.1.call-done = bf16[256,4096]{1,0:T(8,128)(2,1)} async-done(((bf16[1024,4096]{1,0:T(8,128)(2,1)}), bf16[256,4096]{1,0:T(8,128)(2,1)}) %reduce-scatter.6.cloned.1.call-update) | async-done | bytes 2097168 | tf_op jit(solution)/shard_map/reduce_scatter | solution.py:347
  894.5 6.6 reshape.397
  901.1 14.2 %slice_reduce_fusion = (f32[256,8,256]{2,1,0:T(8,128)S(1)}, f32[256,8,256]{2,1,0:T(8,128)S(1)}) fusion(f32[256,8,2,256]{3,2,1,0:T(2,128)} %reshape.397), kind=kLoop, calls=%fused_computation.36 | loop fusion | bytes 8388608 | tf_op jit(solution)/shard_map/slice | solution.py:539
  (512 shorter events, 232.9 us)
Async XLA Ops:
  7.2 91.2 %all-gather.5.cloned.1.call-start = ((), (), s32[]{:S(2)}) async-start(), calls=%async_computation.3 | async-start | bytes 9437184 | tf_op jit(solution)/shard_map/all_gather | solution.py:378
  13.0 242.7 %all-gather.7.cloned.1.call-start = ((), (), s32[]{:S(2)}) async-start(), calls=%async_computation.4 | async-start | bytes 18874368 | tf_op jit(solution)/shard_map/all_gather | solution.py:379
  29.5 302.4 %all-gather.9.cloned.1.call-start = ((), (), s32[]{:S(2)}) async-start(), calls=%async_computation.5 | async-start | bytes 9437184 | tf_op jit(solution)/shard_map/all_gather | solution.py:380
  29.5 26.2 %collective-permute-start = (bf16[256,2048]{1,0:T(8,128)(2,1)S(1)}, bf16[256,2048]{1,0:T(8,128)(2,1)S(1)}, u32[]{:S(2)}, u32[]{:S(2)}) collective-permute-start(bf16[256,2048]{1,0:T(8,128)(2,1)S(1)} %copy-done.31), channel_id=1, source_target_pairs={{0,1},{1,0},{2,3},{3,2},{4,5},{5,4},{6,7},{7,6},{8,9},{9,8},{10,11... | collective-permute-start | bytes 3145736 | tf_op jit(solution)/shard_map/ppermute | solution.py:45
  32.6 40.4 %collective-permute-start.1 = (bf16[256,2048]{1,0:T(8,128)(2,1)S(1)}, bf16[256,2048]{1,0:T(8,128)(2,1)}, u32[]{:S(2)}, u32[]{:S(2)}) collective-permute-start(bf16[256,2048]{1,0:T(8,128)(2,1)S(1)} %copy-done.31), channel_id=1, source_target_pairs={{0,2},{1,3},{2,0},{3,1},{4,6},{5,7},{6,4},{7,5},{8,10},{9,11},{10,... | collective-permute-start | bytes 3145736 | tf_op jit(solution)/shard_map/ppermute | solution.py:45
  34.1 683.4 %reduce-scatter.8.cloned.1.call-start = ((), (), s32[]{:S(2)}) async-start(), calls=%async_computation.8 | async-start | bytes 5242880 | tf_op jit(solution)/shard_map/reduce_scatter | solution.py:347
  56.6 22.5 %collective-permute-start.2 = (bf16[128,2048]{1,0:T(8,128)(2,1)}, bf16[128,2048]{1,0:T(8,128)(2,1)}, u32[]{:S(2)}, u32[]{:S(2)}) collective-permute-start(bf16[128,2048]{1,0:T(8,128)(2,1)} %slice.679), channel_id=1, source_target_pairs={{0,2},{1,3},{2,0},{3,1},{4,6},{5,7},{6,4},{7,5},{8,10},{9,11},{10,... | collective-permute-start | bytes 1572872 | tf_op jit(solution)/shard_map/ppermute | solution.py:45
  74.1 14.2 %collective-permute-start.3 = (bf16[128,2048]{1,0:T(8,128)(2,1)S(1)}, bf16[128,2048]{1,0:T(8,128)(2,1)S(1)}, u32[]{:S(2)}, u32[]{:S(2)}) collective-permute-start(bf16[128,2048]{1,0:T(8,128)(2,1)S(1)} %slice.680), channel_id=1, source_target_pairs={{0,1},{1,0},{2,3},{3,2},{4,5},{5,4},{6,7},{7,6},{8,9},{9,8},{10,11... | collective-permute-start | bytes 1572872 | tf_op jit(solution)/shard_map/ppermute | solution.py:45
  112.2 21.7 %collective-permute-start.5 = (f32[2,4,256]{2,1,0:T(4,128)S(1)}, f32[2,4,256]{2,1,0:T(4,128)S(1)}, u32[]{:S(2)}, u32[]{:S(2)}) collective-permute-start(f32[2,4,256]{2,1,0:T(4,128)S(1)} %constant_dynamic-update-slice_fusion.8), channel_id=1, source_target_pairs={{0,2},{1,3},{2,0},{3,1},{4,6},{5,7},{6,4},{7,5},{8,10},{9,11},{10,... | collective-permute-start | bytes 24584 | tf_op jit(solution)/shard_map/ppermute | solution.py:45
  118.2 15.7 %collective-permute-start.6 = (f32[2,4,256]{2,1,0:T(4,128)S(1)}, f32[2,4,256]{2,1,0:T(4,128)S(1)}, u32[]{:S(2)}, u32[]{:S(2)}) collective-permute-start(f32[2,4,256]{2,1,0:T(4,128)S(1)} %constant_dynamic-update-slice_fusion.8), channel_id=1, source_target_pairs={{0,3},{1,2},{2,1},{3,0},{4,7},{5,6},{6,5},{7,4},{8,11},{9,10},{10,... | collective-permute-start | bytes 24584 | tf_op jit(solution)/shard_map/ppermute | solution.py:45
  119.7 14.3 %collective-permute-start.4 = (f32[2,4,256]{2,1,0:T(4,128)S(1)}, f32[2,4,256]{2,1,0:T(4,128)S(1)}, u32[]{:S(2)}, u32[]{:S(2)}) collective-permute-start(f32[2,4,256]{2,1,0:T(4,128)S(1)} %constant_dynamic-update-slice_fusion.8), channel_id=1, source_target_pairs={{0,1},{1,0},{2,3},{3,2},{4,5},{5,4},{6,7},{7,6},{8,9},{9,8},{10,11... | collective-permute-start | bytes 24584 | tf_op jit(solution)/shard_map/ppermute | solution.py:45
  176.0 13.3 %collective-permute-start.7 = (bf16[128,2048]{1,0:T(8,128)(2,1)S(1)}, bf16[128,2048]{1,0:T(8,128)(2,1)S(1)}, u32[]{:S(2)}, u32[]{:S(2)}) collective-permute-start(bf16[128,2048]{1,0:T(8,128)(2,1)S(1)} %get-tuple-element.120), channel_id=1, source_target_pairs={{0,2},{1,3},{2,0},{3,1},{4,6},{5,7},{6,4},{7,5},{8,10},{9,11},{10,... | collective-permute-start | bytes 1572872 | tf_op jit(solution)/shard_map/ppermute | solution.py:45
  177.5 13.0 %collective-permute-start.9 = (bf16[128,2048]{1,0:T(8,128)(2,1)S(1)}, bf16[128,2048]{1,0:T(8,128)(2,1)S(1)}, u32[]{:S(2)}, u32[]{:S(2)}) collective-permute-start(bf16[128,2048]{1,0:T(8,128)(2,1)S(1)} %get-tuple-element.119), channel_id=1, source_target_pairs={{0,1},{1,0},{2,3},{3,2},{4,5},{5,4},{6,7},{7,6},{8,9},{9,8},{10,11... | collective-permute-start | bytes 1572872 | tf_op jit(solution)/shard_map/ppermute | solution.py:45
  191.0 23.5 %collective-permute-start.10 = (bf16[256,2048]{1,0:T(8,128)(2,1)S(1)}, bf16[256,2048]{1,0:T(8,128)(2,1)S(1)}, u32[]{:S(2)}, u32[]{:S(2)}) collective-permute-start(bf16[256,2048]{1,0:T(8,128)(2,1)S(1)} %pad_maximum_fusion.11), channel_id=1, source_target_pairs={{0,2},{1,3},{2,0},{3,1},{4,6},{5,7},{6,4},{7,5},{8,10},{9,11},{10,... | collective-permute-start | bytes 3145736 | tf_op jit(solution)/shard_map/ppermute | solution.py:45
  191.6 23.4 %collective-permute-start.8 = (bf16[256,2048]{1,0:T(8,128)(2,1)S(1)}, bf16[256,2048]{1,0:T(8,128)(2,1)S(1)}, u32[]{:S(2)}, u32[]{:S(2)}) collective-permute-start(bf16[256,2048]{1,0:T(8,128)(2,1)S(1)} %pad_maximum_fusion.10), channel_id=1, source_target_pairs={{0,1},{1,0},{2,3},{3,2},{4,5},{5,4},{6,7},{7,6},{8,9},{9,8},{10,11... | collective-permute-start | bytes 3145736 | tf_op jit(solution)/shard_map/ppermute | solution.py:45
  217.9 22.5 %collective-permute-start.11 = (bf16[256,2048]{1,0:T(8,128)(2,1)S(1)}, bf16[256,2048]{1,0:T(8,128)(2,1)S(1)}, u32[]{:S(2)}, u32[]{:S(2)}) collective-permute-start(bf16[256,2048]{1,0:T(8,128)(2,1)S(1)} %get-tuple-element.67), channel_id=1, source_target_pairs={{0,1},{1,0},{2,3},{3,2},{4,5},{5,4},{6,7},{7,6},{8,9},{9,8},{10,11... | collective-permute-start | bytes 3145736 | tf_op jit(solution)/shard_map/ppermute | solution.py:45
  219.4 24.6 %collective-permute-start.12 = (bf16[256,2048]{1,0:T(8,128)(2,1)S(1)}, bf16[256,2048]{1,0:T(8,128)(2,1)S(1)}, u32[]{:S(2)}, u32[]{:S(2)}) collective-permute-start(bf16[256,2048]{1,0:T(8,128)(2,1)S(1)} %get-tuple-element.67), channel_id=1, source_target_pairs={{0,2},{1,3},{2,0},{3,1},{4,6},{5,7},{6,4},{7,5},{8,10},{9,11},{10,... | collective-permute-start | bytes 3145736 | tf_op jit(solution)/shard_map/ppermute | solution.py:45
  241.3 11.7 %collective-permute-start.13 = (bf16[128,2048]{1,0:T(8,128)(2,1)}, bf16[128,2048]{1,0:T(8,128)(2,1)}, u32[]{:S(2)}, u32[]{:S(2)}) collective-permute-start(bf16[128,2048]{1,0:T(8,128)(2,1)} %slice.711), channel_id=1, source_target_pairs={{0,2},{1,3},{2,0},{3,1},{4,6},{5,7},{6,4},{7,5},{8,10},{9,11},{10,... | collective-permute-start | bytes 1572872 | tf_op jit(solution)/shard_map/ppermute | solution.py:45
  244.0 10.9 %collective-permute-start.14 = (bf16[128,2048]{1,0:T(8,128)(2,1)S(1)}, bf16[128,2048]{1,0:T(8,128)(2,1)S(1)}, u32[]{:S(2)}, u32[]{:S(2)}) collective-permute-start(bf16[128,2048]{1,0:T(8,128)(2,1)S(1)} %slice.712), channel_id=1, source_target_pairs={{0,1},{1,0},{2,3},{3,2},{4,5},{5,4},{6,7},{7,6},{8,9},{9,8},{10,11... | collective-permute-start | bytes 1572872 | tf_op jit(solution)/shard_map/ppermute | solution.py:45
  338.2 14.1 %collective-permute-start.17 = (bf16[128,2048]{1,0:T(8,128)(2,1)S(1)}, bf16[128,2048]{1,0:T(8,128)(2,1)S(1)}, u32[]{:S(2)}, u32[]{:S(2)}) collective-permute-start(bf16[128,2048]{1,0:T(8,128)(2,1)S(1)} %get-tuple-element.153), channel_id=1, source_target_pairs={{0,1},{1,0},{2,3},{3,2},{4,5},{5,4},{6,7},{7,6},{8,9},{9,8},{10,11... | collective-permute-start | bytes 1572872 | tf_op jit(solution)/shard_map/ppermute | solution.py:45
  339.7 13.8 %collective-permute-start.15 = (bf16[128,2048]{1,0:T(8,128)(2,1)S(1)}, bf16[128,2048]{1,0:T(8,128)(2,1)S(1)}, u32[]{:S(2)}, u32[]{:S(2)}) collective-permute-start(bf16[128,2048]{1,0:T(8,128)(2,1)S(1)} %get-tuple-element.154), channel_id=1, source_target_pairs={{0,2},{1,3},{2,0},{3,1},{4,6},{5,7},{6,4},{7,5},{8,10},{9,11},{10,... | collective-permute-start | bytes 1572872 | tf_op jit(solution)/shard_map/ppermute | solution.py:45
  353.9 24.2 %collective-permute-start.16 = (bf16[256,2048]{1,0:T(8,128)(2,1)S(1)}, bf16[256,2048]{1,0:T(8,128)(2,1)S(1)}, u32[]{:S(2)}, u32[]{:S(2)}) collective-permute-start(bf16[256,2048]{1,0:T(8,128)(2,1)S(1)} %pad_maximum_fusion.12), channel_id=1, source_target_pairs={{0,1},{1,0},{2,3},{3,2},{4,5},{5,4},{6,7},{7,6},{8,9},{9,8},{10,11... | collective-permute-start | bytes 3145736 | tf_op jit(solution)/shard_map/ppermute | solution.py:45
  354.6 24.1 %collective-permute-start.18 = (bf16[256,2048]{1,0:T(8,128)(2,1)S(1)}, bf16[256,2048]{1,0:T(8,128)(2,1)}, u32[]{:S(2)}, u32[]{:S(2)}) collective-permute-start(bf16[256,2048]{1,0:T(8,128)(2,1)S(1)} %pad_maximum_fusion.13), channel_id=1, source_target_pairs={{0,2},{1,3},{2,0},{3,1},{4,6},{5,7},{6,4},{7,5},{8,10},{9,11},{10,... | collective-permute-start | bytes 3145736 | tf_op jit(solution)/shard_map/ppermute | solution.py:45
  385.7 23.7 %collective-permute-start.19 = (bf16[256,2048]{1,0:T(8,128)(2,1)}, bf16[256,2048]{1,0:T(8,128)(2,1)S(1)}, u32[]{:S(2)}, u32[]{:S(2)}) collective-permute-start(bf16[256,2048]{1,0:T(8,128)(2,1)} %get-tuple-element.36), channel_id=1, source_target_pairs={{0,1},{1,0},{2,3},{3,2},{4,5},{5,4},{6,7},{7,6},{8,9},{9,8},{10,11... | collective-permute-start | bytes 3145736 | tf_op jit(solution)/shard_map/ppermute | solution.py:45
  386.8 24.2 %collective-permute-start.20 = (bf16[256,2048]{1,0:T(8,128)(2,1)}, bf16[256,2048]{1,0:T(8,128)(2,1)S(1)}, u32[]{:S(2)}, u32[]{:S(2)}) collective-permute-start(bf16[256,2048]{1,0:T(8,128)(2,1)} %get-tuple-element.36), channel_id=1, source_target_pairs={{0,2},{1,3},{2,0},{3,1},{4,6},{5,7},{6,4},{7,5},{8,10},{9,11},{10,... | collective-permute-start | bytes 3145736 | tf_op jit(solution)/shard_map/ppermute | solution.py:45
  409.5 12.7 %collective-permute-start.21 = (bf16[128,2048]{1,0:T(8,128)(2,1)S(1)}, bf16[128,2048]{1,0:T(8,128)(2,1)S(1)}, u32[]{:S(2)}, u32[]{:S(2)}) collective-permute-start(bf16[128,2048]{1,0:T(8,128)(2,1)S(1)} %slice.721), channel_id=1, source_target_pairs={{0,2},{1,3},{2,0},{3,1},{4,6},{5,7},{6,4},{7,5},{8,10},{9,11},{10,... | collective-permute-start | bytes 1572872 | tf_op jit(solution)/shard_map/ppermute | solution.py:45
  411.1 11.3 %collective-permute-start.22 = (bf16[128,2048]{1,0:T(8,128)(2,1)S(1)}, bf16[128,2048]{1,0:T(8,128)(2,1)S(1)}, u32[]{:S(2)}, u32[]{:S(2)}) collective-permute-start(bf16[128,2048]{1,0:T(8,128)(2,1)S(1)} %slice.722), channel_id=1, source_target_pairs={{0,1},{1,0},{2,3},{3,2},{4,5},{5,4},{6,7},{7,6},{8,9},{9,8},{10,11... | collective-permute-start | bytes 1572872 | tf_op jit(solution)/shard_map/ppermute | solution.py:45
  474.0 63.8 %collective-permute-start.28 = (bf16[1024,4096]{1,0:T(8,128)(2,1)}, bf16[1024,4096]{1,0:T(8,128)(2,1)}, u32[]{:S(2)}, u32[]{:S(2)}) collective-permute-start(bf16[1024,4096]{1,0:T(8,128)(2,1)} %convolution_convert_fusion), channel_id=1, source_target_pairs={{0,4},{4,0},{8,12},{12,8},{16,20},{20,16},{24,28},{28,24},{1,5},{5... | collective-permute-start | bytes 25165832 | tf_op jit(solution)/shard_map/ppermute | solution.py:328
  495.4 14.3 %collective-permute-start.24 = (bf16[128,2048]{1,0:T(8,128)(2,1)S(1)}, bf16[128,2048]{1,0:T(8,128)(2,1)S(1)}, u32[]{:S(2)}, u32[]{:S(2)}) collective-permute-start(bf16[128,2048]{1,0:T(8,128)(2,1)S(1)} %get-tuple-element.106), channel_id=1, source_target_pairs={{0,2},{1,3},{2,0},{3,1},{4,6},{5,7},{6,4},{7,5},{8,10},{9,11},{10,... | collective-permute-start | bytes 1572872 | tf_op jit(solution)/shard_map/ppermute | solution.py:45
  496.9 13.9 %collective-permute-start.26 = (bf16[128,2048]{1,0:T(8,128)(2,1)S(1)}, bf16[128,2048]{1,0:T(8,128)(2,1)S(1)}, u32[]{:S(2)}, u32[]{:S(2)}) collective-permute-start(bf16[128,2048]{1,0:T(8,128)(2,1)S(1)} %get-tuple-element.105), channel_id=1, source_target_pairs={{0,1},{1,0},{2,3},{3,2},{4,5},{5,4},{6,7},{7,6},{8,9},{9,8},{10,11... | collective-permute-start | bytes 1572872 | tf_op jit(solution)/shard_map/ppermute | solution.py:45
  511.3 24.4 %collective-permute-start.27 = (bf16[256,2048]{1,0:T(8,128)(2,1)S(1)}, bf16[256,2048]{1,0:T(8,128)(2,1)S(1)}, u32[]{:S(2)}, u32[]{:S(2)}) collective-permute-start(bf16[256,2048]{1,0:T(8,128)(2,1)S(1)} %pad_maximum_fusion.15), channel_id=1, source_target_pairs={{0,2},{1,3},{2,0},{3,1},{4,6},{5,7},{6,4},{7,5},{8,10},{9,11},{10,... | collective-permute-start | bytes 3145736 | tf_op jit(solution)/shard_map/ppermute | solution.py:45
  512.0 24.1 %collective-permute-start.25 = (bf16[256,2048]{1,0:T(8,128)(2,1)S(1)}, bf16[256,2048]{1,0:T(8,128)(2,1)S(1)}, u32[]{:S(2)}, u32[]{:S(2)}) collective-permute-start(bf16[256,2048]{1,0:T(8,128)(2,1)S(1)} %pad_maximum_fusion.14), channel_id=1, source_target_pairs={{0,1},{1,0},{2,3},{3,2},{4,5},{5,4},{6,7},{7,6},{8,9},{9,8},{10,11... | collective-permute-start | bytes 3145736 | tf_op jit(solution)/shard_map/ppermute | solution.py:45
  561.5 23.4 %collective-permute-start.29 = (bf16[256,2048]{1,0:T(8,128)(2,1)}, bf16[256,2048]{1,0:T(8,128)(2,1)S(1)}, u32[]{:S(2)}, u32[]{:S(2)}) collective-permute-start(bf16[256,2048]{1,0:T(8,128)(2,1)} %get-tuple-element.64), channel_id=1, source_target_pairs={{0,1},{1,0},{2,3},{3,2},{4,5},{5,4},{6,7},{7,6},{8,9},{9,8},{10,11... | collective-permute-start | bytes 3145736 | tf_op jit(solution)/shard_map/ppermute | solution.py:45
  563.3 24.8 %collective-permute-start.30 = (bf16[256,2048]{1,0:T(8,128)(2,1)}, bf16[256,2048]{1,0:T(8,128)(2,1)S(1)}, u32[]{:S(2)}, u32[]{:S(2)}) collective-permute-start(bf16[256,2048]{1,0:T(8,128)(2,1)} %get-tuple-element.64), channel_id=1, source_target_pairs={{0,2},{1,3},{2,0},{3,1},{4,6},{5,7},{6,4},{7,5},{8,10},{9,11},{10,... | collective-permute-start | bytes 3145736 | tf_op jit(solution)/shard_map/ppermute | solution.py:45
  584.9 12.8 %collective-permute-start.31 = (bf16[128,2048]{1,0:T(8,128)(2,1)S(1)}, bf16[128,2048]{1,0:T(8,128)(2,1)S(1)}, u32[]{:S(2)}, u32[]{:S(2)}) collective-permute-start(bf16[128,2048]{1,0:T(8,128)(2,1)S(1)} %slice.751), channel_id=1, source_target_pairs={{0,2},{1,3},{2,0},{3,1},{4,6},{5,7},{6,4},{7,5},{8,10},{9,11},{10,... | collective-permute-start | bytes 1572872 | tf_op jit(solution)/shard_map/ppermute | solution.py:45
  587.1 160.1 %reduce-scatter.4.cloned.1.call-start = ((), (), s32[]{:S(2)}) async-start(), calls=%async_computation.6 | async-start | bytes 5242880 | tf_op jit(solution)/shard_map/reduce_scatter | solution.py:347
  588.1 10.4 %collective-permute-start.32 = (bf16[128,2048]{1,0:T(8,128)(2,1)S(1)}, bf16[128,2048]{1,0:T(8,128)(2,1)S(1)}, u32[]{:S(2)}, u32[]{:S(2)}) collective-permute-start(bf16[128,2048]{1,0:T(8,128)(2,1)S(1)} %slice.752), channel_id=1, source_target_pairs={{0,1},{1,0},{2,3},{3,2},{4,5},{5,4},{6,7},{7,6},{8,9},{9,8},{10,11... | collective-permute-start | bytes 1572872 | tf_op jit(solution)/shard_map/ppermute | solution.py:45
  647.9 14.7 %collective-permute-start.46 = (bf16[1024,1536]{1,0:T(8,128)(2,1)}, bf16[1024,1536]{1,0:T(8,128)(2,1)}, u32[]{:S(2)}, u32[]{:S(2)}) collective-permute-start(bf16[1024,1536]{1,0:T(8,128)(2,1)} %convolution_convert_fusion.1), channel_id=1, source_target_pairs={{0,4},{4,0},{8,12},{12,8},{16,20},{20,16},{24,28},{28,24},{1,5},{5... | collective-permute-start | bytes 9437192 | tf_op jit(solution)/shard_map/ppermute | solution.py:328
  671.7 222.8 %reduce-scatter.6.cloned.1.call-start = ((), (), s32[]{:S(2)}) async-start(), calls=%async_computation.7 | async-start | bytes 10485760 | tf_op jit(solution)/shard_map/reduce_scatter | solution.py:347
  684.1 15.4 %collective-permute-start.48 = (bf16[128,2048]{1,0:T(8,128)(2,1)S(1)}, bf16[128,2048]{1,0:T(8,128)(2,1)S(1)}, u32[]{:S(2)}, u32[]{:S(2)}) collective-permute-start(bf16[128,2048]{1,0:T(8,128)(2,1)S(1)} %get-tuple-element.86), channel_id=1, source_target_pairs={{0,2},{1,3},{2,0},{3,1},{4,6},{5,7},{6,4},{7,5},{8,10},{9,11},{10,... | collective-permute-start | bytes 1572872 | tf_op jit(solution)/shard_map/ppermute | solution.py:45
  684.8 14.8 %collective-permute-start.50 = (bf16[128,2048]{1,0:T(8,128)(2,1)S(1)}, bf16[128,2048]{1,0:T(8,128)(2,1)S(1)}, u32[]{:S(2)}, u32[]{:S(2)}) collective-permute-start(bf16[128,2048]{1,0:T(8,128)(2,1)S(1)} %get-tuple-element.85), channel_id=1, source_target_pairs={{0,1},{1,0},{2,3},{3,2},{4,5},{5,4},{6,7},{7,6},{8,9},{9,8},{10,11... | collective-permute-start | bytes 1572872 | tf_op jit(solution)/shard_map/ppermute | solution.py:45
  687.3 17.9 %collective-permute-start.34 = (f32[8,2048]{1,0:T(8,128)S(1)}, f32[8,2048]{1,0:T(8,128)S(1)}, u32[]{:S(2)}, u32[]{:S(2)}) collective-permute-start(f32[8,2048]{1,0:T(8,128)S(1)} %concatenate.157), channel_id=1, source_target_pairs={{0,2},{1,3},{2,0},{3,1},{4,6},{5,7},{6,4},{7,5},{8,10},{9,11},{10,... | collective-permute-start | bytes 196616 | tf_op jit(solution)/shard_map/ppermute | solution.py:45
  688.9 16.3 %collective-permute-start.35 = (f32[8,2048]{1,0:T(8,128)S(1)}, f32[8,2048]{1,0:T(8,128)S(1)}, u32[]{:S(2)}, u32[]{:S(2)}) collective-permute-start(f32[8,2048]{1,0:T(8,128)S(1)} %concatenate.157), channel_id=1, source_target_pairs={{0,3},{1,2},{2,1},{3,0},{4,7},{5,6},{6,5},{7,4},{8,11},{9,10},{10,... | collective-permute-start | bytes 196616 | tf_op jit(solution)/shard_map/ppermute | solution.py:45
  690.7 14.5 %collective-permute-start.33 = (f32[8,2048]{1,0:T(8,128)S(1)}, f32[8,2048]{1,0:T(8,128)S(1)}, u32[]{:S(2)}, u32[]{:S(2)}) collective-permute-start(f32[8,2048]{1,0:T(8,128)S(1)} %concatenate.157), channel_id=1, source_target_pairs={{0,1},{1,0},{2,3},{3,2},{4,5},{5,4},{6,7},{7,6},{8,9},{9,8},{10,11... | collective-permute-start | bytes 196616 | tf_op jit(solution)/shard_map/ppermute | solution.py:45
  702.5 23.3 %collective-permute-start.51 = (bf16[256,2048]{1,0:T(8,128)(2,1)}, bf16[256,2048]{1,0:T(8,128)(2,1)}, u32[]{:S(2)}, u32[]{:S(2)}) collective-permute-start(bf16[256,2048]{1,0:T(8,128)(2,1)} %pad_maximum_fusion.17), channel_id=1, source_target_pairs={{0,2},{1,3},{2,0},{3,1},{4,6},{5,7},{6,4},{7,5},{8,10},{9,11},{10,... | collective-permute-start | bytes 3145736 | tf_op jit(solution)/shard_map/ppermute | solution.py:45
  704.9 23.0 %collective-permute-start.49 = (bf16[256,2048]{1,0:T(8,128)(2,1)}, bf16[256,2048]{1,0:T(8,128)(2,1)S(1)}, u32[]{:S(2)}, u32[]{:S(2)}) collective-permute-start(bf16[256,2048]{1,0:T(8,128)(2,1)} %pad_maximum_fusion.16), channel_id=1, source_target_pairs={{0,1},{1,0},{2,3},{3,2},{4,5},{5,4},{6,7},{7,6},{8,9},{9,8},{10,11... | collective-permute-start | bytes 3145736 | tf_op jit(solution)/shard_map/ppermute | solution.py:45
  705.3 8.2 collective-permute-start.41
  706.2 7.3 collective-permute-start.40
  (123 other events, 1035.0 us)
Sparse Core Ops, SparseCore 0:
  13.1 85.1 all-gather.4
  100.0 149.5 all-gather.6
  251.2 80.6 all-gather.8
  587.2 74.2 reduce-scatter.7
  671.8 75.3 reduce-scatter.3
  749.4 145.0 reduce-scatter.5

commit v3 on v2

--- a/solution.py
+++ b/solution.py
@@ -51,16 +51,22 @@
         self.me = lax.axis_index("tensor")
         self.order = self.me ^ jnp.arange(size)
 
-    def gather_parts(self, own):
+    def gather_halves(self, upper, lower):
+        across_a = hop(upper, 1)
+        along_a = hop(upper, 2)
+        across_b = hop(lower, 1)
+        along_b = hop(lower, 2)
+        first = hop(across_a, 2)
+        second = hop(along_b, 1)
+        return upper, lower, across_a, across_b, along_a, along_b, first, second
+
+    def gather(self, own):
         half = own.shape[0] // 2
         across = hop(own, 1)
         along = hop(own, 2)
         first = hop(across[:half], 2)
         second = hop(along[half:], 1)
-        return own, across, along, first, second
-
-    def gather(self, own):
-        return jnp.concatenate(self.gather_parts(own), axis=0)
+        return jnp.concatenate([own, across, along, first, second], axis=0)
 
     def scatter_product(self, left, right):
         rows = left.shape[0] // 4
@@ -69,13 +75,12 @@
         first = hop(far[:half], 1)
         second = hop(far[half:], 2)
         near = lax.optimization_barrier(times(left[rows : 3 * rows], right))
-        across, along = near[:rows], near[rows:]
-        along = jnp.concatenate([along[:half] + first.astype(F32), along[half:]], axis=0).astype(BF)
-        across = jnp.concatenate([across[:half], across[half:] + second.astype(F32)], axis=0).astype(BF)
-        across = hop(across, 1)
-        along = hop(along, 2)
+        across_a = hop(near[:half].astype(BF), 1)
+        along_a = hop((near[rows : rows + half] + first.astype(F32)).astype(BF), 2)
+        across_b = hop((near[half:rows] + second.astype(F32)).astype(BF), 1)
+        along_b = hop(near[rows + half :].astype(BF), 2)
         own = times(left[:rows], right)
-        return own, across, along
+        return own, (across_a, along_a), (across_b, along_b)
 
     def scatter(self, parts):
         rows = parts.shape[0] // 4
@@ -112,7 +117,7 @@
         return lax.all_gather(own, "tensor", axis=0, tiled=True)
 
     def scatter_product(self, left, right):
-        return (self.scatter(times(left, right)),)
+        return self.scatter(times(left, right))
 
     def scatter(self, parts):
         return lax.psum_scatter(
@@ -237,14 +242,16 @@
     )(piece, down, pair)
 
 
-def loss_and_back(parts, resid, teacher, valid, gain, block=64):
+def loss_and_back(own, arrived, resid, teacher, valid, gain, first, last, kept=None, block=64):
     rows, width = resid.shape
-    count = len(parts)
+    count = len(arrived)
+    held = () if kept is None else tuple(kept)
 
     def body(*refs):
-        x_ref, t_ref, v_ref, w_ref, o_ref, g_ref, b_ref, sum_ref = refs[count:]
-        branch = refs[0][...]
-        for ref in refs[1:count]:
+        own_ref, x_ref, t_ref, v_ref, w_ref = refs[:5]
+        o_ref, g_ref, b_ref, sum_ref = refs[5 + count + len(held) :]
+        branch = own_ref[...]
+        for ref in refs[5 : 5 + count]:
             branch = branch + ref[...].astype(F32)
         scale = lax.rsqrt(jnp.mean(branch * branch, axis=1, keepdims=True) + EPS)
         normed = branch * scale
@@ -264,23 +271,31 @@
         sum_ref[0:1, :] += jnp.sum(grad * normed, axis=0, keepdims=True)
         sum_ref[1:2, :] += jnp.sum(error * error * v_ref[:, 0:1], axis=0, keepdims=True)
 
-    row = pl.BlockSpec((block, width), lambda i: (i, 0))
-    arrays = (*parts, resid, teacher)
+    skip = first // block
+    row = pl.BlockSpec((block, width), lambda i: (i + skip, 0))
+    part = pl.BlockSpec((block, width), lambda i: (i, 0))
+    arrays = (own, resid, teacher)
     return pl.pallas_call(
         body,
-        grid=(rows // block,),
-        in_specs=[row] * len(arrays)
-        + [pl.BlockSpec((block, 2), lambda i: (i, 0)), pl.BlockSpec((1, width), lambda i: (0, 0))],
-        out_specs=[row, row, row, pl.BlockSpec((8, width), lambda i: (0, 0))],
+        grid=((last - first) // block,),
+        in_specs=[row] * 3
+        + [
+            pl.BlockSpec((block, 2), lambda i: (i + skip, 0)),
+            pl.BlockSpec((1, width), lambda i: (0, 0)),
+        ]
+        + [part] * count
+        + [pl.BlockSpec(memory_space=pl.ANY)] * len(held),
+        out_specs=[row, row, part, pl.BlockSpec((8, width), lambda i: (0, 0))],
         out_shape=[
             jax.ShapeDtypeStruct((rows, width), BF),
             jax.ShapeDtypeStruct((rows, width), F32),
-            jax.ShapeDtypeStruct((rows, width), BF),
+            jax.ShapeDtypeStruct((last - first, width), BF),
             jax.ShapeDtypeStruct((8, width), F32),
         ],
-        cost_estimate=cost(30 * rows * width, *arrays),
+        input_output_aliases={5 + count + i: i for i in range(len(held))},
+        cost_estimate=cost(30 * (last - first) * width, *arrived, *arrived),
         name="loss_and_back",
-    )(*arrays, valid, gain.reshape(1, width))
+    )(*arrays, valid, gain.reshape(1, width), *arrived, *held)
 
 
 def pair_forward(rows, weights, block=BLOCK):
@@ -441,17 +456,23 @@
     my_segment = lax.dynamic_slice_in_dim(segment, ring.me * rows, rows)
     valid = (my_segment != 0).astype(F32)
     valid = jnp.stack([valid, valid * (2.0 * (rows * dp * tensor) / valid_total)], axis=1)
-    parts = ring.scatter_product(hidden, full_down)
-    output, grad_output, grad_branch_ffn, sums = loss_and_back(
-        parts, resid, teacher, valid, gain_ffn
-    )
+    rest = (resid, teacher, valid, gain_ffn)
+    if tensor == 4:
+        half = rows // 2
+        own, arrived_a, arrived_b = ring.scatter_product(hidden, full_down)
+        *kept, upper, sums_a = loss_and_back(own, arrived_a, *rest, 0, half)
+        output, grad_output, lower, sums_b = loss_and_back(own, arrived_b, *rest, half, rows, kept)
+        sums = sums_a + sums_b
+    else:
+        own = ring.scatter_product(hidden, full_down)
+        output, grad_output, grad_branch_ffn, sums = loss_and_back(own, (), *rest, 0, rows)
     grad_gain_ffn = sums[0]
     loss_part = jnp.sum(sums[1])
     if tensor == 4:
-        got_rows = ring.gather_parts(grad_branch_ffn)
+        got_rows = ring.gather_halves(upper, lower)
         cut = 3 * rows
-        near_halves = pick_halves(jnp.concatenate(got_rows[:3], axis=0), 1)
-        far_halves = pick_halves(jnp.concatenate(got_rows[3:], axis=0), 1)
+        near_halves = pick_halves(jnp.concatenate(got_rows[:6], axis=0), 1)
+        far_halves = pick_halves(jnp.concatenate(got_rows[6:], axis=0), 1)
         near = lax.optimization_barrier(
             tuple(inner_rows(hidden[:cut], half) for half in near_halves)
         )

time: 936 us -> 943 us (level)
    ppermute x41 -> x45, waiting for transfers between devices: 192 us -> 200 us  [hop(): return lax.ppermute(value, 'tensor', [(i, i ^ way) for i in range(size)])]
    unnamed x270 -> x285, local copies, waits for them, and re-layouts: 62.9 us -> 64.3 us
    ppermute x41 -> x45, starting transfers between devices: 51.4 us -> 51.8 us  [hop(): return lax.ppermute(value, 'tensor', [(i, i ^ way) for i in range(size)])]
  transfers between devices with their start and end apart: 58 -> 62, of which waited for: 34 -> 38; matrix products, arithmetic and copies ran while one was open for 25% -> 24% of each run, Pallas kernels for 5% -> 6%
where the time goes in v3:
time: 943 us; the launch traced here: 935 us
  waiting for transfers between devices  431 us (46%)
  matrix products  149 us (16%)
  local copies, waits for them, and re-layouts  128 us (14%)
  Pallas kernels  71.5 us (8%)
  starting transfers between devices  60.4 us (6%)
  other arithmetic  60.2 us (6%)
  between operations  19.7 us (2%)
  blocking collectives  14.7 us (2%)
    ppermute x45, waiting for transfers between devices, hop(): return lax.ppermute(value, 'tensor', [(i, i ^ way) for i in range(size)])  200 us
    reduce_scatter x3, waiting for transfers between devices, scatter_pairs(): lax.psum_scatter(value, 'dp', scatter_dimension=axis, axis_index_groups=g...  160 us
    dot_general x10, matrix products, inner_rows(): lax.dot_general(left, right, (((0,), (0,)), ((), ())), preferred_element_...  64.5 us
    unnamed x285, local copies, waits for them, and re-layouts  64.3 us
    ppermute x45, starting transfers between devices, hop(): return lax.ppermute(value, 'tensor', [(i, i ^ way) for i in range(size)])  51.8 us
    all_gather x1, waiting for transfers between devices, layer(): full_down = lax.all_gather(wd, 'dp', axis=1, tiled=True)  49.5 us
    dot_general x3, matrix products, times_transposed(): lax.dot_general(left, right, (((1,), (1,)), ((), ())), preferred_element_...  36.7 us
    dot_general x5, matrix products, times(): return jnp.dot(left, right, preferred_element_type=F32)  26.7 us
  transfers between devices with their start and end apart: 62, of which 38 were waited for; matrix products, arithmetic and copies ran while one was open for 24% of the time, Pallas kernels for 6%

profile of v3, /device:TPU:0, one launch (start us, length us, event | category | flops | bytes accessed | tf_op | source)
XLA Modules:
  0.0 935.1 jit_solution(745095047910600626)
XLA Ops:
  43.0 12.7 %collective-permute-done = bf16[256,2048]{1,0:T(8,128)(2,1)S(1)} collective-permute-done((bf16[256,2048]{1,0:T(8,128)(2,1)S(1)}, bf16[256,2048]{1,0:T(8,128)(2,1)S(1)}, u32[]{:S(2)}, u32[]{:S(2)}) %collective-permute-start) | collective-permute-done | bytes 1048608 | tf_op jit(solution)/shard_map/ppermute | solution.py:45
  58.3 14.7 %all-gather = f32[8,2048]{1,0:T(8,128)S(1)} all-gather(f32[8,256]{1,0:T(8,128)S(1)} %concatenate.124), channel_id=2, replica_groups=mesh['dp'=8,'tensor'=4] {'dp'}, dimensions={1}, use_global_device_ids=true | all-gather | bytes 73728 | tf_op jit(solution)/shard_map/all_gather | solution.py:404
  81.0 7.4 collective-permute-done.3
  89.2 9.2 all-gather.5.cloned.1.call-done
  98.4 10.0 %fusion.5 = f32[1024,1536]{1,0:T(8,128)S(1)} fusion(bf16[1024,2048]{1,0:T(8,128)(2,1)} %constant_dynamic-update-slice_fusion, bf16[2048,2048]{1,0:T(8,128)(2,1)} %all-gather.5.cloned.1.call-done), kind=kOutput, calls=%fused_computation.15 | convolution fusion | flops 6442450944 | bytes 16777216 | tf_op jit(solution)/shard_map/dot_general | solution.py:37
  124.6 4.3 reshape.386
  140.2 14.6 %fusion = (f32[4,1024]{1,0:T(4,128)S(1)}, f32[4,1024,1024]{1,2,0:T(8,128)}) fusion(pred[1024,1024]{0,1:T(8,128)(4,1)} %copy.62, f32[1024,128]{1,0:T(8,128)} %get-tuple-element.178.c_ref.cq_ref, f32[1024,128]{1,0:T(8,128)} %get-tuple-element.177, f32[1024,4,64]{2,0,1:T(8,128)S(1)} %get-tuple-element.142, f32[1024,4,64]{2,0,1:T(8,128)S(1)} %get-tuple-element.141, ...), kind=kOutput, calls=%fused_computation.6 | convolution fusion | flops 1091563520 | bytes 27279360 | tf_op jit(solution)/shard_map/qhd,khd->hqk/dot_general | solution.py:135
  154.8 8.7 fusion.1
  166.4 7.0 fusion.45
  179.0 10.2 %collective-permute-done.7 = bf16[128,2048]{1,0:T(8,128)(2,1)S(1)} collective-permute-done((bf16[128,2048]{1,0:T(8,128)(2,1)S(1)}, bf16[128,2048]{1,0:T(8,128)(2,1)S(1)}, u32[]{:S(2)}, u32[]{:S(2)}) %collective-permute-start.7) | collective-permute-done | bytes 524320 | tf_op jit(solution)/shard_map/ppermute | solution.py:45
  193.7 20.7 %collective-permute-done.10 = bf16[256,2048]{1,0:T(8,128)(2,1)S(1)} collective-permute-done((bf16[256,2048]{1,0:T(8,128)(2,1)S(1)}, bf16[256,2048]{1,0:T(8,128)(2,1)S(1)}, u32[]{:S(2)}, u32[]{:S(2)}) %collective-permute-start.10) | collective-permute-done | bytes 1048608 | tf_op jit(solution)/shard_map/ppermute | solution.py:45
  222.3 18.1 %collective-permute-done.11 = bf16[256,2048]{1,0:T(8,128)(2,1)S(1)} collective-permute-done((bf16[256,2048]{1,0:T(8,128)(2,1)S(1)}, bf16[256,2048]{1,0:T(8,128)(2,1)S(1)}, u32[]{:S(2)}, u32[]{:S(2)}) %collective-permute-start.11) | collective-permute-done | bytes 1048608 | tf_op jit(solution)/shard_map/ppermute | solution.py:45
  247.2 5.8 collective-permute-done.13
  255.7 24.7 %pair_forward.1 = (f32[1024,4096]{1,0:T(8,128)}, bf16[1024,2048]{1,0:T(8,128)(2,1)S(1)}) custom-call(bf16[1024,2048]{1,0:T(8,128)(2,1)} %constant_dynamic-update-slice_fusion.10.x_ref, bf16[2048,4096]{1,0:T(8,128)(2,1)} %all-gather.7.cloned.1.call-done.w_ref), custom_call_target="tpu_custom_call" | custom-call | flops 17179869184 | bytes 20971520 | tf_op jit(solution)/shard_map/pair_forward/pallas_call | solution.py:311
  282.4 49.5 %all-gather.9.cloned.1.call-done.w_ref = bf16[2048,2048]{1,0:T(8,128)(2,1)} async-done(((bf16[2048,256]{1,0:T(8,128)(2,1)}), bf16[2048,2048]{1,0:T(8,128)(2,1)}) %all-gather.9.cloned.1.call-update) | async-done | bytes 8388624 | tf_op jit(solution)/shard_map/all_gather | solution.py:395
  331.9 6.2 convolution_convert_fusion.2
  341.2 4.5 fusion.33
  347.2 5.8 collective-permute-done.19
  360.5 3.7 collective-permute-done.18.refs_5_
  364.2 11.7 %collective-permute-done.20.refs_6_ = bf16[128,2048]{1,0:T(8,128)(2,1)S(1)} collective-permute-done((bf16[128,2048]{1,0:T(8,128)(2,1)S(1)}, bf16[128,2048]{1,0:T(8,128)(2,1)S(1)}, u32[]{:S(2)}, u32[]{:S(2)}) %collective-permute-start.20) | collective-permute-done | bytes 524320 | tf_op jit(solution)/shard_map/ppermute | solution.py:45
  381.9 3.9 loss_and_back.3
  390.7 4.7 collective-permute-done.21
  395.5 9.3 collective-permute-done.22
  404.9 6.2 collective-permute-done.24
  422.5 6.0 collective-permute-done.25
  436.3 4.2 collective-permute-done.27
  446.3 18.2 %pair_backward.1 = bf16[1024,4096]{1,0:T(8,128)(2,1)} custom-call(bf16[1024,2048]{1,0:T(8,128)(2,1)S(1)} %copy-done.1, bf16[2048,2048]{1,0:T(8,128)(2,1)} %all-gather.9.cloned.1.call-done.w_ref, f32[1024,4096]{1,0:T(8,128)} %get-tuple-element.47.p_ref), custom_call_target="tpu_custom_call" | custom-call | flops 8589934592 | bytes 29360128 | tf_op jit(solution)/shard_map/pair_backward/pallas_call | solution.py:229
  464.6 16.6 %convolution_convert_fusion = bf16[1024,4096]{1,0:T(8,128)(2,1)} fusion(bf16[1024,4096]{1,0:T(8,128)(2,1)} %pair_backward.1, pred[]{:T(512)S(6)} %eq.43, bf16[1024,256]{1,0:T(8,128)(2,1)S(1)} %copy-done.67, bf16[1024,256]{1,0:T(8,128)(2,1)S(1)} %copy-done.68, bf16[1024,256]{1,0:T(8,128)(2,1)S(1)} %copy-done.69, bf16[1024,256]{1,0:T(8,128)(2,1)S(1)} %copy-done.70, ...), kind=kOutput, calls=%fused_computation.11 | convolution fusion | flops 8611954688 | bytes 20971520 | tf_op jit(solution)/shard_map/dot_general | solution.py:33
  481.4 20.3 %fusion.126 = f32[1024,2048]{1,0:T(8,128)S(1)} fusion(bf16[1024,4096]{1,0:T(8,128)(2,1)S(1)} %copy-done.28, bf16[2048,4096]{1,0:T(8,128)(2,1)} %all-gather.7.cloned.1.call-done.w_ref), kind=kOutput, calls=%fused_computation.292 | convolution fusion | flops 17179869184 | bytes 33554432 | tf_op jit(solution)/shard_map/dot_general | solution.py:41
  503.8 13.1 %collective-permute-done.28 = bf16[128,2048]{1,0:T(8,128)(2,1)S(1)} collective-permute-done((bf16[128,2048]{1,0:T(8,128)(2,1)S(1)}, bf16[128,2048]{1,0:T(8,128)(2,1)S(1)}, u32[]{:S(2)}, u32[]{:S(2)}) %collective-permute-start.28) | collective-permute-done | bytes 524320 | tf_op jit(solution)/shard_map/ppermute | solution.py:45
  524.8 17.1 %collective-permute-done.31 = bf16[256,2048]{1,0:T(8,128)(2,1)S(1)} collective-permute-done((bf16[256,2048]{1,0:T(8,128)(2,1)S(1)}, bf16[256,2048]{1,0:T(8,128)(2,1)S(1)}, u32[]{:S(2)}, u32[]{:S(2)}) %collective-permute-start.31) | collective-permute-done | bytes 1048608 | tf_op jit(solution)/shard_map/ppermute | solution.py:45
  545.1 18.3 %add_convert_fusion = bf16[1024,4096]{1,0:T(8,128)(2,1)} fusion(bf16[1024,4096]{1,0:T(8,128)(2,1)} %collective-permute-done.32, bf16[1024,4096]{1,0:T(8,128)(2,1)} %pair_backward.1, pred[]{:T(512)S(6)} %eq.43, bf16[1024,256]{1,0:T(8,128)(2,1)S(1)} %copy-done.67, bf16[1024,256]{1,0:T(8,128)(2,1)S(1)} %copy-done.68, bf16[1024,256]{1,0:T(8,128)(2,1)S(1)} %copy-done.69, ...), kind=kOutput, calls=%fused_computation.2 | convolution fusion | flops 8620343296 | bytes 29360128 | tf_op jit(solution)/shard_map/dot_general | solution.py:33
  575.1 17.0 %collective-permute-done.33 = bf16[256,2048]{1,0:T(8,128)(2,1)S(1)} collective-permute-done((bf16[256,2048]{1,0:T(8,128)(2,1)}, bf16[256,2048]{1,0:T(8,128)(2,1)S(1)}, u32[]{:S(2)}, u32[]{:S(2)}) %collective-permute-start.33) | collective-permute-done | bytes 1048608 | tf_op jit(solution)/shard_map/ppermute | solution.py:45
  599.9 5.0 collective-permute-done.35
  606.6 5.6 convolution_convert_fusion.3.g_ref
  612.2 21.1 %attend_backward.1 = (f32[1024,512]{1,0:T(8,128)}, f32[1024,512]{1,0:T(8,128)}, bf16[1024,512]{1,0:T(8,128)(2,1)}) custom-call(bf16[1024,512]{1,0:T(8,128)(2,1)} %get-tuple-element.84.q_ref, bf16[1024,512]{1,0:T(8,128)(2,1)} %get-tuple-element.83.k_ref, bf16[1024,512]{1,0:T(8,128)(2,1)} %copy-done.33, bf16[1024,512]{1,0:T(8,128)(2,1)} %convolution_convert_fusion.3.g_ref, ...), custom_call_target="tpu_custom_call" | custom-call | flops 5368709120 | bytes 8388608 | tf_op jit(solution)/shard_map/attend_backward/pallas_call | solution.py:196
  633.2 4.2 multiply_reduce_fusion
  649.1 5.2 convolution_convert_fusion.1
  661.6 3.8 add_convert_fusion.4
  669.8 5.8 add_convert_fusion.3
  679.6 10.8 %fusion.125 = (bf16[1024,2048]{1,0:T(8,128)(2,1)S(1)}, f32[1024,2048]{1,0:T(8,128)}) fusion(bf16[1024,1536]{1,0:T(8,128)(2,1)S(1)} %pad_maximum_fusion.1, bf16[2048,2048]{1,0:T(8,128)(2,1)} %all-gather.5.cloned.1.call-done), kind=kOutput, calls=%fused_computation.291 | convolution fusion | flops 6444548096 | bytes 22020096 | tf_op jit(solution)/shard_map/dot_general | solution.py:41
  697.0 8.8 collective-permute-done.52
  716.7 3.8 collective-permute-start.43
  734.2 3.7 fusion.17
  737.9 16.3 %reduce-scatter.4.cloned.1.call-done = bf16[256,2048]{1,0:T(8,128)(2,1)} async-done(((bf16[1024,2048]{1,0:T(8,128)(2,1)}), bf16[256,2048]{1,0:T(8,128)(2,1)}) %reduce-scatter.4.cloned.1.call-update) | async-done | bytes 1048592 | tf_op jit(solution)/shard_map/reduce_scatter | solution.py:362
  757.8 143.7 %reduce-scatter.6.cloned.1.call-done = bf16[256,4096]{1,0:T(8,128)(2,1)} async-done(((bf16[1024,4096]{1,0:T(8,128)(2,1)}), bf16[256,4096]{1,0:T(8,128)(2,1)}) %reduce-scatter.6.cloned.1.call-update) | async-done | bytes 2097168 | tf_op jit(solution)/shard_map/reduce_scatter | solution.py:362
  901.5 6.6 reshape.397
  908.1 14.3 %slice_reduce_fusion = (f32[256,8,256]{2,1,0:T(8,128)S(1)}, f32[256,8,256]{2,1,0:T(8,128)S(1)}) fusion(f32[256,8,2,256]{3,2,1,0:T(2,128)} %reshape.397), kind=kLoop, calls=%fused_computation.36 | loop fusion | bytes 8388608 | tf_op jit(solution)/shard_map/slice | solution.py:560
  (533 shorter events, 252.6 us)
Async XLA Ops:
  7.2 91.2 %all-gather.5.cloned.1.call-start = ((), (), s32[]{:S(2)}) async-start(), calls=%async_computation.3 | async-start | bytes 9437184 | tf_op jit(solution)/shard_map/all_gather | solution.py:393
  13.0 242.7 %all-gather.7.cloned.1.call-start = ((), (), s32[]{:S(2)}) async-start(), calls=%async_computation.4 | async-start | bytes 18874368 | tf_op jit(solution)/shard_map/all_gather | solution.py:394
  29.5 302.4 %all-gather.9.cloned.1.call-start = ((), (), s32[]{:S(2)}) async-start(), calls=%async_computation.5 | async-start | bytes 9437184 | tf_op jit(solution)/shard_map/all_gather | solution.py:395
  29.5 26.2 %collective-permute-start = (bf16[256,2048]{1,0:T(8,128)(2,1)S(1)}, bf16[256,2048]{1,0:T(8,128)(2,1)S(1)}, u32[]{:S(2)}, u32[]{:S(2)}) collective-permute-start(bf16[256,2048]{1,0:T(8,128)(2,1)S(1)} %copy-done.31), channel_id=1, source_target_pairs={{0,1},{1,0},{2,3},{3,2},{4,5},{5,4},{6,7},{7,6},{8,9},{9,8},{10,11... | collective-permute-start | bytes 3145736 | tf_op jit(solution)/shard_map/ppermute | solution.py:45
  32.6 40.4 %collective-permute-start.1 = (bf16[256,2048]{1,0:T(8,128)(2,1)S(1)}, bf16[256,2048]{1,0:T(8,128)(2,1)}, u32[]{:S(2)}, u32[]{:S(2)}) collective-permute-start(bf16[256,2048]{1,0:T(8,128)(2,1)S(1)} %copy-done.31), channel_id=1, source_target_pairs={{0,2},{1,3},{2,0},{3,1},{4,6},{5,7},{6,4},{7,5},{8,10},{9,11},{10,... | collective-permute-start | bytes 3145736 | tf_op jit(solution)/shard_map/ppermute | solution.py:45
  34.1 690.5 %reduce-scatter.8.cloned.1.call-start = ((), (), s32[]{:S(2)}) async-start(), calls=%async_computation.8 | async-start | bytes 5242880 | tf_op jit(solution)/shard_map/reduce_scatter | solution.py:362
  56.6 22.5 %collective-permute-start.2 = (bf16[128,2048]{1,0:T(8,128)(2,1)}, bf16[128,2048]{1,0:T(8,128)(2,1)}, u32[]{:S(2)}, u32[]{:S(2)}) collective-permute-start(bf16[128,2048]{1,0:T(8,128)(2,1)} %slice.665), channel_id=1, source_target_pairs={{0,2},{1,3},{2,0},{3,1},{4,6},{5,7},{6,4},{7,5},{8,10},{9,11},{10,... | collective-permute-start | bytes 1572872 | tf_op jit(solution)/shard_map/ppermute | solution.py:45
  74.1 14.2 %collective-permute-start.3 = (bf16[128,2048]{1,0:T(8,128)(2,1)S(1)}, bf16[128,2048]{1,0:T(8,128)(2,1)S(1)}, u32[]{:S(2)}, u32[]{:S(2)}) collective-permute-start(bf16[128,2048]{1,0:T(8,128)(2,1)S(1)} %slice.666), channel_id=1, source_target_pairs={{0,1},{1,0},{2,3},{3,2},{4,5},{5,4},{6,7},{7,6},{8,9},{9,8},{10,11... | collective-permute-start | bytes 1572872 | tf_op jit(solution)/shard_map/ppermute | solution.py:45
  112.2 21.7 %collective-permute-start.5 = (f32[2,4,256]{2,1,0:T(4,128)S(1)}, f32[2,4,256]{2,1,0:T(4,128)S(1)}, u32[]{:S(2)}, u32[]{:S(2)}) collective-permute-start(f32[2,4,256]{2,1,0:T(4,128)S(1)} %constant_dynamic-update-slice_fusion.8), channel_id=1, source_target_pairs={{0,2},{1,3},{2,0},{3,1},{4,6},{5,7},{6,4},{7,5},{8,10},{9,11},{10,... | collective-permute-start | bytes 24584 | tf_op jit(solution)/shard_map/ppermute | solution.py:45
  118.2 15.7 %collective-permute-start.6 = (f32[2,4,256]{2,1,0:T(4,128)S(1)}, f32[2,4,256]{2,1,0:T(4,128)S(1)}, u32[]{:S(2)}, u32[]{:S(2)}) collective-permute-start(f32[2,4,256]{2,1,0:T(4,128)S(1)} %constant_dynamic-update-slice_fusion.8), channel_id=1, source_target_pairs={{0,3},{1,2},{2,1},{3,0},{4,7},{5,6},{6,5},{7,4},{8,11},{9,10},{10,... | collective-permute-start | bytes 24584 | tf_op jit(solution)/shard_map/ppermute | solution.py:45
  119.7 14.3 %collective-permute-start.4 = (f32[2,4,256]{2,1,0:T(4,128)S(1)}, f32[2,4,256]{2,1,0:T(4,128)S(1)}, u32[]{:S(2)}, u32[]{:S(2)}) collective-permute-start(f32[2,4,256]{2,1,0:T(4,128)S(1)} %constant_dynamic-update-slice_fusion.8), channel_id=1, source_target_pairs={{0,1},{1,0},{2,3},{3,2},{4,5},{5,4},{6,7},{7,6},{8,9},{9,8},{10,11... | collective-permute-start | bytes 24584 | tf_op jit(solution)/shard_map/ppermute | solution.py:45
  176.0 13.3 %collective-permute-start.7 = (bf16[128,2048]{1,0:T(8,128)(2,1)S(1)}, bf16[128,2048]{1,0:T(8,128)(2,1)S(1)}, u32[]{:S(2)}, u32[]{:S(2)}) collective-permute-start(bf16[128,2048]{1,0:T(8,128)(2,1)S(1)} %get-tuple-element.128), channel_id=1, source_target_pairs={{0,2},{1,3},{2,0},{3,1},{4,6},{5,7},{6,4},{7,5},{8,10},{9,11},{10,... | collective-permute-start | bytes 1572872 | tf_op jit(solution)/shard_map/ppermute | solution.py:45
  177.5 13.0 %collective-permute-start.9 = (bf16[128,2048]{1,0:T(8,128)(2,1)S(1)}, bf16[128,2048]{1,0:T(8,128)(2,1)S(1)}, u32[]{:S(2)}, u32[]{:S(2)}) collective-permute-start(bf16[128,2048]{1,0:T(8,128)(2,1)S(1)} %get-tuple-element.127), channel_id=1, source_target_pairs={{0,1},{1,0},{2,3},{3,2},{4,5},{5,4},{6,7},{7,6},{8,9},{9,8},{10,11... | collective-permute-start | bytes 1572872 | tf_op jit(solution)/shard_map/ppermute | solution.py:45
  191.0 23.5 %collective-permute-start.10 = (bf16[256,2048]{1,0:T(8,128)(2,1)S(1)}, bf16[256,2048]{1,0:T(8,128)(2,1)S(1)}, u32[]{:S(2)}, u32[]{:S(2)}) collective-permute-start(bf16[256,2048]{1,0:T(8,128)(2,1)S(1)} %pad_maximum_fusion.11), channel_id=1, source_target_pairs={{0,2},{1,3},{2,0},{3,1},{4,6},{5,7},{6,4},{7,5},{8,10},{9,11},{10,... | collective-permute-start | bytes 3145736 | tf_op jit(solution)/shard_map/ppermute | solution.py:45
  191.6 23.3 %collective-permute-start.8 = (bf16[256,2048]{1,0:T(8,128)(2,1)S(1)}, bf16[256,2048]{1,0:T(8,128)(2,1)S(1)}, u32[]{:S(2)}, u32[]{:S(2)}) collective-permute-start(bf16[256,2048]{1,0:T(8,128)(2,1)S(1)} %pad_maximum_fusion.10), channel_id=1, source_target_pairs={{0,1},{1,0},{2,3},{3,2},{4,5},{5,4},{6,7},{7,6},{8,9},{9,8},{10,11... | collective-permute-start | bytes 3145736 | tf_op jit(solution)/shard_map/ppermute | solution.py:45
  217.9 22.5 %collective-permute-start.11 = (bf16[256,2048]{1,0:T(8,128)(2,1)S(1)}, bf16[256,2048]{1,0:T(8,128)(2,1)S(1)}, u32[]{:S(2)}, u32[]{:S(2)}) collective-permute-start(bf16[256,2048]{1,0:T(8,128)(2,1)S(1)} %get-tuple-element.75), channel_id=1, source_target_pairs={{0,1},{1,0},{2,3},{3,2},{4,5},{5,4},{6,7},{7,6},{8,9},{9,8},{10,11... | collective-permute-start | bytes 3145736 | tf_op jit(solution)/shard_map/ppermute | solution.py:45
  219.4 24.0 %collective-permute-start.12 = (bf16[256,2048]{1,0:T(8,128)(2,1)S(1)}, bf16[256,2048]{1,0:T(8,128)(2,1)S(1)}, u32[]{:S(2)}, u32[]{:S(2)}) collective-permute-start(bf16[256,2048]{1,0:T(8,128)(2,1)S(1)} %get-tuple-element.75), channel_id=1, source_target_pairs={{0,2},{1,3},{2,0},{3,1},{4,6},{5,7},{6,4},{7,5},{8,10},{9,11},{10,... | collective-permute-start | bytes 3145736 | tf_op jit(solution)/shard_map/ppermute | solution.py:45
  241.3 11.7 %collective-permute-start.13 = (bf16[128,2048]{1,0:T(8,128)(2,1)}, bf16[128,2048]{1,0:T(8,128)(2,1)}, u32[]{:S(2)}, u32[]{:S(2)}) collective-permute-start(bf16[128,2048]{1,0:T(8,128)(2,1)} %slice.697), channel_id=1, source_target_pairs={{0,2},{1,3},{2,0},{3,1},{4,6},{5,7},{6,4},{7,5},{8,10},{9,11},{10,... | collective-permute-start | bytes 1572872 | tf_op jit(solution)/shard_map/ppermute | solution.py:45
  243.5 11.4 %collective-permute-start.14 = (bf16[128,2048]{1,0:T(8,128)(2,1)S(1)}, bf16[128,2048]{1,0:T(8,128)(2,1)S(1)}, u32[]{:S(2)}, u32[]{:S(2)}) collective-permute-start(bf16[128,2048]{1,0:T(8,128)(2,1)S(1)} %slice.698), channel_id=1, source_target_pairs={{0,1},{1,0},{2,3},{3,2},{4,5},{5,4},{6,7},{7,6},{8,9},{9,8},{10,11... | collective-permute-start | bytes 1572872 | tf_op jit(solution)/shard_map/ppermute | solution.py:45
  338.1 14.9 %collective-permute-start.19 = (bf16[128,2048]{1,0:T(8,128)(2,1)S(1)}, bf16[128,2048]{1,0:T(8,128)(2,1)S(1)}, u32[]{:S(2)}, u32[]{:S(2)}) collective-permute-start(bf16[128,2048]{1,0:T(8,128)(2,1)S(1)} %get-tuple-element.155), channel_id=1, source_target_pairs={{0,1},{1,0},{2,3},{3,2},{4,5},{5,4},{6,7},{7,6},{8,9},{9,8},{10,11... | collective-permute-start | bytes 1572872 | tf_op jit(solution)/shard_map/ppermute | solution.py:45
  339.7 14.8 %collective-permute-start.15 = (bf16[128,2048]{1,0:T(8,128)(2,1)S(1)}, bf16[128,2048]{1,0:T(8,128)(2,1)S(1)}, u32[]{:S(2)}, u32[]{:S(2)}) collective-permute-start(bf16[128,2048]{1,0:T(8,128)(2,1)S(1)} %get-tuple-element.156), channel_id=1, source_target_pairs={{0,2},{1,3},{2,0},{3,1},{4,6},{5,7},{6,4},{7,5},{8,10},{9,11},{10,... | collective-permute-start | bytes 1572872 | tf_op jit(solution)/shard_map/ppermute | solution.py:45
  346.1 34.9 %collective-permute-start.17 = (bf16[128,2048]{1,0:T(8,128)(2,1)S(1)}, bf16[128,2048]{1,0:T(8,128)(2,1)S(1)}, u32[]{:S(2)}, u32[]{:S(2)}) collective-permute-start(bf16[128,2048]{1,0:T(8,128)(2,1)S(1)} %get-tuple-element.138), channel_id=1, source_target_pairs={{0,2},{1,3},{2,0},{3,1},{4,6},{5,7},{6,4},{7,5},{8,10},{9,11},{10,... | collective-permute-start | bytes 1572872 | tf_op jit(solution)/shard_map/ppermute | solution.py:45
  346.7 17.6 %collective-permute-start.18 = (bf16[128,2048]{1,0:T(8,128)(2,1)S(1)}, bf16[128,2048]{1,0:T(8,128)(2,1)S(1)}, u32[]{:S(2)}, u32[]{:S(2)}) collective-permute-start(bf16[128,2048]{1,0:T(8,128)(2,1)S(1)} %get-tuple-element.137), channel_id=1, source_target_pairs={{0,1},{1,0},{2,3},{3,2},{4,5},{5,4},{6,7},{7,6},{8,9},{9,8},{10,11... | collective-permute-start | bytes 1572872 | tf_op jit(solution)/shard_map/ppermute | solution.py:45
  354.8 26.2 %collective-permute-start.16 = (bf16[128,2048]{1,0:T(8,128)(2,1)S(1)}, bf16[128,2048]{1,0:T(8,128)(2,1)S(1)}, u32[]{:S(2)}, u32[]{:S(2)}) collective-permute-start(bf16[128,2048]{1,0:T(8,128)(2,1)S(1)} %get-tuple-element.124), channel_id=1, source_target_pairs={{0,1},{1,0},{2,3},{3,2},{4,5},{5,4},{6,7},{7,6},{8,9},{9,8},{10,11... | collective-permute-start | bytes 1572872 | tf_op jit(solution)/shard_map/ppermute | solution.py:45
  355.4 20.6 %collective-permute-start.20 = (bf16[128,2048]{1,0:T(8,128)(2,1)S(1)}, bf16[128,2048]{1,0:T(8,128)(2,1)S(1)}, u32[]{:S(2)}, u32[]{:S(2)}) collective-permute-start(bf16[128,2048]{1,0:T(8,128)(2,1)S(1)} %get-tuple-element.123), channel_id=1, source_target_pairs={{0,2},{1,3},{2,0},{3,1},{4,6},{5,7},{6,4},{7,5},{8,10},{9,11},{10,... | collective-permute-start | bytes 1572872 | tf_op jit(solution)/shard_map/ppermute | solution.py:45
  380.3 15.1 %collective-permute-start.21 = (bf16[128,2048]{1,0:T(8,128)(2,1)}, bf16[128,2048]{1,0:T(8,128)(2,1)S(1)}, u32[]{:S(2)}, u32[]{:S(2)}) collective-permute-start(bf16[128,2048]{1,0:T(8,128)(2,1)} %get-tuple-element.42), channel_id=1, source_target_pairs={{0,1},{1,0},{2,3},{3,2},{4,5},{5,4},{6,7},{7,6},{8,9},{9,8},{10,11... | collective-permute-start | bytes 1572872 | tf_op jit(solution)/shard_map/ppermute | solution.py:45
  385.8 18.9 %collective-permute-start.22 = (bf16[128,2048]{1,0:T(8,128)(2,1)}, bf16[128,2048]{1,0:T(8,128)(2,1)S(1)}, u32[]{:S(2)}, u32[]{:S(2)}) collective-permute-start(bf16[128,2048]{1,0:T(8,128)(2,1)} %get-tuple-element.43), channel_id=1, source_target_pairs={{0,1},{1,0},{2,3},{3,2},{4,5},{5,4},{6,7},{7,6},{8,9},{9,8},{10,11... | collective-permute-start | bytes 1572872 | tf_op jit(solution)/shard_map/ppermute | solution.py:45
  387.5 17.4 %collective-permute-start.23 = (bf16[128,2048]{1,0:T(8,128)(2,1)S(1)}, bf16[128,2048]{1,0:T(8,128)(2,1)S(1)}, u32[]{:S(2)}, u32[]{:S(2)}) collective-permute-start(bf16[128,2048]{1,0:T(8,128)(2,1)S(1)} %copy-done.77), channel_id=1, source_target_pairs={{0,2},{1,3},{2,0},{3,1},{4,6},{5,7},{6,4},{7,5},{8,10},{9,11},{10,... | collective-permute-start | bytes 1572872 | tf_op jit(solution)/shard_map/ppermute | solution.py:45
  389.0 22.1 %collective-permute-start.24 = (bf16[128,2048]{1,0:T(8,128)(2,1)}, bf16[128,2048]{1,0:T(8,128)(2,1)S(1)}, u32[]{:S(2)}, u32[]{:S(2)}) collective-permute-start(bf16[128,2048]{1,0:T(8,128)(2,1)} %get-tuple-element.43), channel_id=1, source_target_pairs={{0,2},{1,3},{2,0},{3,1},{4,6},{5,7},{6,4},{7,5},{8,10},{9,11},{10,... | collective-permute-start | bytes 1572872 | tf_op jit(solution)/shard_map/ppermute | solution.py:45
  416.9 11.6 %collective-permute-start.25 = (bf16[128,2048]{1,0:T(8,128)(2,1)S(1)}, bf16[128,2048]{1,0:T(8,128)(2,1)S(1)}, u32[]{:S(2)}, u32[]{:S(2)}) collective-permute-start(bf16[128,2048]{1,0:T(8,128)(2,1)S(1)} %collective-permute-done.21), channel_id=1, source_target_pairs={{0,2},{1,3},{2,0},{3,1},{4,6},{5,7},{6,4},{7,5},{8,10},{9,11},{10,... | collective-permute-start | bytes 1572872 | tf_op jit(solution)/shard_map/ppermute | solution.py:45
  481.3 63.8 %collective-permute-start.32 = (bf16[1024,4096]{1,0:T(8,128)(2,1)}, bf16[1024,4096]{1,0:T(8,128)(2,1)}, u32[]{:S(2)}, u32[]{:S(2)}) collective-permute-start(bf16[1024,4096]{1,0:T(8,128)(2,1)} %convolution_convert_fusion), channel_id=1, source_target_pairs={{0,4},{4,0},{8,12},{12,8},{16,20},{20,16},{24,28},{28,24},{1,5},{5... | collective-permute-start | bytes 25165832 | tf_op jit(solution)/shard_map/ppermute | solution.py:343
  502.6 14.3 %collective-permute-start.28 = (bf16[128,2048]{1,0:T(8,128)(2,1)S(1)}, bf16[128,2048]{1,0:T(8,128)(2,1)S(1)}, u32[]{:S(2)}, u32[]{:S(2)}) collective-permute-start(bf16[128,2048]{1,0:T(8,128)(2,1)S(1)} %get-tuple-element.114), channel_id=1, source_target_pairs={{0,2},{1,3},{2,0},{3,1},{4,6},{5,7},{6,4},{7,5},{8,10},{9,11},{10,... | collective-permute-start | bytes 1572872 | tf_op jit(solution)/shard_map/ppermute | solution.py:45
  503.2 13.9 %collective-permute-start.30 = (bf16[128,2048]{1,0:T(8,128)(2,1)S(1)}, bf16[128,2048]{1,0:T(8,128)(2,1)S(1)}, u32[]{:S(2)}, u32[]{:S(2)}) collective-permute-start(bf16[128,2048]{1,0:T(8,128)(2,1)S(1)} %get-tuple-element.113), channel_id=1, source_target_pairs={{0,1},{1,0},{2,3},{3,2},{4,5},{5,4},{6,7},{7,6},{8,9},{9,8},{10,11... | collective-permute-start | bytes 1572872 | tf_op jit(solution)/shard_map/ppermute | solution.py:45
  517.6 24.4 %collective-permute-start.31 = (bf16[256,2048]{1,0:T(8,128)(2,1)S(1)}, bf16[256,2048]{1,0:T(8,128)(2,1)S(1)}, u32[]{:S(2)}, u32[]{:S(2)}) collective-permute-start(bf16[256,2048]{1,0:T(8,128)(2,1)S(1)} %pad_maximum_fusion.13), channel_id=1, source_target_pairs={{0,2},{1,3},{2,0},{3,1},{4,6},{5,7},{6,4},{7,5},{8,10},{9,11},{10,... | collective-permute-start | bytes 3145736 | tf_op jit(solution)/shard_map/ppermute | solution.py:45
  519.2 24.1 %collective-permute-start.29 = (bf16[256,2048]{1,0:T(8,128)(2,1)S(1)}, bf16[256,2048]{1,0:T(8,128)(2,1)S(1)}, u32[]{:S(2)}, u32[]{:S(2)}) collective-permute-start(bf16[256,2048]{1,0:T(8,128)(2,1)S(1)} %pad_maximum_fusion.12), channel_id=1, source_target_pairs={{0,1},{1,0},{2,3},{3,2},{4,5},{5,4},{6,7},{7,6},{8,9},{9,8},{10,11... | collective-permute-start | bytes 3145736 | tf_op jit(solution)/shard_map/ppermute | solution.py:45
  568.7 23.4 %collective-permute-start.33 = (bf16[256,2048]{1,0:T(8,128)(2,1)}, bf16[256,2048]{1,0:T(8,128)(2,1)S(1)}, u32[]{:S(2)}, u32[]{:S(2)}) collective-permute-start(bf16[256,2048]{1,0:T(8,128)(2,1)} %get-tuple-element.72), channel_id=1, source_target_pairs={{0,1},{1,0},{2,3},{3,2},{4,5},{5,4},{6,7},{7,6},{8,9},{9,8},{10,11... | collective-permute-start | bytes 3145736 | tf_op jit(solution)/shard_map/ppermute | solution.py:45
  570.5 24.8 %collective-permute-start.34 = (bf16[256,2048]{1,0:T(8,128)(2,1)}, bf16[256,2048]{1,0:T(8,128)(2,1)S(1)}, u32[]{:S(2)}, u32[]{:S(2)}) collective-permute-start(bf16[256,2048]{1,0:T(8,128)(2,1)} %get-tuple-element.72), channel_id=1, source_target_pairs={{0,2},{1,3},{2,0},{3,1},{4,6},{5,7},{6,4},{7,5},{8,10},{9,11},{10,... | collective-permute-start | bytes 3145736 | tf_op jit(solution)/shard_map/ppermute | solution.py:45
  592.2 12.8 %collective-permute-start.35 = (bf16[128,2048]{1,0:T(8,128)(2,1)S(1)}, bf16[128,2048]{1,0:T(8,128)(2,1)S(1)}, u32[]{:S(2)}, u32[]{:S(2)}) collective-permute-start(bf16[128,2048]{1,0:T(8,128)(2,1)S(1)} %slice.735), channel_id=1, source_target_pairs={{0,2},{1,3},{2,0},{3,1},{4,6},{5,7},{6,4},{7,5},{8,10},{9,11},{10,... | collective-permute-start | bytes 1572872 | tf_op jit(solution)/shard_map/ppermute | solution.py:45
  593.5 160.7 %reduce-scatter.4.cloned.1.call-start = ((), (), s32[]{:S(2)}) async-start(), calls=%async_computation.6 | async-start | bytes 5242880 | tf_op jit(solution)/shard_map/reduce_scatter | solution.py:362
  654.3 14.7 %collective-permute-start.50 = (bf16[1024,1536]{1,0:T(8,128)(2,1)}, bf16[1024,1536]{1,0:T(8,128)(2,1)}, u32[]{:S(2)}, u32[]{:S(2)}) collective-permute-start(bf16[1024,1536]{1,0:T(8,128)(2,1)} %convolution_convert_fusion.1), channel_id=1, source_target_pairs={{0,4},{4,0},{8,12},{12,8},{16,20},{20,16},{24,28},{28,24},{1,5},{5... | collective-permute-start | bytes 9437192 | tf_op jit(solution)/shard_map/ppermute | solution.py:343
  678.2 223.3 %reduce-scatter.6.cloned.1.call-start = ((), (), s32[]{:S(2)}) async-start(), calls=%async_computation.7 | async-start | bytes 10485760 | tf_op jit(solution)/shard_map/reduce_scatter | solution.py:362
  690.5 15.4 %collective-permute-start.52 = (bf16[128,2048]{1,0:T(8,128)(2,1)S(1)}, bf16[128,2048]{1,0:T(8,128)(2,1)S(1)}, u32[]{:S(2)}, u32[]{:S(2)}) collective-permute-start(bf16[128,2048]{1,0:T(8,128)(2,1)S(1)} %get-tuple-element.94), channel_id=1, source_target_pairs={{0,2},{1,3},{2,0},{3,1},{4,6},{5,7},{6,4},{7,5},{8,10},{9,11},{10,... | collective-permute-start | bytes 1572872 | tf_op jit(solution)/shard_map/ppermute | solution.py:45
  691.9 14.8 %collective-permute-start.54 = (bf16[128,2048]{1,0:T(8,128)(2,1)S(1)}, bf16[128,2048]{1,0:T(8,128)(2,1)S(1)}, u32[]{:S(2)}, u32[]{:S(2)}) collective-permute-start(bf16[128,2048]{1,0:T(8,128)(2,1)S(1)} %get-tuple-element.93), channel_id=1, source_target_pairs={{0,1},{1,0},{2,3},{3,2},{4,5},{5,4},{6,7},{7,6},{8,9},{9,8},{10,11... | collective-permute-start | bytes 1572872 | tf_op jit(solution)/shard_map/ppermute | solution.py:45
  693.5 17.9 %collective-permute-start.38 = (f32[8,2048]{1,0:T(8,128)S(1)}, f32[8,2048]{1,0:T(8,128)S(1)}, u32[]{:S(2)}, u32[]{:S(2)}) collective-permute-start(f32[8,2048]{1,0:T(8,128)S(1)} %concatenate.147), channel_id=1, source_target_pairs={{0,2},{1,3},{2,0},{3,1},{4,6},{5,7},{6,4},{7,5},{8,10},{9,11},{10,... | collective-permute-start | bytes 196616 | tf_op jit(solution)/shard_map/ppermute | solution.py:45
  694.2 17.2 %collective-permute-start.39 = (f32[8,2048]{1,0:T(8,128)S(1)}, f32[8,2048]{1,0:T(8,128)S(1)}, u32[]{:S(2)}, u32[]{:S(2)}) collective-permute-start(f32[8,2048]{1,0:T(8,128)S(1)} %concatenate.147), channel_id=1, source_target_pairs={{0,3},{1,2},{2,1},{3,0},{4,7},{5,6},{6,5},{7,4},{8,11},{9,10},{10,... | collective-permute-start | bytes 196616 | tf_op jit(solution)/shard_map/ppermute | solution.py:45
  696.9 14.5 %collective-permute-start.37 = (f32[8,2048]{1,0:T(8,128)S(1)}, f32[8,2048]{1,0:T(8,128)S(1)}, u32[]{:S(2)}, u32[]{:S(2)}) collective-permute-start(f32[8,2048]{1,0:T(8,128)S(1)} %concatenate.147), channel_id=1, source_target_pairs={{0,1},{1,0},{2,3},{3,2},{4,5},{5,4},{6,7},{7,6},{8,9},{9,8},{10,11... | collective-permute-start | bytes 196616 | tf_op jit(solution)/shard_map/ppermute | solution.py:45
  709.6 23.2 %collective-permute-start.55 = (bf16[256,2048]{1,0:T(8,128)(2,1)}, bf16[256,2048]{1,0:T(8,128)(2,1)}, u32[]{:S(2)}, u32[]{:S(2)}) collective-permute-start(bf16[256,2048]{1,0:T(8,128)(2,1)} %pad_maximum_fusion.15), channel_id=1, source_target_pairs={{0,2},{1,3},{2,0},{3,1},{4,6},{5,7},{6,4},{7,5},{8,10},{9,11},{10,... | collective-permute-start | bytes 3145736 | tf_op jit(solution)/shard_map/ppermute | solution.py:45
  711.3 22.9 %collective-permute-start.53 = (bf16[256,2048]{1,0:T(8,128)(2,1)}, bf16[256,2048]{1,0:T(8,128)(2,1)S(1)}, u32[]{:S(2)}, u32[]{:S(2)}) collective-permute-start(bf16[256,2048]{1,0:T(8,128)(2,1)} %pad_maximum_fusion.14), channel_id=1, source_target_pairs={{0,1},{1,0},{2,3},{3,2},{4,5},{5,4},{6,7},{7,6},{8,9},{9,8},{10,11... | collective-permute-start | bytes 3145736 | tf_op jit(solution)/shard_map/ppermute | solution.py:45
  (133 other events, 1080.6 us)
Sparse Core Ops, SparseCore 0:
  13.1 85.1 all-gather.4
  100.0 149.5 all-gather.6
  251.2 80.6 all-gather.8
  593.6 74.9 reduce-scatter.7
  678.3 75.8 reduce-scatter.3
  756.4 145.0 reduce-scatter.5

commit v4 on v3

--- a/solution.py
+++ b/solution.py
@@ -155,6 +155,25 @@
 
 def turn_back(grad, cosine, sine):
     return grad * cosine + pltpu.roll(grad * sine, HD // 2, 1)
+
+
+def join_attention(wq, wk, wv, wo):
+    share, width = wq.shape
+    side = wo.shape[1]
+
+    def body(q_ref, k_ref, v_ref, o_ref, out_ref):
+        for i, ref in enumerate((q_ref, k_ref, v_ref)):
+            out_ref[:, i * width : (i + 1) * width] = ref[...]
+        for i in range(wo.shape[0] // share):
+            start = 3 * width + i * side
+            out_ref[:, start : start + side] = o_ref[i * share : (i + 1) * share, :]
+
+    return pl.pallas_call(
+        body,
+        out_shape=jax.ShapeDtypeStruct((share, 3 * width + wo.size // share), BF),
+        cost_estimate=cost(0, wq, wk, wv, wo, wq, wk, wv, wo),
+        name="join_attention",
+    )(wq, wk, wv, wo)
 
 
 def attend_backward(query, key, value, grad_mixed, logsum, bias, cosine, sine, block=512):
@@ -388,8 +407,7 @@
     assert group == LEN and rows * tensor == group
 
     pieces = local_width // share
-    wo_side = jnp.concatenate([wo[i * share : (i + 1) * share] for i in range(pieces)], axis=1)
-    attn_shard = jnp.concatenate([wq, wk, wv, wo_side], axis=1)
+    attn_shard = join_attention(wq, wk, wv, wo)
     attn_all = lax.all_gather(attn_shard, "dp", axis=0, tiled=True)
     pair_all = lax.all_gather(interleave(wg, wu, BLOCK), "dp", axis=0, tiled=True)
     full_down = lax.all_gather(wd, "dp", axis=1, tiled=True)

time: 943 us -> 940 us (level)
    unnamed x285 -> x279, local copies, waits for them, and re-layouts: 64.3 us -> 59.5 us
where the time goes in v4:
time: 940 us; the launch traced here: 932 us
  waiting for transfers between devices  432 us (46%)
  matrix products  150 us (16%)
  local copies, waits for them, and re-layouts  122 us (13%)
  Pallas kernels  73.7 us (8%)
  other arithmetic  60.2 us (6%)
  starting transfers between devices  60 us (6%)
  between operations  19.7 us (2%)
  blocking collectives  14.8 us (2%)
    ppermute x45, waiting for transfers between devices, hop(): return lax.ppermute(value, 'tensor', [(i, i ^ way) for i in range(size)])  200 us
    reduce_scatter x3, waiting for transfers between devices, scatter_pairs(): lax.psum_scatter(value, 'dp', scatter_dimension=axis, axis_index_groups=g...  160 us
    dot_general x10, matrix products, inner_rows(): lax.dot_general(left, right, (((0,), (0,)), ((), ())), preferred_element_...  64.5 us
    unnamed x279, local copies, waits for them, and re-layouts  59.5 us
    ppermute x45, starting transfers between devices, hop(): return lax.ppermute(value, 'tensor', [(i, i ^ way) for i in range(size)])  51.8 us
    all_gather x1, waiting for transfers between devices, layer(): full_down = lax.all_gather(wd, 'dp', axis=1, tiled=True)  49.5 us
    dot_general x3, matrix products, times_transposed(): lax.dot_general(left, right, (((1,), (1,)), ((), ())), preferred_element_...  36.7 us
    dot_general x5, matrix products, times(): return jnp.dot(left, right, preferred_element_type=F32)  26.7 us
  transfers between devices with their start and end apart: 62, of which 38 were waited for; matrix products, arithmetic and copies ran while one was open for 24% of the time, Pallas kernels for 6%

profile of v4, /device:TPU:0, one launch (start us, length us, event | category | flops | bytes accessed | tf_op | source)
XLA Modules:
  0.0 932.1 jit_solution(5900971997281114423)
XLA Ops:
  39.5 12.7 %collective-permute-done = bf16[256,2048]{1,0:T(8,128)(2,1)S(1)} collective-permute-done((bf16[256,2048]{1,0:T(8,128)(2,1)S(1)}, bf16[256,2048]{1,0:T(8,128)(2,1)S(1)}, u32[]{:S(2)}, u32[]{:S(2)}) %collective-permute-start) | collective-permute-done | bytes 1048608 | tf_op jit(solution)/shard_map/ppermute | solution.py:45
  54.8 14.8 %all-gather = f32[8,2048]{1,0:T(8,128)S(1)} all-gather(f32[8,256]{1,0:T(8,128)S(1)} %concatenate.120), channel_id=2, replica_groups=mesh['dp'=8,'tensor'=4] {'dp'}, dimensions={1}, use_global_device_ids=true | all-gather | bytes 73728 | tf_op jit(solution)/shard_map/all_gather | solution.py:422
  77.7 7.3 collective-permute-done.3
  85.9 9.5 %all-gather.5.cloned.1.call-done = bf16[2048,2048]{1,0:T(8,128)(2,1)} async-done(((bf16[256,2048]{1,0:T(8,128)(2,1)}), bf16[2048,2048]{1,0:T(8,128)(2,1)}) %all-gather.5.cloned.1.call-update) | async-done | bytes 8388624 | tf_op jit(solution)/shard_map/all_gather | solution.py:411
  95.4 10.0 %fusion.5 = f32[1024,1536]{1,0:T(8,128)S(1)} fusion(bf16[1024,2048]{1,0:T(8,128)(2,1)} %constant_dynamic-update-slice_fusion, bf16[2048,2048]{1,0:T(8,128)(2,1)} %all-gather.5.cloned.1.call-done), kind=kOutput, calls=%fused_computation.15 | convolution fusion | flops 6442450944 | bytes 16777216 | tf_op jit(solution)/shard_map/dot_general | solution.py:37
  121.6 4.3 reshape.386
  137.2 14.6 %fusion = (f32[4,1024]{1,0:T(4,128)S(1)}, f32[4,1024,1024]{1,2,0:T(8,128)}) fusion(pred[1024,1024]{0,1:T(8,128)(4,1)} %copy.62, f32[1024,128]{1,0:T(8,128)} %get-tuple-element.178.c_ref.cq_ref, f32[1024,128]{1,0:T(8,128)} %get-tuple-element.177, f32[1024,4,64]{2,0,1:T(8,128)S(1)} %get-tuple-element.142, f32[1024,4,64]{2,0,1:T(8,128)S(1)} %get-tuple-element.141, ...), kind=kOutput, calls=%fused_computation.6 | convolution fusion | flops 1091563520 | bytes 27279360 | tf_op jit(solution)/shard_map/qhd,khd->hqk/dot_general | solution.py:135
  151.8 8.7 fusion.1
  163.4 7.0 fusion.45
  176.0 10.2 %collective-permute-done.7 = bf16[128,2048]{1,0:T(8,128)(2,1)S(1)} collective-permute-done((bf16[128,2048]{1,0:T(8,128)(2,1)S(1)}, bf16[128,2048]{1,0:T(8,128)(2,1)S(1)}, u32[]{:S(2)}, u32[]{:S(2)}) %collective-permute-start.7) | collective-permute-done | bytes 524320 | tf_op jit(solution)/shard_map/ppermute | solution.py:45
  190.8 20.7 %collective-permute-done.10 = bf16[256,2048]{1,0:T(8,128)(2,1)S(1)} collective-permute-done((bf16[256,2048]{1,0:T(8,128)(2,1)S(1)}, bf16[256,2048]{1,0:T(8,128)(2,1)S(1)}, u32[]{:S(2)}, u32[]{:S(2)}) %collective-permute-start.10) | collective-permute-done | bytes 1048608 | tf_op jit(solution)/shard_map/ppermute | solution.py:45
  219.4 18.2 %collective-permute-done.11 = bf16[256,2048]{1,0:T(8,128)(2,1)S(1)} collective-permute-done((bf16[256,2048]{1,0:T(8,128)(2,1)S(1)}, bf16[256,2048]{1,0:T(8,128)(2,1)S(1)}, u32[]{:S(2)}, u32[]{:S(2)}) %collective-permute-start.11) | collective-permute-done | bytes 1048608 | tf_op jit(solution)/shard_map/ppermute | solution.py:45
  244.3 5.7 collective-permute-done.13
  252.8 24.7 %pair_forward.1 = (f32[1024,4096]{1,0:T(8,128)}, bf16[1024,2048]{1,0:T(8,128)(2,1)S(1)}) custom-call(bf16[1024,2048]{1,0:T(8,128)(2,1)} %constant_dynamic-update-slice_fusion.7.x_ref, bf16[2048,4096]{1,0:T(8,128)(2,1)} %all-gather.7.cloned.1.call-done.w_ref), custom_call_target="tpu_custom_call" | custom-call | flops 17179869184 | bytes 20971520 | tf_op jit(solution)/shard_map/pair_forward/pallas_call | solution.py:330
  279.4 49.5 %all-gather.9.cloned.1.call-done.w_ref = bf16[2048,2048]{1,0:T(8,128)(2,1)} async-done(((bf16[2048,256]{1,0:T(8,128)(2,1)}), bf16[2048,2048]{1,0:T(8,128)(2,1)}) %all-gather.9.cloned.1.call-update) | async-done | bytes 8388624 | tf_op jit(solution)/shard_map/all_gather | solution.py:413
  328.9 6.2 convolution_convert_fusion.2
  338.2 4.5 fusion.33
  344.3 5.8 collective-permute-done.19
  357.5 3.7 collective-permute-done.18.refs_5_
  361.3 11.7 %collective-permute-done.20.refs_6_ = bf16[128,2048]{1,0:T(8,128)(2,1)S(1)} collective-permute-done((bf16[128,2048]{1,0:T(8,128)(2,1)S(1)}, bf16[128,2048]{1,0:T(8,128)(2,1)S(1)}, u32[]{:S(2)}, u32[]{:S(2)}) %collective-permute-start.20) | collective-permute-done | bytes 524320 | tf_op jit(solution)/shard_map/ppermute | solution.py:45
  378.9 3.9 loss_and_back.3
  387.7 4.7 collective-permute-done.21
  392.5 9.3 collective-permute-done.22
  402.0 6.2 collective-permute-done.24
  419.5 6.0 collective-permute-done.25
  433.4 4.2 collective-permute-done.27
  443.4 18.3 %pair_backward.1 = bf16[1024,4096]{1,0:T(8,128)(2,1)} custom-call(bf16[1024,2048]{1,0:T(8,128)(2,1)S(1)} %copy-done.1, bf16[2048,2048]{1,0:T(8,128)(2,1)} %all-gather.9.cloned.1.call-done.w_ref, f32[1024,4096]{1,0:T(8,128)} %get-tuple-element.47.p_ref), custom_call_target="tpu_custom_call" | custom-call | flops 8589934592 | bytes 29360128 | tf_op jit(solution)/shard_map/pair_backward/pallas_call | solution.py:248
  461.7 16.6 %convolution_convert_fusion = bf16[1024,4096]{1,0:T(8,128)(2,1)} fusion(bf16[1024,4096]{1,0:T(8,128)(2,1)} %pair_backward.1, pred[]{:T(512)S(6)} %eq.43, bf16[1024,256]{1,0:T(8,128)(2,1)S(1)} %copy-done.66, bf16[1024,256]{1,0:T(8,128)(2,1)S(1)} %copy-done.67, bf16[1024,256]{1,0:T(8,128)(2,1)S(1)} %copy-done.68, bf16[1024,256]{1,0:T(8,128)(2,1)S(1)} %copy-done.69, ...), kind=kOutput, calls=%fused_computation.11 | convolution fusion | flops 8611954688 | bytes 20971520 | tf_op jit(solution)/shard_map/dot_general | solution.py:33
  478.4 20.3 %fusion.126 = f32[1024,2048]{1,0:T(8,128)S(1)} fusion(bf16[1024,4096]{1,0:T(8,128)(2,1)S(1)} %copy-done.28, bf16[2048,4096]{1,0:T(8,128)(2,1)} %all-gather.7.cloned.1.call-done.w_ref), kind=kOutput, calls=%fused_computation.287 | convolution fusion | flops 17179869184 | bytes 33554432 | tf_op jit(solution)/shard_map/dot_general | solution.py:41
  500.8 13.1 %collective-permute-done.28 = bf16[128,2048]{1,0:T(8,128)(2,1)S(1)} collective-permute-done((bf16[128,2048]{1,0:T(8,128)(2,1)S(1)}, bf16[128,2048]{1,0:T(8,128)(2,1)S(1)}, u32[]{:S(2)}, u32[]{:S(2)}) %collective-permute-start.28) | collective-permute-done | bytes 524320 | tf_op jit(solution)/shard_map/ppermute | solution.py:45
  521.9 17.2 %collective-permute-done.31 = bf16[256,2048]{1,0:T(8,128)(2,1)S(1)} collective-permute-done((bf16[256,2048]{1,0:T(8,128)(2,1)S(1)}, bf16[256,2048]{1,0:T(8,128)(2,1)S(1)}, u32[]{:S(2)}, u32[]{:S(2)}) %collective-permute-start.31) | collective-permute-done | bytes 1048608 | tf_op jit(solution)/shard_map/ppermute | solution.py:45
  542.2 18.3 %add_convert_fusion = bf16[1024,4096]{1,0:T(8,128)(2,1)} fusion(bf16[1024,4096]{1,0:T(8,128)(2,1)} %collective-permute-done.32, bf16[1024,4096]{1,0:T(8,128)(2,1)} %pair_backward.1, pred[]{:T(512)S(6)} %eq.43, bf16[1024,256]{1,0:T(8,128)(2,1)S(1)} %copy-done.66, bf16[1024,256]{1,0:T(8,128)(2,1)S(1)} %copy-done.67, bf16[1024,256]{1,0:T(8,128)(2,1)S(1)} %copy-done.68, ...), kind=kOutput, calls=%fused_computation.2 | convolution fusion | flops 8620343296 | bytes 29360128 | tf_op jit(solution)/shard_map/dot_general | solution.py:33
  572.2 17.0 %collective-permute-done.33 = bf16[256,2048]{1,0:T(8,128)(2,1)S(1)} collective-permute-done((bf16[256,2048]{1,0:T(8,128)(2,1)}, bf16[256,2048]{1,0:T(8,128)(2,1)S(1)}, u32[]{:S(2)}, u32[]{:S(2)}) %collective-permute-start.33) | collective-permute-done | bytes 1048608 | tf_op jit(solution)/shard_map/ppermute | solution.py:45
  597.0 5.0 collective-permute-done.35
  603.7 5.6 convolution_convert_fusion.3.g_ref
  609.3 21.0 %attend_backward.1 = (f32[1024,512]{1,0:T(8,128)}, f32[1024,512]{1,0:T(8,128)}, bf16[1024,512]{1,0:T(8,128)(2,1)}) custom-call(bf16[1024,512]{1,0:T(8,128)(2,1)} %get-tuple-element.84.q_ref, bf16[1024,512]{1,0:T(8,128)(2,1)} %get-tuple-element.83.k_ref, bf16[1024,512]{1,0:T(8,128)(2,1)} %copy-done.33, bf16[1024,512]{1,0:T(8,128)(2,1)} %convolution_convert_fusion.3.g_ref, ...), custom_call_target="tpu_custom_call" | custom-call | flops 5368709120 | bytes 8388608 | tf_op jit(solution)/shard_map/attend_backward/pallas_call | solution.py:215
  630.3 4.2 multiply_reduce_fusion
  646.2 5.2 convolution_convert_fusion.1
  658.7 3.8 add_convert_fusion.4
  666.9 5.8 add_convert_fusion.3
  676.7 10.8 %fusion.125 = (bf16[1024,2048]{1,0:T(8,128)(2,1)S(1)}, f32[1024,2048]{1,0:T(8,128)}) fusion(bf16[1024,1536]{1,0:T(8,128)(2,1)S(1)} %pad_maximum_fusion.1, bf16[2048,2048]{1,0:T(8,128)(2,1)} %all-gather.5.cloned.1.call-done), kind=kOutput, calls=%fused_computation.286 | convolution fusion | flops 6444548096 | bytes 22020096 | tf_op jit(solution)/shard_map/dot_general | solution.py:41
  694.2 8.8 collective-permute-done.52
  726.2 3.8 collective-permute-done.55
  731.3 3.7 fusion.17
  735.1 16.1 %reduce-scatter.4.cloned.1.call-done = bf16[256,2048]{1,0:T(8,128)(2,1)} async-done(((bf16[1024,2048]{1,0:T(8,128)(2,1)}), bf16[256,2048]{1,0:T(8,128)(2,1)}) %reduce-scatter.4.cloned.1.call-update) | async-done | bytes 1048592 | tf_op jit(solution)/shard_map/reduce_scatter | solution.py:381
  754.8 143.7 %reduce-scatter.6.cloned.1.call-done = bf16[256,4096]{1,0:T(8,128)(2,1)} async-done(((bf16[1024,4096]{1,0:T(8,128)(2,1)}), bf16[256,4096]{1,0:T(8,128)(2,1)}) %reduce-scatter.6.cloned.1.call-update) | async-done | bytes 2097168 | tf_op jit(solution)/shard_map/reduce_scatter | solution.py:381
  898.5 6.6 reshape.397
  905.1 14.3 %slice_reduce_fusion = (f32[256,8,256]{2,1,0:T(8,128)S(1)}, f32[256,8,256]{2,1,0:T(8,128)S(1)}) fusion(f32[256,8,2,256]{3,2,1,0:T(2,128)} %reshape.397), kind=kLoop, calls=%fused_computation.36 | loop fusion | bytes 8388608 | tf_op jit(solution)/shard_map/slice | solution.py:578
  (527 shorter events, 249.1 us)
Async XLA Ops:
  7.2 88.2 %all-gather.5.cloned.1.call-start = ((), (), s32[]{:S(2)}) async-start(), calls=%async_computation.3 | async-start | bytes 9437184 | tf_op jit(solution)/shard_map/all_gather | solution.py:411
  9.5 243.3 %all-gather.7.cloned.1.call-start = ((), (), s32[]{:S(2)}) async-start(), calls=%async_computation.4 | async-start | bytes 18874368 | tf_op jit(solution)/shard_map/all_gather | solution.py:412
  26.0 302.9 %all-gather.9.cloned.1.call-start = ((), (), s32[]{:S(2)}) async-start(), calls=%async_computation.5 | async-start | bytes 9437184 | tf_op jit(solution)/shard_map/all_gather | solution.py:413
  26.0 26.2 %collective-permute-start = (bf16[256,2048]{1,0:T(8,128)(2,1)S(1)}, bf16[256,2048]{1,0:T(8,128)(2,1)S(1)}, u32[]{:S(2)}, u32[]{:S(2)}) collective-permute-start(bf16[256,2048]{1,0:T(8,128)(2,1)S(1)} %copy-done.31), channel_id=1, source_target_pairs={{0,1},{1,0},{2,3},{3,2},{4,5},{5,4},{6,7},{7,6},{8,9},{9,8},{10,11... | collective-permute-start | bytes 3145736 | tf_op jit(solution)/shard_map/ppermute | solution.py:45
  29.1 40.6 %collective-permute-start.1 = (bf16[256,2048]{1,0:T(8,128)(2,1)S(1)}, bf16[256,2048]{1,0:T(8,128)(2,1)}, u32[]{:S(2)}, u32[]{:S(2)}) collective-permute-start(bf16[256,2048]{1,0:T(8,128)(2,1)S(1)} %copy-done.31), channel_id=1, source_target_pairs={{0,2},{1,3},{2,0},{3,1},{4,6},{5,7},{6,4},{7,5},{8,10},{9,11},{10,... | collective-permute-start | bytes 3145736 | tf_op jit(solution)/shard_map/ppermute | solution.py:45
  30.6 691.0 %reduce-scatter.8.cloned.1.call-start = ((), (), s32[]{:S(2)}) async-start(), calls=%async_computation.8 | async-start | bytes 5242880 | tf_op jit(solution)/shard_map/reduce_scatter | solution.py:381
  53.1 22.7 %collective-permute-start.2 = (bf16[128,2048]{1,0:T(8,128)(2,1)}, bf16[128,2048]{1,0:T(8,128)(2,1)}, u32[]{:S(2)}, u32[]{:S(2)}) collective-permute-start(bf16[128,2048]{1,0:T(8,128)(2,1)} %slice.657), channel_id=1, source_target_pairs={{0,2},{1,3},{2,0},{3,1},{4,6},{5,7},{6,4},{7,5},{8,10},{9,11},{10,... | collective-permute-start | bytes 1572872 | tf_op jit(solution)/shard_map/ppermute | solution.py:45
  70.8 14.2 %collective-permute-start.3 = (bf16[128,2048]{1,0:T(8,128)(2,1)S(1)}, bf16[128,2048]{1,0:T(8,128)(2,1)S(1)}, u32[]{:S(2)}, u32[]{:S(2)}) collective-permute-start(bf16[128,2048]{1,0:T(8,128)(2,1)S(1)} %slice.658), channel_id=1, source_target_pairs={{0,1},{1,0},{2,3},{3,2},{4,5},{5,4},{6,7},{7,6},{8,9},{9,8},{10,11... | collective-permute-start | bytes 1572872 | tf_op jit(solution)/shard_map/ppermute | solution.py:45
  109.2 21.7 %collective-permute-start.5 = (f32[2,4,256]{2,1,0:T(4,128)S(1)}, f32[2,4,256]{2,1,0:T(4,128)S(1)}, u32[]{:S(2)}, u32[]{:S(2)}) collective-permute-start(f32[2,4,256]{2,1,0:T(4,128)S(1)} %constant_dynamic-update-slice_fusion.5), channel_id=1, source_target_pairs={{0,2},{1,3},{2,0},{3,1},{4,6},{5,7},{6,4},{7,5},{8,10},{9,11},{10,... | collective-permute-start | bytes 24584 | tf_op jit(solution)/shard_map/ppermute | solution.py:45
  115.3 15.7 %collective-permute-start.6 = (f32[2,4,256]{2,1,0:T(4,128)S(1)}, f32[2,4,256]{2,1,0:T(4,128)S(1)}, u32[]{:S(2)}, u32[]{:S(2)}) collective-permute-start(f32[2,4,256]{2,1,0:T(4,128)S(1)} %constant_dynamic-update-slice_fusion.5), channel_id=1, source_target_pairs={{0,3},{1,2},{2,1},{3,0},{4,7},{5,6},{6,5},{7,4},{8,11},{9,10},{10,... | collective-permute-start | bytes 24584 | tf_op jit(solution)/shard_map/ppermute | solution.py:45
  116.8 14.3 %collective-permute-start.4 = (f32[2,4,256]{2,1,0:T(4,128)S(1)}, f32[2,4,256]{2,1,0:T(4,128)S(1)}, u32[]{:S(2)}, u32[]{:S(2)}) collective-permute-start(f32[2,4,256]{2,1,0:T(4,128)S(1)} %constant_dynamic-update-slice_fusion.5), channel_id=1, source_target_pairs={{0,1},{1,0},{2,3},{3,2},{4,5},{5,4},{6,7},{7,6},{8,9},{9,8},{10,11... | collective-permute-start | bytes 24584 | tf_op jit(solution)/shard_map/ppermute | solution.py:45
  173.0 13.3 %collective-permute-start.7 = (bf16[128,2048]{1,0:T(8,128)(2,1)S(1)}, bf16[128,2048]{1,0:T(8,128)(2,1)S(1)}, u32[]{:S(2)}, u32[]{:S(2)}) collective-permute-start(bf16[128,2048]{1,0:T(8,128)(2,1)S(1)} %get-tuple-element.128), channel_id=1, source_target_pairs={{0,2},{1,3},{2,0},{3,1},{4,6},{5,7},{6,4},{7,5},{8,10},{9,11},{10,... | collective-permute-start | bytes 1572872 | tf_op jit(solution)/shard_map/ppermute | solution.py:45
  174.6 13.0 %collective-permute-start.9 = (bf16[128,2048]{1,0:T(8,128)(2,1)S(1)}, bf16[128,2048]{1,0:T(8,128)(2,1)S(1)}, u32[]{:S(2)}, u32[]{:S(2)}) collective-permute-start(bf16[128,2048]{1,0:T(8,128)(2,1)S(1)} %get-tuple-element.127), channel_id=1, source_target_pairs={{0,1},{1,0},{2,3},{3,2},{4,5},{5,4},{6,7},{7,6},{8,9},{9,8},{10,11... | collective-permute-start | bytes 1572872 | tf_op jit(solution)/shard_map/ppermute | solution.py:45
  188.0 23.5 %collective-permute-start.10 = (bf16[256,2048]{1,0:T(8,128)(2,1)S(1)}, bf16[256,2048]{1,0:T(8,128)(2,1)S(1)}, u32[]{:S(2)}, u32[]{:S(2)}) collective-permute-start(bf16[256,2048]{1,0:T(8,128)(2,1)S(1)} %pad_maximum_fusion.11), channel_id=1, source_target_pairs={{0,2},{1,3},{2,0},{3,1},{4,6},{5,7},{6,4},{7,5},{8,10},{9,11},{10,... | collective-permute-start | bytes 3145736 | tf_op jit(solution)/shard_map/ppermute | solution.py:45
  188.6 23.4 %collective-permute-start.8 = (bf16[256,2048]{1,0:T(8,128)(2,1)S(1)}, bf16[256,2048]{1,0:T(8,128)(2,1)S(1)}, u32[]{:S(2)}, u32[]{:S(2)}) collective-permute-start(bf16[256,2048]{1,0:T(8,128)(2,1)S(1)} %pad_maximum_fusion.10), channel_id=1, source_target_pairs={{0,1},{1,0},{2,3},{3,2},{4,5},{5,4},{6,7},{7,6},{8,9},{9,8},{10,11... | collective-permute-start | bytes 3145736 | tf_op jit(solution)/shard_map/ppermute | solution.py:45
  215.0 22.5 %collective-permute-start.11 = (bf16[256,2048]{1,0:T(8,128)(2,1)S(1)}, bf16[256,2048]{1,0:T(8,128)(2,1)S(1)}, u32[]{:S(2)}, u32[]{:S(2)}) collective-permute-start(bf16[256,2048]{1,0:T(8,128)(2,1)S(1)} %get-tuple-element.75), channel_id=1, source_target_pairs={{0,1},{1,0},{2,3},{3,2},{4,5},{5,4},{6,7},{7,6},{8,9},{9,8},{10,11... | collective-permute-start | bytes 3145736 | tf_op jit(solution)/shard_map/ppermute | solution.py:45
  216.5 24.1 %collective-permute-start.12 = (bf16[256,2048]{1,0:T(8,128)(2,1)S(1)}, bf16[256,2048]{1,0:T(8,128)(2,1)S(1)}, u32[]{:S(2)}, u32[]{:S(2)}) collective-permute-start(bf16[256,2048]{1,0:T(8,128)(2,1)S(1)} %get-tuple-element.75), channel_id=1, source_target_pairs={{0,2},{1,3},{2,0},{3,1},{4,6},{5,7},{6,4},{7,5},{8,10},{9,11},{10,... | collective-permute-start | bytes 3145736 | tf_op jit(solution)/shard_map/ppermute | solution.py:45
  238.4 11.7 %collective-permute-start.13 = (bf16[128,2048]{1,0:T(8,128)(2,1)}, bf16[128,2048]{1,0:T(8,128)(2,1)}, u32[]{:S(2)}, u32[]{:S(2)}) collective-permute-start(bf16[128,2048]{1,0:T(8,128)(2,1)} %slice.689), channel_id=1, source_target_pairs={{0,2},{1,3},{2,0},{3,1},{4,6},{5,7},{6,4},{7,5},{8,10},{9,11},{10,... | collective-permute-start | bytes 1572872 | tf_op jit(solution)/shard_map/ppermute | solution.py:45
  240.6 11.4 %collective-permute-start.14 = (bf16[128,2048]{1,0:T(8,128)(2,1)S(1)}, bf16[128,2048]{1,0:T(8,128)(2,1)S(1)}, u32[]{:S(2)}, u32[]{:S(2)}) collective-permute-start(bf16[128,2048]{1,0:T(8,128)(2,1)S(1)} %slice.690), channel_id=1, source_target_pairs={{0,1},{1,0},{2,3},{3,2},{4,5},{5,4},{6,7},{7,6},{8,9},{9,8},{10,11... | collective-permute-start | bytes 1572872 | tf_op jit(solution)/shard_map/ppermute | solution.py:45
  335.2 14.9 %collective-permute-start.19 = (bf16[128,2048]{1,0:T(8,128)(2,1)S(1)}, bf16[128,2048]{1,0:T(8,128)(2,1)S(1)}, u32[]{:S(2)}, u32[]{:S(2)}) collective-permute-start(bf16[128,2048]{1,0:T(8,128)(2,1)S(1)} %get-tuple-element.155), channel_id=1, source_target_pairs={{0,1},{1,0},{2,3},{3,2},{4,5},{5,4},{6,7},{7,6},{8,9},{9,8},{10,11... | collective-permute-start | bytes 1572872 | tf_op jit(solution)/shard_map/ppermute | solution.py:45
  336.7 14.8 %collective-permute-start.15 = (bf16[128,2048]{1,0:T(8,128)(2,1)S(1)}, bf16[128,2048]{1,0:T(8,128)(2,1)S(1)}, u32[]{:S(2)}, u32[]{:S(2)}) collective-permute-start(bf16[128,2048]{1,0:T(8,128)(2,1)S(1)} %get-tuple-element.156), channel_id=1, source_target_pairs={{0,2},{1,3},{2,0},{3,1},{4,6},{5,7},{6,4},{7,5},{8,10},{9,11},{10,... | collective-permute-start | bytes 1572872 | tf_op jit(solution)/shard_map/ppermute | solution.py:45
  343.1 34.9 %collective-permute-start.17 = (bf16[128,2048]{1,0:T(8,128)(2,1)S(1)}, bf16[128,2048]{1,0:T(8,128)(2,1)S(1)}, u32[]{:S(2)}, u32[]{:S(2)}) collective-permute-start(bf16[128,2048]{1,0:T(8,128)(2,1)S(1)} %get-tuple-element.138), channel_id=1, source_target_pairs={{0,2},{1,3},{2,0},{3,1},{4,6},{5,7},{6,4},{7,5},{8,10},{9,11},{10,... | collective-permute-start | bytes 1572872 | tf_op jit(solution)/shard_map/ppermute | solution.py:45
  343.7 17.6 %collective-permute-start.18 = (bf16[128,2048]{1,0:T(8,128)(2,1)S(1)}, bf16[128,2048]{1,0:T(8,128)(2,1)S(1)}, u32[]{:S(2)}, u32[]{:S(2)}) collective-permute-start(bf16[128,2048]{1,0:T(8,128)(2,1)S(1)} %get-tuple-element.137), channel_id=1, source_target_pairs={{0,1},{1,0},{2,3},{3,2},{4,5},{5,4},{6,7},{7,6},{8,9},{9,8},{10,11... | collective-permute-start | bytes 1572872 | tf_op jit(solution)/shard_map/ppermute | solution.py:45
  351.8 26.2 %collective-permute-start.16 = (bf16[128,2048]{1,0:T(8,128)(2,1)S(1)}, bf16[128,2048]{1,0:T(8,128)(2,1)S(1)}, u32[]{:S(2)}, u32[]{:S(2)}) collective-permute-start(bf16[128,2048]{1,0:T(8,128)(2,1)S(1)} %get-tuple-element.124), channel_id=1, source_target_pairs={{0,1},{1,0},{2,3},{3,2},{4,5},{5,4},{6,7},{7,6},{8,9},{9,8},{10,11... | collective-permute-start | bytes 1572872 | tf_op jit(solution)/shard_map/ppermute | solution.py:45
  352.4 20.6 %collective-permute-start.20 = (bf16[128,2048]{1,0:T(8,128)(2,1)S(1)}, bf16[128,2048]{1,0:T(8,128)(2,1)S(1)}, u32[]{:S(2)}, u32[]{:S(2)}) collective-permute-start(bf16[128,2048]{1,0:T(8,128)(2,1)S(1)} %get-tuple-element.123), channel_id=1, source_target_pairs={{0,2},{1,3},{2,0},{3,1},{4,6},{5,7},{6,4},{7,5},{8,10},{9,11},{10,... | collective-permute-start | bytes 1572872 | tf_op jit(solution)/shard_map/ppermute | solution.py:45
  377.3 15.1 %collective-permute-start.21 = (bf16[128,2048]{1,0:T(8,128)(2,1)}, bf16[128,2048]{1,0:T(8,128)(2,1)S(1)}, u32[]{:S(2)}, u32[]{:S(2)}) collective-permute-start(bf16[128,2048]{1,0:T(8,128)(2,1)} %get-tuple-element.42), channel_id=1, source_target_pairs={{0,1},{1,0},{2,3},{3,2},{4,5},{5,4},{6,7},{7,6},{8,9},{9,8},{10,11... | collective-permute-start | bytes 1572872 | tf_op jit(solution)/shard_map/ppermute | solution.py:45
  382.9 18.9 %collective-permute-start.22 = (bf16[128,2048]{1,0:T(8,128)(2,1)}, bf16[128,2048]{1,0:T(8,128)(2,1)S(1)}, u32[]{:S(2)}, u32[]{:S(2)}) collective-permute-start(bf16[128,2048]{1,0:T(8,128)(2,1)} %get-tuple-element.43), channel_id=1, source_target_pairs={{0,1},{1,0},{2,3},{3,2},{4,5},{5,4},{6,7},{7,6},{8,9},{9,8},{10,11... | collective-permute-start | bytes 1572872 | tf_op jit(solution)/shard_map/ppermute | solution.py:45
  384.5 17.4 %collective-permute-start.23 = (bf16[128,2048]{1,0:T(8,128)(2,1)S(1)}, bf16[128,2048]{1,0:T(8,128)(2,1)S(1)}, u32[]{:S(2)}, u32[]{:S(2)}) collective-permute-start(bf16[128,2048]{1,0:T(8,128)(2,1)S(1)} %copy-done.76), channel_id=1, source_target_pairs={{0,2},{1,3},{2,0},{3,1},{4,6},{5,7},{6,4},{7,5},{8,10},{9,11},{10,... | collective-permute-start | bytes 1572872 | tf_op jit(solution)/shard_map/ppermute | solution.py:45
  386.0 22.1 %collective-permute-start.24 = (bf16[128,2048]{1,0:T(8,128)(2,1)}, bf16[128,2048]{1,0:T(8,128)(2,1)S(1)}, u32[]{:S(2)}, u32[]{:S(2)}) collective-permute-start(bf16[128,2048]{1,0:T(8,128)(2,1)} %get-tuple-element.43), channel_id=1, source_target_pairs={{0,2},{1,3},{2,0},{3,1},{4,6},{5,7},{6,4},{7,5},{8,10},{9,11},{10,... | collective-permute-start | bytes 1572872 | tf_op jit(solution)/shard_map/ppermute | solution.py:45
  413.9 11.6 %collective-permute-start.25 = (bf16[128,2048]{1,0:T(8,128)(2,1)S(1)}, bf16[128,2048]{1,0:T(8,128)(2,1)S(1)}, u32[]{:S(2)}, u32[]{:S(2)}) collective-permute-start(bf16[128,2048]{1,0:T(8,128)(2,1)S(1)} %collective-permute-done.21), channel_id=1, source_target_pairs={{0,2},{1,3},{2,0},{3,1},{4,6},{5,7},{6,4},{7,5},{8,10},{9,11},{10,... | collective-permute-start | bytes 1572872 | tf_op jit(solution)/shard_map/ppermute | solution.py:45
  478.3 63.8 %collective-permute-start.32 = (bf16[1024,4096]{1,0:T(8,128)(2,1)}, bf16[1024,4096]{1,0:T(8,128)(2,1)}, u32[]{:S(2)}, u32[]{:S(2)}) collective-permute-start(bf16[1024,4096]{1,0:T(8,128)(2,1)} %convolution_convert_fusion), channel_id=1, source_target_pairs={{0,4},{4,0},{8,12},{12,8},{16,20},{20,16},{24,28},{28,24},{1,5},{5... | collective-permute-start | bytes 25165832 | tf_op jit(solution)/shard_map/ppermute | solution.py:362
  499.7 14.3 %collective-permute-start.28 = (bf16[128,2048]{1,0:T(8,128)(2,1)S(1)}, bf16[128,2048]{1,0:T(8,128)(2,1)S(1)}, u32[]{:S(2)}, u32[]{:S(2)}) collective-permute-start(bf16[128,2048]{1,0:T(8,128)(2,1)S(1)} %get-tuple-element.114), channel_id=1, source_target_pairs={{0,2},{1,3},{2,0},{3,1},{4,6},{5,7},{6,4},{7,5},{8,10},{9,11},{10,... | collective-permute-start | bytes 1572872 | tf_op jit(solution)/shard_map/ppermute | solution.py:45
  500.3 13.9 %collective-permute-start.30 = (bf16[128,2048]{1,0:T(8,128)(2,1)S(1)}, bf16[128,2048]{1,0:T(8,128)(2,1)S(1)}, u32[]{:S(2)}, u32[]{:S(2)}) collective-permute-start(bf16[128,2048]{1,0:T(8,128)(2,1)S(1)} %get-tuple-element.113), channel_id=1, source_target_pairs={{0,1},{1,0},{2,3},{3,2},{4,5},{5,4},{6,7},{7,6},{8,9},{9,8},{10,11... | collective-permute-start | bytes 1572872 | tf_op jit(solution)/shard_map/ppermute | solution.py:45
  514.6 24.4 %collective-permute-start.31 = (bf16[256,2048]{1,0:T(8,128)(2,1)S(1)}, bf16[256,2048]{1,0:T(8,128)(2,1)S(1)}, u32[]{:S(2)}, u32[]{:S(2)}) collective-permute-start(bf16[256,2048]{1,0:T(8,128)(2,1)S(1)} %pad_maximum_fusion.13), channel_id=1, source_target_pairs={{0,2},{1,3},{2,0},{3,1},{4,6},{5,7},{6,4},{7,5},{8,10},{9,11},{10,... | collective-permute-start | bytes 3145736 | tf_op jit(solution)/shard_map/ppermute | solution.py:45
  516.3 24.1 %collective-permute-start.29 = (bf16[256,2048]{1,0:T(8,128)(2,1)S(1)}, bf16[256,2048]{1,0:T(8,128)(2,1)S(1)}, u32[]{:S(2)}, u32[]{:S(2)}) collective-permute-start(bf16[256,2048]{1,0:T(8,128)(2,1)S(1)} %pad_maximum_fusion.12), channel_id=1, source_target_pairs={{0,1},{1,0},{2,3},{3,2},{4,5},{5,4},{6,7},{7,6},{8,9},{9,8},{10,11... | collective-permute-start | bytes 3145736 | tf_op jit(solution)/shard_map/ppermute | solution.py:45
  565.8 23.4 %collective-permute-start.33 = (bf16[256,2048]{1,0:T(8,128)(2,1)}, bf16[256,2048]{1,0:T(8,128)(2,1)S(1)}, u32[]{:S(2)}, u32[]{:S(2)}) collective-permute-start(bf16[256,2048]{1,0:T(8,128)(2,1)} %get-tuple-element.72), channel_id=1, source_target_pairs={{0,1},{1,0},{2,3},{3,2},{4,5},{5,4},{6,7},{7,6},{8,9},{9,8},{10,11... | collective-permute-start | bytes 3145736 | tf_op jit(solution)/shard_map/ppermute | solution.py:45
  567.6 24.8 %collective-permute-start.34 = (bf16[256,2048]{1,0:T(8,128)(2,1)}, bf16[256,2048]{1,0:T(8,128)(2,1)S(1)}, u32[]{:S(2)}, u32[]{:S(2)}) collective-permute-start(bf16[256,2048]{1,0:T(8,128)(2,1)} %get-tuple-element.72), channel_id=1, source_target_pairs={{0,2},{1,3},{2,0},{3,1},{4,6},{5,7},{6,4},{7,5},{8,10},{9,11},{10,... | collective-permute-start | bytes 3145736 | tf_op jit(solution)/shard_map/ppermute | solution.py:45
  589.3 12.8 %collective-permute-start.35 = (bf16[128,2048]{1,0:T(8,128)(2,1)S(1)}, bf16[128,2048]{1,0:T(8,128)(2,1)S(1)}, u32[]{:S(2)}, u32[]{:S(2)}) collective-permute-start(bf16[128,2048]{1,0:T(8,128)(2,1)S(1)} %slice.727), channel_id=1, source_target_pairs={{0,2},{1,3},{2,0},{3,1},{4,6},{5,7},{6,4},{7,5},{8,10},{9,11},{10,... | collective-permute-start | bytes 1572872 | tf_op jit(solution)/shard_map/ppermute | solution.py:45
  590.6 160.6 %reduce-scatter.4.cloned.1.call-start = ((), (), s32[]{:S(2)}) async-start(), calls=%async_computation.6 | async-start | bytes 5242880 | tf_op jit(solution)/shard_map/reduce_scatter | solution.py:381
  651.3 14.7 %collective-permute-start.50 = (bf16[1024,1536]{1,0:T(8,128)(2,1)}, bf16[1024,1536]{1,0:T(8,128)(2,1)}, u32[]{:S(2)}, u32[]{:S(2)}) collective-permute-start(bf16[1024,1536]{1,0:T(8,128)(2,1)} %convolution_convert_fusion.1), channel_id=1, source_target_pairs={{0,4},{4,0},{8,12},{12,8},{16,20},{20,16},{24,28},{28,24},{1,5},{5... | collective-permute-start | bytes 9437192 | tf_op jit(solution)/shard_map/ppermute | solution.py:362
  675.2 223.2 %reduce-scatter.6.cloned.1.call-start = ((), (), s32[]{:S(2)}) async-start(), calls=%async_computation.7 | async-start | bytes 10485760 | tf_op jit(solution)/shard_map/reduce_scatter | solution.py:381
  687.7 15.4 %collective-permute-start.52 = (bf16[128,2048]{1,0:T(8,128)(2,1)S(1)}, bf16[128,2048]{1,0:T(8,128)(2,1)S(1)}, u32[]{:S(2)}, u32[]{:S(2)}) collective-permute-start(bf16[128,2048]{1,0:T(8,128)(2,1)S(1)} %get-tuple-element.94), channel_id=1, source_target_pairs={{0,2},{1,3},{2,0},{3,1},{4,6},{5,7},{6,4},{7,5},{8,10},{9,11},{10,... | collective-permute-start | bytes 1572872 | tf_op jit(solution)/shard_map/ppermute | solution.py:45
  689.1 14.8 %collective-permute-start.54 = (bf16[128,2048]{1,0:T(8,128)(2,1)S(1)}, bf16[128,2048]{1,0:T(8,128)(2,1)S(1)}, u32[]{:S(2)}, u32[]{:S(2)}) collective-permute-start(bf16[128,2048]{1,0:T(8,128)(2,1)S(1)} %get-tuple-element.93), channel_id=1, source_target_pairs={{0,1},{1,0},{2,3},{3,2},{4,5},{5,4},{6,7},{7,6},{8,9},{9,8},{10,11... | collective-permute-start | bytes 1572872 | tf_op jit(solution)/shard_map/ppermute | solution.py:45
  690.6 17.9 %collective-permute-start.38 = (f32[8,2048]{1,0:T(8,128)S(1)}, f32[8,2048]{1,0:T(8,128)S(1)}, u32[]{:S(2)}, u32[]{:S(2)}) collective-permute-start(f32[8,2048]{1,0:T(8,128)S(1)} %concatenate.143), channel_id=1, source_target_pairs={{0,2},{1,3},{2,0},{3,1},{4,6},{5,7},{6,4},{7,5},{8,10},{9,11},{10,... | collective-permute-start | bytes 196616 | tf_op jit(solution)/shard_map/ppermute | solution.py:45
  691.4 17.2 %collective-permute-start.39 = (f32[8,2048]{1,0:T(8,128)S(1)}, f32[8,2048]{1,0:T(8,128)S(1)}, u32[]{:S(2)}, u32[]{:S(2)}) collective-permute-start(f32[8,2048]{1,0:T(8,128)S(1)} %concatenate.143), channel_id=1, source_target_pairs={{0,3},{1,2},{2,1},{3,0},{4,7},{5,6},{6,5},{7,4},{8,11},{9,10},{10,... | collective-permute-start | bytes 196616 | tf_op jit(solution)/shard_map/ppermute | solution.py:45
  694.1 14.5 %collective-permute-start.37 = (f32[8,2048]{1,0:T(8,128)S(1)}, f32[8,2048]{1,0:T(8,128)S(1)}, u32[]{:S(2)}, u32[]{:S(2)}) collective-permute-start(f32[8,2048]{1,0:T(8,128)S(1)} %concatenate.143), channel_id=1, source_target_pairs={{0,1},{1,0},{2,3},{3,2},{4,5},{5,4},{6,7},{7,6},{8,9},{9,8},{10,11... | collective-permute-start | bytes 196616 | tf_op jit(solution)/shard_map/ppermute | solution.py:45
  706.7 23.3 %collective-permute-start.55 = (bf16[256,2048]{1,0:T(8,128)(2,1)}, bf16[256,2048]{1,0:T(8,128)(2,1)}, u32[]{:S(2)}, u32[]{:S(2)}) collective-permute-start(bf16[256,2048]{1,0:T(8,128)(2,1)} %pad_maximum_fusion.15), channel_id=1, source_target_pairs={{0,2},{1,3},{2,0},{3,1},{4,6},{5,7},{6,4},{7,5},{8,10},{9,11},{10,... | collective-permute-start | bytes 3145736 | tf_op jit(solution)/shard_map/ppermute | solution.py:45
  708.4 22.9 %collective-permute-start.53 = (bf16[256,2048]{1,0:T(8,128)(2,1)}, bf16[256,2048]{1,0:T(8,128)(2,1)S(1)}, u32[]{:S(2)}, u32[]{:S(2)}) collective-permute-start(bf16[256,2048]{1,0:T(8,128)(2,1)} %pad_maximum_fusion.14), channel_id=1, source_target_pairs={{0,1},{1,0},{2,3},{3,2},{4,5},{5,4},{6,7},{7,6},{8,9},{9,8},{10,11... | collective-permute-start | bytes 3145736 | tf_op jit(solution)/shard_map/ppermute | solution.py:45
  (132 other events, 1079.8 us)
Sparse Core Ops, SparseCore 0:
  10.2 85.1 all-gather.4
  97.0 149.5 all-gather.6
  248.2 80.6 all-gather.8
  590.7 74.8 reduce-scatter.7
  675.4 75.7 reduce-scatter.3
  753.4 145.0 reduce-scatter.5
